TPU v7x, 512 devices: a whole 4x4x16 slice. The times are simulated.
512 devices in a mesh: blk: 128 (over y_hi, z, x), feat: 4 (over y_lo, core).
Axes of the slice: x: 4, y: 4 (y_hi: 2, y_lo: 2; y = y_hi * 2 + y_lo), z: 16, core: 2. Of those that a mesh axis runs over, the one named last changes fastest.
Arguments:
- features: bfloat16 [256, 131072], P('feat', 'blk'), may hold values from -6 to 6
- block_values: bfloat16 [17408, 128, 128], P('blk'), may hold values from 0 to 1, as said below
- block_rows: int32 [17408], P('blk'), may hold values from 0 to 7, as said below
- block_cols: int32 [17408], P('blk'), may hold values from 0 to 1023, as said below
- block_count: int32 [128], P('blk'), may hold values from 8 to 136, as said below
- labels: int32 [131072], P(('blk', 'feat')), may hold values from 0 to 127
- weight_in: bfloat16 [256, 256], replicated, may hold values from -0.375 to 0.375
- weight_out: bfloat16 [256, 128], replicated, may hold values from -1 to 1
Outputs:
- logits: float32 [128, 131072], P(None, ('blk', 'feat'))
- grad_in: float32 [256, 256], replicated
- grad_out: float32 [256, 128], replicated
Inputs may be any that keep to these rules, and one draw needn't show every extreme that they name: The first block_count[s] slots of stripe s are its blocks; the remaining slots hold blocks that are not part of the matrix; every stripe holds its 8 diagonal blocks, and the busiest stripe fills all 136 slots. `block_rows`: block row of a slot inside its stripe. `block_cols`: every slot's block column lies within 8 blocks of its global block row, counted around the loop of 1024 block columns; the live slots of a stripe name distinct blocks. `block_values`: the matrix assembled from the live slots is symmetric: live block (r, c) is the transpose of live block (c, r).
All inputs are finite; a program needn't handle non-finite values.
Results may differ from a plain program's by a relative error of at most 0.002.
The roundings to bfloat16 on the way count: a program that leaves them out, or rounds other values in their place, can miss the bound.
Values may be sent and summed in bfloat16 or wider, within the bound.
No kernel may reach another device: no remote copies, remote signals or barrier semaphores. Data moves between devices by JAX's collectives and lax.ppermute only.
A program may use at most 64 MiB of HBM per device.

v0:
```python
import math

import jax
import jax.numpy as jnp
from jax import lax
from jax.sharding import PartitionSpec as P


def extended_2(cells, sides, width):
    for axis, dim in sides:
        count = lax.axis_size(axis)
        head = lax.slice_in_dim(cells, 0, width, axis=dim)
        tail = lax.slice_in_dim(cells, cells.shape[dim] - width, cells.shape[dim], axis=dim)
        cells = jnp.concatenate(
            [
                lax.ppermute(tail, axis, [(i, (i + 1) % count) for i in range(count)]),
                cells,
                lax.ppermute(head, axis, [((i + 1) % count, i) for i in range(count)]),
            ],
            axis=dim,
        )
    return cells


def propagate(extended, block_values, local_index, placing, precise):
    channels = extended.shape[0]
    block_size = block_values.shape[1]
    blocked = extended.reshape(channels, extended.shape[1] // block_size, block_size)
    gathered = jnp.take(blocked, local_index, axis=1)
    if precise:
        products = jnp.einsum(
            "csb,sab->csa",
            gathered,
            block_values.astype(jnp.float32),
            precision=lax.Precision.HIGHEST,
        )
    else:
        products = jnp.einsum(
            "csb,sab->csa", gathered, block_values, preferred_element_type=jnp.float32
        )
    placed = jnp.einsum("csa,sr->cra", products, placing, precision=lax.Precision.HIGHEST)
    return placed.reshape(channels, placing.shape[1] * block_size)


def activation(entry_value):
    return jax.nn.gelu(entry_value, approximate=True)


def on_device(
    features, block_values, block_rows, block_cols, block_count, labels, weight_in, weight_out
):
    device_count = lax.axis_size("blk")
    stripe_index = lax.axis_index("blk")
    block_size = block_values.shape[1]
    slot_count = block_rows.shape[0]
    stripe_rows = features.shape[1]
    stripe_blocks = stripe_rows // block_size
    reach_blocks = (slot_count // stripe_blocks - 1) // 2
    total_blocks = stripe_blocks * device_count
    local_index = jnp.mod(block_cols - (stripe_index * stripe_blocks - reach_blocks), total_blocks)
    live_slots = jnp.arange(slot_count, dtype=jnp.int32) < block_count[0]
    placing = (
        (block_rows[:, None] == jnp.arange(stripe_blocks, dtype=jnp.int32)[None, :])
        & live_slots[:, None]
    ).astype(jnp.float32)
    band_width = reach_blocks * block_size
    node_scale = 1.0 / math.sqrt(device_count * stripe_rows)
    input_ext = extended_2(features, (("blk", 1),), band_width)
    prop_in = propagate(input_ext, block_values, local_index, placing, False).astype(jnp.bfloat16)
    prop_rows_in = lax.all_to_all(prop_in, "feat", split_axis=1, concat_axis=0, tiled=True)
    pre_hidden = jnp.einsum(
        "ih,ir->hr", weight_in, prop_rows_in, preferred_element_type=jnp.float32
    )
    hidden = activation(pre_hidden).astype(jnp.bfloat16)
    hidden_cols = lax.all_to_all(hidden, "feat", split_axis=0, concat_axis=1, tiled=True)
    hidden_ext = extended_2(hidden_cols, (("blk", 1),), band_width)
    prop_hid = propagate(hidden_ext, block_values, local_index, placing, False).astype(jnp.bfloat16)
    prop_rows_hid = lax.all_to_all(prop_hid, "feat", split_axis=1, concat_axis=0, tiled=True)
    logits = jnp.einsum("hc,hr->cr", weight_out, prop_rows_hid, preferred_element_type=jnp.float32)
    class_count = weight_out.shape[1]
    shifted = logits - jnp.max(logits, axis=0, keepdims=True)
    exponent = jnp.exp(shifted)
    probability = exponent / jnp.sum(exponent, axis=0, keepdims=True)
    onehot = (labels[None, :] == jnp.arange(class_count, dtype=jnp.int32)[:, None]).astype(
        jnp.float32
    )
    dlogits = ((probability - onehot) * node_scale).astype(jnp.bfloat16)
    out_share = jnp.einsum("hr,cr->hc", prop_rows_hid, dlogits, preferred_element_type=jnp.float32)
    grad_out = lax.psum(out_share, ("blk", "feat"))
    back_rows = jnp.einsum("hc,cr->hr", weight_out, dlogits, preferred_element_type=jnp.float32)
    back_cols = lax.all_to_all(
        back_rows.astype(jnp.bfloat16), "feat", split_axis=0, concat_axis=1, tiled=True
    ).astype(back_rows.dtype)
    back_ext = extended_2(back_cols.astype(jnp.bfloat16), (("blk", 1),), band_width).astype(
        back_cols.dtype
    )
    back_prop = propagate(back_ext, block_values, local_index, placing, True)
    back_hid = lax.all_to_all(
        back_prop.astype(jnp.bfloat16), "feat", split_axis=1, concat_axis=0, tiled=True
    ).astype(back_prop.dtype)
    unused_output, pullback = jax.vjp(activation, pre_hidden)
    grad_pre = pullback(back_hid)[0].astype(jnp.bfloat16)
    in_share = jnp.einsum("ir,hr->ih", prop_rows_in, grad_pre, preferred_element_type=jnp.float32)
    grad_in = lax.psum(in_share, ("blk", "feat"))
    return (logits, grad_in, grad_out)


def solution(mesh):
    placed = (
        P("feat", "blk"),
        P("blk", None, None),
        P("blk"),
        P("blk"),
        P("blk"),
        P(("blk", "feat")),
        P(),
        P(),
    )
    return jax.shard_map(
        on_device,
        mesh=mesh,
        in_specs=placed,
        out_specs=(P(None, ("blk", "feat")), P(), P()),
        check_vma=False,
    )
```

profile of v0, /device:TPU:1, one launch (start us, length us, event | category | flops | bytes accessed | tf_op | source)
XLA Modules:
  0.0 617.8 jit_solution(3650204196831870399)
XLA Ops:
  7.2 0.0 copy-start
  7.2 4.1 collective-permute-start
  11.3 14.8 %collective-permute-start.1 = (bf16[64,1024]{1,0:T(8,128)(2,1)}, bf16[64,1024]{1,0:T(8,128)(2,1)S(1)}, u32[]{:S(2)}, u32[]{:S(2)}) collective-permute-start(bf16[64,1024]{1,0:T(8,128)(2,1)} %param.10), channel_id=1, source_target_pairs={{4,0},{8,4},{12,8},{16,12},{20,16},{24,20},{28,24},{32,28},{36,32}... | collective-permute-start | bytes 393224 | tf_op jit(solution)/shard_map/ppermute | solution.py:18
  26.7 0.7 compare_and_fusion
  27.4 0.1 collective-permute-done
  27.5 1.0 collective-permute-done.1
  28.5 1.0 copy_bitcast_fusion
  29.5 1.0 gather_fusion.1
  30.5 0.0 copy-start.3
  30.5 5.4 fusion.19
  35.9 0.0 copy-done.3
  35.9 4.0 fusion.43
  39.9 0.1 convert_element_type.67
  40.0 7.5 %all_to_all.80 = bf16[64,4,256]{2,0,1:T(8,128)(2,1)S(1)} all-to-all(bf16[64,4,256]{2,0,1:T(8,128)(2,1)S(1)} %copy.36), channel_id=1, replica_groups=mesh['blk'=128,'feat'=4] {'feat'}, dimensions={1} | all-to-all | bytes 262144 | tf_op jit(solution)/shard_map/all_to_all | solution.py:70
  47.5 0.0 copy-done
  47.5 0.3 multiply_convert_fusion
  47.8 7.0 %all_to_all.81 = bf16[4,64,256]{2,1,0:T(8,128)(2,1)S(1)} all-to-all(bf16[4,64,256]{2,1,0:T(8,128)(2,1)S(1)} %bitcast.120), channel_id=1, replica_groups=mesh['blk'=128,'feat'=4] {'feat'}, dimensions={0} | all-to-all | bytes 262144 | tf_op jit(solution)/shard_map/all_to_all | solution.py:75
  54.8 9.7 %collective-permute-start.3 = (bf16[64,1024]{1,0:T(8,128)(2,1)S(1)}, bf16[64,1024]{1,0:T(8,128)(2,1)S(1)}, u32[]{:S(2)}, u32[]{:S(2)}) collective-permute-start(bf16[64,1024]{1,0:T(8,128)(2,1)S(1)} %bitcast.116), channel_id=1, source_target_pairs={{4,0},{8,4},{12,8},{16,12},{20,16},{24,20},{28,24},{32,28},{36,32}... | collective-permute-start | bytes 393224 | tf_op jit(solution)/shard_map/ppermute | solution.py:18
  64.5 2.1 collective-permute-start.2
  66.7 0.1 copy.37
  66.8 0.1 concatenate.25
  66.9 0.0 collective-permute-done.3
  66.9 9.1 %collective-permute-done.2 = bf16[64,1024]{1,0:T(8,128)(2,1)S(1)} collective-permute-done((bf16[64,1024]{1,0:T(8,128)(2,1)S(1)}, bf16[64,1024]{1,0:T(8,128)(2,1)S(1)}, u32[]{:S(2)}, u32[]{:S(2)}) %collective-permute-start.2) | collective-permute-done | bytes 131104 | tf_op jit(solution)/shard_map/ppermute | solution.py:16
  76.1 1.0 gather_fusion.2
  77.1 5.4 fusion.22
  82.4 0.0 copy-start.2
  82.4 0.0 copy-start.4
  82.4 4.0 fusion.40
  86.5 0.1 convert_element_type.71
  86.6 8.4 %all_to_all.82 = bf16[64,4,256]{2,0,1:T(8,128)(2,1)S(1)} all-to-all(bf16[64,4,256]{2,0,1:T(8,128)(2,1)S(1)} %copy.43), channel_id=1, replica_groups=mesh['blk'=128,'feat'=4] {'feat'}, dimensions={1} | all-to-all | bytes 262144 | tf_op jit(solution)/shard_map/all_to_all | solution.py:78
  95.0 0.0 copy-done.2
  95.0 0.2 fusion.75
  95.3 0.0 copy-start.1
  95.3 0.0 copy-done.4
  95.3 0.2 convolution_convert_fusion
  95.5 7.0 %all_to_all.83 = bf16[4,64,256]{2,1,0:T(8,128)(2,1)S(1)} all-to-all(bf16[4,64,256]{2,1,0:T(8,128)(2,1)S(1)} %bitcast.121), channel_id=1, replica_groups=mesh['blk'=128,'feat'=4] {'feat'}, dimensions={0} | all-to-all | bytes 262144 | tf_op jit(solution)/shard_map/all_to_all | solution.py:91
  102.5 1.9 collective-permute-start.5
  104.5 3.6 collective-permute-start.4
  108.0 0.1 copy.44
  108.2 0.1 concatenate.29
  108.3 0.0 collective-permute-done.5
  108.3 7.6 %collective-permute-done.4 = bf16[64,1024]{1,0:T(8,128)(2,1)S(1)} collective-permute-done((bf16[64,1024]{1,0:T(8,128)(2,1)S(1)}, bf16[64,1024]{1,0:T(8,128)(2,1)S(1)}, u32[]{:S(2)}, u32[]{:S(2)}) %collective-permute-start.4) | collective-permute-done | bytes 131104 | tf_op jit(solution)/shard_map/ppermute | solution.py:16
  115.9 0.1 maximum_convert_fusion
  116.0 2.9 gather_fusion
  118.9 11.1 %fusion.25 = f32[64,136,128]{2,0,1:T(8,128)S(1)} fusion(bf16[136,128,128]{2,1,0:T(8,128)(2,1)} %param.11, f32[136,64,128]{2,1,0:T(8,128)} %gather_fusion, pred[136]{0:T(512)(128)(4,1)S(1)} %get-tuple-element.6), kind=kOutput, calls=%fused_computation.24 | convolution fusion | flops 1712390144 | bytes 13369480 | tf_op jit(solution)/shard_map/csb,sab->csa/dot_general | solution.py:31
  129.9 4.0 fusion.37
  134.0 0.1 convert_element_type.79
  134.1 0.7 copy.50
  134.7 5.5 all-to-all-start.4
  140.2 0.0 all-reduce.3.cloned.1.call-start
  140.2 0.0 copy-done.1
  140.2 0.9 fusion.74
  141.1 2.7 all-to-all-done.4
  143.8 0.2 fusion.54
  144.0 0.9 fusion.76
  144.9 0.0 all-reduce.3.cloned.1.call-update
  144.9 462.8 %all-reduce.3.cloned.1.call-done = (f32[256,256]{1,0:T(8,128)}, f32[256,128]{1,0:T(8,128)}) async-done(((f32[256,256]{1,0:T(8,128)}, f32[256,128]{1,0:T(8,128)}), (f32[256,256]{1,0:T(8,128)}, f32[256,128]{1,0:T(8,128)})) %all-reduce.3.cloned.1.call-update) | async-done | bytes 393232 | tf_op jit(solution)/shard_map/psum | solution.py:104
  607.7 1.7 copy.84
  609.4 1.6 copy.85
  (14 shorter events, 0.3 us)
Async XLA Ops:
  7.2 40.4 %copy-start = (bf16[256,256]{1,0:T(8,128)(2,1)S(1)}, bf16[256,256]{1,0:T(8,128)(2,1)}, u32[]{:S(2)}) copy-start(bf16[256,256]{1,0:T(8,128)(2,1)} %param.16) | copy-start | bytes 393220
  7.2 20.3 %collective-permute-start = (bf16[64,1024]{1,0:T(8,128)(2,1)}, bf16[64,1024]{1,0:T(8,128)(2,1)S(1)}, u32[]{:S(2)}, u32[]{:S(2)}) collective-permute-start(bf16[64,1024]{1,0:T(8,128)(2,1)} %param.10), channel_id=1, source_target_pairs={{0,4},{4,8},{8,12},{12,16},{16,20},{20,24},{24,28},{28,32},{32,36}... | collective-permute-start | bytes 393224 | tf_op jit(solution)/shard_map/ppermute | solution.py:16
  11.3 17.2 %collective-permute-start.1 = (bf16[64,1024]{1,0:T(8,128)(2,1)}, bf16[64,1024]{1,0:T(8,128)(2,1)S(1)}, u32[]{:S(2)}, u32[]{:S(2)}) collective-permute-start(bf16[64,1024]{1,0:T(8,128)(2,1)} %param.10), channel_id=1, source_target_pairs={{4,0},{8,4},{12,8},{16,12},{20,16},{24,20},{28,24},{32,28},{36,32}... | collective-permute-start | bytes 393224 | tf_op jit(solution)/shard_map/ppermute | solution.py:18
  30.5 5.4 copy-start.3
  54.8 12.0 %collective-permute-start.3 = (bf16[64,1024]{1,0:T(8,128)(2,1)S(1)}, bf16[64,1024]{1,0:T(8,128)(2,1)S(1)}, u32[]{:S(2)}, u32[]{:S(2)}) collective-permute-start(bf16[64,1024]{1,0:T(8,128)(2,1)S(1)} %bitcast.116), channel_id=1, source_target_pairs={{4,0},{8,4},{12,8},{16,12},{20,16},{24,20},{28,24},{32,28},{36,32}... | collective-permute-start | bytes 393224 | tf_op jit(solution)/shard_map/ppermute | solution.py:18
  64.5 11.4 %collective-permute-start.2 = (bf16[64,1024]{1,0:T(8,128)(2,1)S(1)}, bf16[64,1024]{1,0:T(8,128)(2,1)S(1)}, u32[]{:S(2)}, u32[]{:S(2)}) collective-permute-start(bf16[64,1024]{1,0:T(8,128)(2,1)S(1)} %bitcast.117), channel_id=1, source_target_pairs={{0,4},{4,8},{8,12},{12,16},{16,20},{20,24},{24,28},{28,32},{32,36}... | collective-permute-start | bytes 393224 | tf_op jit(solution)/shard_map/ppermute | solution.py:16
  82.4 12.6 %copy-start.2 = (bf16[256,128]{1,0:T(8,128)(2,1)S(1)}, bf16[256,128]{1,0:T(8,128)(2,1)}, u32[]{:S(2)}) copy-start(bf16[256,128]{1,0:T(8,128)(2,1)} %param.17) | copy-start | bytes 196612
  82.4 12.9 %copy-start.4 = (s32[256]{0:T(256)S(1)}, s32[256]{0:T(256)}, u32[]{:S(2)}) copy-start(s32[256]{0:T(256)} %param.15) | copy-start | bytes 3076
  95.3 45.0 %copy-start.1 = (f32[256,128]{0,1:T(8,128)}, f32[256,128]{0,1:T(8,128)S(1)}, u32[]{:S(2)}) copy-start(f32[256,128]{0,1:T(8,128)S(1)} %get-tuple-element.11) | copy-start | bytes 393220
  102.5 5.7 collective-permute-start.5
  104.5 11.4 %collective-permute-start.4 = (bf16[64,1024]{1,0:T(8,128)(2,1)S(1)}, bf16[64,1024]{1,0:T(8,128)(2,1)S(1)}, u32[]{:S(2)}, u32[]{:S(2)}) collective-permute-start(bf16[64,1024]{1,0:T(8,128)(2,1)S(1)} %bitcast.119), channel_id=1, source_target_pairs={{0,4},{4,8},{8,12},{12,16},{16,20},{20,24},{24,28},{28,32},{32,36}... | collective-permute-start | bytes 393224 | tf_op jit(solution)/shard_map/ppermute | solution.py:16
  134.7 9.0 %all-to-all-start.4 = ((bf16[64,4,256]{2,0,1:T(8,128)(2,1)}), bf16[64,4,256]{2,0,1:T(8,128)(2,1)S(1)}, u32[]{:S(2)}, u32[]{:S(2)}) async-start(bf16[64,4,256]{2,0,1:T(8,128)(2,1)} %copy.50), calls=%async_computation.4 | async-start | bytes 262144 | tf_op jit(solution)/shard_map/all_to_all | solution.py:98
  140.2 467.5 %all-reduce.3.cloned.1.call-start = ((), (), s32[]{:S(2)}) async-start(), calls=%async_computation.5 | async-start | bytes 786432 | tf_op jit(solution)/shard_map/psum | solution.py:104
Sparse Core Ops, SparseCore 0:
  147.0 460.6 all-reduce.2
where the time goes:
time: 619 us; the launch traced here: 618 us
  waiting for transfers between devices  483 us (78%)
  starting transfers between devices  41.6 us (7%)
  matrix products  36.4 us (6%)
  blocking collectives  29.9 us (5%)
  between operations  15 us (2%)
  local copies, waits for them, and re-layouts  9.57 us (2%)
    psum x1, waiting for transfers between devices, on_device(): grad_in = lax.psum(in_share, ('blk', 'feat'))  463 us
    ppermute x3, starting transfers between devices, extended_2(): lax.ppermute(head, axis, [((i + 1) % count, i) for i in range(count)])  26.4 us
    ppermute x3, waiting for transfers between devices, extended_2(): lax.ppermute(tail, axis, [(i, (i + 1) % count) for i in range(count)])  16.8 us
  transfers between devices with their start and end apart: 8, of which 6 were waited for; matrix products, arithmetic and copies ran while one was open for 0% of the time, Pallas kernels for 0%

commit v1 on v0

v1 whole, which is shorter than its diff:
```python
import functools
import math

import jax
import jax.numpy as jnp
from jax import lax
from jax.experimental import pallas as pl
from jax.experimental.pallas import tpu as pltpu
from jax.sharding import Mesh
from jax.sharding import PartitionSpec as P

BLK = ("yh", "z", "x")
FEAT = ("yl", "co")
PLANE = ("yh", "x")
F32 = jnp.float32
BF16 = jnp.bfloat16
BS = 128
WIDTH = 18 * BS
TILE = 2 * BS
NT = (((1,), (1,)), ((), ()))
NN = (((1,), (0,)), ((), ()))
TN = (((0,), (0,)), ((), ()))
GELU_A = math.sqrt(2.0 / math.pi)
GELU_B = 0.044715


def dot(a, b, dims):
    return lax.dot_general(a, b, dims, preferred_element_type=F32)


def params(mib):
    return pltpu.CompilerParams(vmem_limit_bytes=mib << 20)


def whole():
    return pl.BlockSpec(memory_space=pltpu.VMEM)


def sds(shape, dtype):
    return jax.ShapeDtypeStruct(shape, dtype)


def assemble_kernel(per_step, rows_ref, cols_ref, count_ref, blocks_ref, dense_ref):
    step = pl.program_id(0)
    stripe_blocks = dense_ref.shape[0] // BS
    total_blocks = stripe_blocks * lax.axis_size(BLK)
    first = (lax.axis_index(BLK) - 1) * stripe_blocks - total_blocks

    @pl.when(step == 0)
    def _():
        dense_ref[...] = jnp.zeros_like(dense_ref)

    for j in range(per_step):
        slot = step * per_step + j

        @pl.when(slot < count_ref[0])
        def _():
            row = rows_ref[slot]
            local = lax.rem(cols_ref[slot] - first, total_blocks)
            col = local - (row // 2) * 2
            row = pl.multiple_of(row * BS, BS)
            col = pl.multiple_of(col * BS, BS)
            dense_ref[pl.ds(row, BS), pl.ds(col, BS)] = blocks_ref[j]


def assemble(block_values, rows, cols, count, stripe_rows):
    slots = block_values.shape[0]
    per_step = 17
    return pl.pallas_call(
        functools.partial(assemble_kernel, per_step),
        grid_spec=pltpu.PrefetchScalarGridSpec(
            num_scalar_prefetch=3,
            grid=(slots // per_step,),
            in_specs=[pl.BlockSpec((per_step, BS, BS), lambda i, *_: (i, 0, 0))],
            out_specs=pl.BlockSpec((stripe_rows, WIDTH), lambda i, *_: (0, 0)),
        ),
        out_shape=sds((stripe_rows, WIDTH), BF16),
        compiler_params=params(24),
        name="assemble",
    )(rows, cols, count, pltpu.with_memory_space_constraint(block_values, pltpu.HBM))


def band_product(left, own, right, dense, t):
    stripe = own.shape[1]
    band = dense.at[pl.ds(t * TILE, TILE)]
    cut = stripe - t * TILE
    acc = dot(left[:, t * TILE :], band[:, :cut], NT)
    acc = acc + dot(own[...], band[:, cut : cut + stripe], NT)
    return acc + dot(right[:, : (t + 1) * TILE], band[:, cut + stripe :], NT)


def tiles_of(stripe):
    return [(t, slice(t * TILE, (t + 1) * TILE)) for t in range(stripe // TILE)]


def prop_in_kernel(left, own, right, labels, dense, out):
    channels = own.shape[0]
    tag = jnp.broadcast_to(labels[...].astype(F32), (16, labels.shape[1])).astype(BF16)
    for t, at in tiles_of(own.shape[1]):
        out[:channels, at] = band_product(left, own, right, dense, t).astype(BF16)
        out[channels:, at] = tag if t == 0 else jnp.zeros_like(tag)


def prop_kernel(left, own, right, dense, out):
    for t, at in tiles_of(own.shape[1]):
        out[:, at] = band_product(left, own, right, dense, t).astype(BF16)


def hidden_kernel(first, second, third, fourth, w_in, hidden, pre_own, prop_in, labels):
    yl = lax.axis_index("yl")
    co = lax.axis_index("co")
    hid = hidden.shape[0]
    half = hid // 2
    depth = prop_in.shape[0] // 4
    for part, dy, dc in ((first, 0, 0), (second, 0, 1), (third, 1, 0), (fourth, 1, 1)):
        place = (yl + dy - 2 * yl * dy) * 2 + (co + dc - 2 * co * dc)
        rows = pl.ds(pl.multiple_of(place * depth, depth), depth)
        prop_in[rows, :] = part[:depth, :]
        labels[:, pl.ds(pl.multiple_of(place * TILE, TILE), TILE)] = part[
            depth : depth + 8, :TILE
        ].astype(F32)
    weight = w_in[:, pl.ds(pl.multiple_of(co * hid, hid), hid)]
    pre = dot(weight, prop_in[...], TN)
    inner = GELU_A * (pre + GELU_B * (pre * pre * pre))
    hidden[...] = (pre * (0.5 * (1.0 + jnp.tanh(inner)))).astype(BF16)
    pre_own[...] = jnp.where(yl == 0, pre[:half], pre[half:])


def logits_kernel(scale, own, other, w_out, labels, out, dl, share, scores):
    yl = lax.axis_index("yl")
    co = lax.axis_index("co")
    hid = own.shape[0]
    w_own = w_out[pl.ds(pl.multiple_of(co * hid, hid), hid), :]
    w_other = w_out[pl.ds(pl.multiple_of((1 - co) * hid, hid), hid), :]
    logit = dot(w_own, own[...], TN) + dot(w_other, other[...], TN)
    scores[...] = logit
    start = pl.multiple_of((yl * 2 + co) * out.shape[1], out.shape[1])
    out[...] = scores[:, pl.ds(start, out.shape[1])]
    shifted = logit - jnp.max(logit, axis=0, keepdims=True)
    exponent = jnp.exp(shifted)
    probability = exponent / jnp.sum(exponent, axis=0, keepdims=True)
    classes = lax.broadcasted_iota(jnp.int32, logit.shape, 0).astype(F32)
    onehot = jnp.where(classes == labels[0:1, :], 1.0, 0.0)
    dlogits = ((probability - onehot) * scale).astype(BF16)
    dl[...] = dlogits
    rows = share.shape[0]
    mine = own[pl.ds(pl.multiple_of(yl * rows, rows), rows), :]
    share[...] = dot(mine, dlogits, NT)


def grads_kernel(left, own, right, w_out, pre_own, prop_in, share_out, dense, out):
    yl = lax.axis_index("yl")
    co = lax.axis_index("co")
    half = pre_own.shape[0]
    w = w_out[pl.ds(pl.multiple_of((co * 2 + yl) * half, half), half), :]
    share = None
    for t, at in tiles_of(own.shape[1]):
        acc = band_product(left, own, right, dense, t)
        high = acc.astype(BF16)
        rest = acc - high.astype(F32)
        middle = rest.astype(BF16)
        low = (rest - middle.astype(F32)).astype(BF16)
        back = dot(w, high, NN) + (dot(w, middle, NN) + dot(w, low, NN))
        v = pre_own[:, at]
        th = jnp.tanh(GELU_A * (v + GELU_B * (v * v * v)))
        slope = 0.5 * (1.0 + th) + (0.5 * v) * (1.0 - th * th) * (
            GELU_A * (1.0 + (3.0 * GELU_B) * (v * v))
        )
        part = dot((back * slope).astype(BF16), prop_in[:, at], NT)
        share = part if share is None else share + part
    pieces, rows, _ = out.shape
    width = share.shape[1]
    for p in range(pieces):
        out[p, :, :width] = share[p * rows : (p + 1) * rows]
        out[p, :, width:] = share_out[p * rows : (p + 1) * rows]


def sum_kernel(parts, out):
    total = parts[0]
    for p in range(1, parts.shape[0]):
        total = total + parts[p]
    for p in range(out.shape[0]):
        out[p] = total


def collect_kernel(parts, grad_in, grad_out, rows_ref):
    planes = parts.shape[0] // 4
    rows = parts.shape[1]
    width = grad_in.shape[0]
    for p in range(planes):
        for yl in range(2):
            for co in range(2):
                at = ((co * 2 + yl) * planes + p) * rows
                rows_ref[at : at + rows, :] = parts[p * 4 + yl * 2 + co]
    grad_in[...] = rows_ref[:, :width].T
    grad_out[...] = rows_ref[:, width:]


def call(kernel, args, out_shape, name, mib=16, scratch=()):
    many = isinstance(out_shape, (tuple, list))
    return pl.pallas_call(
        kernel,
        in_specs=[whole()] * len(args),
        out_specs=[whole()] * len(out_shape) if many else whole(),
        out_shape=out_shape,
        scratch_shapes=list(scratch),
        compiler_params=params(mib),
        name=name,
    )(*args)


def neighbours(value):
    count = lax.axis_size(BLK)
    left = lax.ppermute(value, BLK, [(i, (i + 1) % count) for i in range(count)])
    right = lax.ppermute(value, BLK, [((i + 1) % count, i) for i in range(count)])
    return left, value, right


def flipped(value, axes):
    shift = {("co",): 1, ("yl",): 2, ("yl", "co"): 3}[axes]
    return lax.ppermute(value, FEAT, [(i, i ^ shift) for i in range(4)])


def on_device(
    features, block_values, block_rows, block_cols, block_count, labels, weight_in, weight_out
):
    devices = lax.axis_size(BLK)
    depth, stripe = features.shape
    node_scale = 1.0 / math.sqrt(devices * stripe)
    hid = weight_in.shape[1]
    classes = weight_out.shape[1]
    mine = labels.shape[0]

    x_pieces = neighbours(features)
    dense = assemble(block_values, block_rows, block_cols, block_count, stripe)
    first = call(
        prop_in_kernel,
        (*x_pieces, labels.reshape(1, mine), dense),
        sds((depth + 16, stripe), BF16),
        "prop_in",
    )
    fourth = flipped(first, ("yl", "co"))
    third = flipped(first, ("yl",))
    second = flipped(first, ("co",))
    hidden, pre_own, prop_in, label_rows = call(
        hidden_kernel,
        (first, second, third, fourth, weight_in),
        (
            sds((hid // 2, stripe), BF16),
            sds((hid // 4, stripe), F32),
            sds((4 * depth, stripe), BF16),
            sds((8, stripe), F32),
        ),
        "hidden",
    )

    prop_own = call(
        prop_kernel, (*neighbours(hidden), dense), sds((hid // 2, stripe), BF16), "prop_hid"
    )
    prop_other = flipped(prop_own, ("co",))
    logits, dl, share_out = call(
        functools.partial(logits_kernel, node_scale),
        (prop_own, prop_other, weight_out, label_rows),
        (
            sds((classes, mine), F32),
            sds((classes, stripe), BF16),
            sds((hid // 4, classes), F32),
        ),
        "logits",
        scratch=[pltpu.VMEM((classes, stripe), F32)],
    )

    plane = lax.axis_size(PLANE)
    rows = hid // 4 // plane
    width = 4 * depth + classes
    share = call(
        grads_kernel,
        (*neighbours(dl), weight_out, pre_own, prop_in, share_out, dense),
        sds((plane, rows, width), F32),
        "grads",
    )
    parts = lax.all_to_all(share, PLANE, 0, 0, tiled=True)
    parts = call(sum_kernel, (parts,), sds((lax.axis_size("z"), rows, width), F32), "sum_plane")
    parts = lax.all_to_all(parts, "z", 0, 0, tiled=True)
    parts = call(sum_kernel, (parts,), sds((plane * 4, rows, width), F32), "sum_z")
    parts = lax.all_to_all(parts, PLANE + FEAT, 0, 0, tiled=True)
    grad_in, grad_out = call(
        collect_kernel,
        (parts,),
        (sds((4 * depth, hid), F32), sds((hid, classes), F32)),
        "collect",
        scratch=[pltpu.VMEM((hid, width), F32)],
    )
    return (logits, grad_in, grad_out)


def solution(mesh):
    fine = Mesh(mesh.devices.reshape(2, 16, 4, 2, 2), BLK + FEAT)
    placed = (
        P(FEAT, BLK),
        P(BLK, None, None),
        P(BLK),
        P(BLK),
        P(BLK),
        P(BLK + FEAT),
        P(),
        P(),
    )
    return jax.shard_map(
        on_device,
        mesh=fine,
        in_specs=placed,
        out_specs=(P(None, BLK + FEAT), P(), P()),
        check_vma=False,
    )
```

time: 619 us -> 133 us (0.21)
  waiting for transfers between devices: 483 us -> 29.6 us
  matrix products: 36.4 us -> 0 us
  Pallas kernels: 0 us -> 16.3 us
  between operations: 15 us -> 1.47 us
  blocking collectives: 29.9 us -> 42.7 us
  local copies, waits for them, and re-layouts: 9.57 us -> 1.37 us
    psum x1 -> x0, waiting for transfers between devices: 463 us -> none  [on_device(): grad_in = lax.psum(in_share, ('blk', 'feat'))]
    dot_general x11 -> x0, matrix products: 36.4 us -> none  [the longest x3 12.1 us: propagate(): jnp.einsum('csa,sr->cra', products, placing, precision=lax.Precision.HIGH...]
    pallas_call x0 -> x9, Pallas kernels: none -> 16.3 us  [the longest x8 9.14 us: call(): pl.pallas_call(kernel, in_specs=[whole()] * len(args), out_specs=[whole()...]
    all_to_all x4 -> x3, blocking collectives: 29.9 us -> 42.7 us  [the longest x1 18.6 us: on_device(): parts = lax.all_to_all(parts, PLANE + FEAT, 0, 0, tiled=True)]
    ppermute x6 -> x10, waiting for transfers between devices: 17.8 us -> 29.6 us  [the longest x3 16.9 us: neighbours(): lax.ppermute(value, BLK, [(i, (i + 1) % count) for i in range(count)])]
    ppermute x6 -> x10, starting transfers between devices: 36.2 us -> 41.3 us  [the longest x3 20.4 us: neighbours(): lax.ppermute(value, BLK, [((i + 1) % count, i) for i in range(count)])]
  transfers between devices with their start and end apart: 8 -> 10, of which waited for: 6 -> 7; matrix products, arithmetic and copies ran while one was open for 0% -> 0% of each run, Pallas kernels for 0% -> 5%
where the time goes in v1:
time: 133 us
  blocking collectives  42.7 us (32%)
  starting transfers between devices  41.3 us (31%)
  waiting for transfers between devices  29.6 us (22%)
  Pallas kernels  16.3 us (12%)
  between operations  1.47 us (1%)
  local copies, waits for them, and re-layouts  1.37 us (1%)
    ppermute x3, starting transfers between devices, neighbours(): lax.ppermute(value, BLK, [((i + 1) % count, i) for i in range(count)])  20.4 us
    all_to_all x1, blocking collectives, on_device(): parts = lax.all_to_all(parts, PLANE + FEAT, 0, 0, tiled=True)  18.6 us
    ppermute x3, waiting for transfers between devices, neighbours(): lax.ppermute(value, BLK, [(i, (i + 1) % count) for i in range(count)])  16.9 us
    all_to_all x1, blocking collectives, on_device(): parts = lax.all_to_all(parts, 'z', 0, 0, tiled=True)  14.9 us
    ppermute x4, starting transfers between devices, flipped(): return lax.ppermute(value, FEAT, [(i, i ^ shift) for i in range(4)])  11.5 us
    ppermute x3, starting transfers between devices, neighbours(): lax.ppermute(value, BLK, [(i, (i + 1) % count) for i in range(count)])  9.35 us
    all_to_all x1, blocking collectives, on_device(): parts = lax.all_to_all(share, PLANE, 0, 0, tiled=True)  9.18 us
    pallas_call x8, Pallas kernels, call(): pl.pallas_call(kernel, in_specs=[whole()] * len(args), out_specs=[whole()...  9.14 us
  transfers between devices with their start and end apart: 10, of which 7 were waited for; matrix products, arithmetic and copies ran while one was open for 0% of the time, Pallas kernels for 5%

profile of v1, /device:TPU:1, one launch (start us, length us, event | category | flops | bytes accessed | tf_op | source)
XLA Modules:
  0.0 132.7 jit_solution(12335366689994399488)
XLA Ops:
  0.6 0.0 copy-start.1
  0.6 0.0 copy-start.3
  0.7 4.1 %collective-permute-start = (bf16[64,1024]{1,0:T(8,128)(2,1)}, bf16[64,1024]{1,0:T(8,128)(2,1)S(1)}, u32[]{:S(2)}, u32[]{:S(2)}) collective-permute-start(bf16[64,1024]{1,0:T(8,128)(2,1)} %own.1), channel_id=1, source_target_pairs={{0,4},{4,8},{8,12},{12,16},{16,20},{20,24},{24,28},{28,32},{32,36}... | collective-permute-start | bytes 393224 | tf_op jit(solution)/shard_map/ppermute | solution.py:214
  4.7 14.7 %collective-permute-start.1 = (bf16[64,1024]{1,0:T(8,128)(2,1)}, bf16[64,1024]{1,0:T(8,128)(2,1)S(1)}, u32[]{:S(2)}, u32[]{:S(2)}) collective-permute-start(bf16[64,1024]{1,0:T(8,128)(2,1)} %own.1), channel_id=1, source_target_pairs={{4,0},{8,4},{12,8},{16,12},{20,16},{24,20},{28,24},{32,28},{36,32}... | collective-permute-start | bytes 393224 | tf_op jit(solution)/shard_map/ppermute | solution.py:215
  20.1 0.0 copy-start.4
  20.1 0.7 copy-done.4
  20.8 0.0 copy-start.5
  20.8 0.7 copy-done.5
  21.5 7.1 %assemble.1.dense = bf16[1024,2304]{1,0:T(8,128)(2,1)S(1)} custom-call(s32[136]{0:T(256)S(1)} %copy-done.4, s32[136]{0:T(256)S(1)} %copy-done.5, s32[1]{0:T(128)S(6)} %copy.11.count_ref, bf16[136,128,128]{2,1,0:T(8,128)(2,1)} %blocks_ref.1), custom_call_target="tpu_custom_call" | custom-call | tf_op jit(solution)/shard_map/assemble/pallas_call | solution.py:69
  28.6 0.0 copy-start.2
  28.6 0.0 collective-permute-done.left
  28.7 0.0 collective-permute-done.1.right
  28.7 0.0 copy-done.1
  28.7 0.0 copy-done.3
  28.7 0.0 copy-start
  28.7 1.5 %prop_in.1.first = bf16[80,1024]{1,0:T(8,128)(2,1)S(1)} custom-call(bf16[64,1024]{1,0:T(8,128)(2,1)S(1)} %collective-permute-done.left, bf16[64,1024]{1,0:T(8,128)(2,1)S(1)} %copy-done.1, bf16[64,1024]{1,0:T(8,128)(2,1)S(1)} %collective-permute-done.1.right, s32[1,256]{1,0:T(1,128)S(1)} %bitcast.1, bf16[1024,2304]{1,0:T(8,128)(2,1)S(1)} %assemble.1.dense), custom_call_target="tpu_custom_call" | custom-call | tf_op jit(solution)/shard_map/prop_in/pallas_call | solution.py:201
  30.2 3.1 %collective-permute-start.4 = (bf16[80,1024]{1,0:T(8,128)(2,1)S(1)}, bf16[80,1024]{1,0:T(8,128)(2,1)S(1)}, u32[]{:S(2)}, u32[]{:S(2)}) collective-permute-start(bf16[80,1024]{1,0:T(8,128)(2,1)S(1)} %prop_in.1.first), channel_id=1, source_target_pairs={{0,3},{1,2},{2,1},{3,0},{4,7},{5,6},{6,5},{7,4},{8,11},{9,10},{10,... | collective-permute-start | bytes 491528 | tf_op jit(solution)/shard_map/ppermute | solution.py:221
  33.4 3.0 %collective-permute-start.3 = (bf16[80,1024]{1,0:T(8,128)(2,1)S(1)}, bf16[80,1024]{1,0:T(8,128)(2,1)S(1)}, u32[]{:S(2)}, u32[]{:S(2)}) collective-permute-start(bf16[80,1024]{1,0:T(8,128)(2,1)S(1)} %prop_in.1.first), channel_id=1, source_target_pairs={{0,2},{1,3},{2,0},{3,1},{4,6},{5,7},{6,4},{7,5},{8,10},{9,11},{10,... | collective-permute-start | bytes 491528 | tf_op jit(solution)/shard_map/ppermute | solution.py:221
  36.4 1.9 %collective-permute-start.2 = (bf16[80,1024]{1,0:T(8,128)(2,1)S(1)}, bf16[80,1024]{1,0:T(8,128)(2,1)S(1)}, u32[]{:S(2)}, u32[]{:S(2)}) collective-permute-start(bf16[80,1024]{1,0:T(8,128)(2,1)S(1)} %prop_in.1.first), channel_id=1, source_target_pairs={{0,1},{1,0},{2,3},{3,2},{4,5},{5,4},{6,7},{7,6},{8,9},{9,8},{10,11... | collective-permute-start | bytes 491528 | tf_op jit(solution)/shard_map/ppermute | solution.py:221
  38.3 0.4 collective-permute-done.4.fourth
  38.7 3.5 %collective-permute-done.3.third = bf16[80,1024]{1,0:T(8,128)(2,1)S(1)} collective-permute-done((bf16[80,1024]{1,0:T(8,128)(2,1)S(1)}, bf16[80,1024]{1,0:T(8,128)(2,1)S(1)}, u32[]{:S(2)}, u32[]{:S(2)}) %collective-permute-start.3) | collective-permute-done | bytes 163872 | tf_op jit(solution)/shard_map/ppermute | solution.py:221
  42.2 0.0 collective-permute-done.2.second
  42.2 0.0 copy-done.2
  42.2 0.4 hidden.1
  42.6 3.8 %collective-permute-start.6 = (bf16[128,1024]{1,0:T(8,128)(2,1)S(1)}, bf16[128,1024]{1,0:T(8,128)(2,1)S(1)}, u32[]{:S(2)}, u32[]{:S(2)}) collective-permute-start(bf16[128,1024]{1,0:T(8,128)(2,1)S(1)} %get-tuple-element.12.own), channel_id=1, source_target_pairs={{4,0},{8,4},{12,8},{16,12},{20,16},{24,20},{28,24},{32,28},{36,32}... | collective-permute-start | bytes 786440 | tf_op jit(solution)/shard_map/ppermute | solution.py:215
  46.4 1.9 %collective-permute-start.5 = (bf16[128,1024]{1,0:T(8,128)(2,1)S(1)}, bf16[128,1024]{1,0:T(8,128)(2,1)S(1)}, u32[]{:S(2)}, u32[]{:S(2)}) collective-permute-start(bf16[128,1024]{1,0:T(8,128)(2,1)S(1)} %get-tuple-element.12.own), channel_id=1, source_target_pairs={{0,4},{4,8},{8,12},{12,16},{16,20},{20,24},{24,28},{28,32},{32,36}... | collective-permute-start | bytes 786440 | tf_op jit(solution)/shard_map/ppermute | solution.py:214
  48.3 3.6 %collective-permute-done.6.right = bf16[128,1024]{1,0:T(8,128)(2,1)S(1)} collective-permute-done((bf16[128,1024]{1,0:T(8,128)(2,1)S(1)}, bf16[128,1024]{1,0:T(8,128)(2,1)S(1)}, u32[]{:S(2)}, u32[]{:S(2)}) %collective-permute-start.6) | collective-permute-done | bytes 262176 | tf_op jit(solution)/shard_map/ppermute | solution.py:215
  51.9 9.2 %collective-permute-done.5.left = bf16[128,1024]{1,0:T(8,128)(2,1)S(1)} collective-permute-done((bf16[128,1024]{1,0:T(8,128)(2,1)S(1)}, bf16[128,1024]{1,0:T(8,128)(2,1)S(1)}, u32[]{:S(2)}, u32[]{:S(2)}) %collective-permute-start.5) | collective-permute-done | bytes 262176 | tf_op jit(solution)/shard_map/ppermute | solution.py:214
  61.2 1.6 %prop_hid.1.own = bf16[128,1024]{1,0:T(8,128)(2,1)S(1)} custom-call(bf16[128,1024]{1,0:T(8,128)(2,1)S(1)} %collective-permute-done.5.left, bf16[128,1024]{1,0:T(8,128)(2,1)S(1)} %get-tuple-element.12.own, bf16[128,1024]{1,0:T(8,128)(2,1)S(1)} %collective-permute-done.6.right, bf16[1024,2304]{1,0:T(8,128)(2,1)S(1)} %assemble.1.dense), custom_call_target="tpu_custom_call" | custom-call | tf_op jit(solution)/shard_map/prop_hid/pallas_call | solution.py:201
  62.8 3.4 %collective-permute-start.7 = (bf16[128,1024]{1,0:T(8,128)(2,1)S(1)}, bf16[128,1024]{1,0:T(8,128)(2,1)S(1)}, u32[]{:S(2)}, u32[]{:S(2)}) collective-permute-start(bf16[128,1024]{1,0:T(8,128)(2,1)S(1)} %prop_hid.1.own), channel_id=1, source_target_pairs={{0,1},{1,0},{2,3},{3,2},{4,5},{5,4},{6,7},{7,6},{8,9},{9,8},{10,11... | collective-permute-start | bytes 786440 | tf_op jit(solution)/shard_map/ppermute | solution.py:221
  66.3 1.1 collective-permute-done.7.other
  67.4 0.0 copy-done
  67.4 1.2 logits.1
  68.6 1.9 %collective-permute-start.9 = (bf16[128,1024]{1,0:T(8,128)(2,1)S(1)}, bf16[128,1024]{1,0:T(8,128)(2,1)S(1)}, u32[]{:S(2)}, u32[]{:S(2)}) collective-permute-start(bf16[128,1024]{1,0:T(8,128)(2,1)S(1)} %get-tuple-element.15.own), channel_id=1, source_target_pairs={{4,0},{8,4},{12,8},{16,12},{20,16},{24,20},{28,24},{32,28},{36,32}... | collective-permute-start | bytes 786440 | tf_op jit(solution)/shard_map/ppermute | solution.py:215
  70.5 3.4 %collective-permute-start.8 = (bf16[128,1024]{1,0:T(8,128)(2,1)S(1)}, bf16[128,1024]{1,0:T(8,128)(2,1)S(1)}, u32[]{:S(2)}, u32[]{:S(2)}) collective-permute-start(bf16[128,1024]{1,0:T(8,128)(2,1)S(1)} %get-tuple-element.15.own), channel_id=1, source_target_pairs={{0,4},{4,8},{8,12},{12,16},{16,20},{20,24},{24,28},{28,32},{32,36}... | collective-permute-start | bytes 786440 | tf_op jit(solution)/shard_map/ppermute | solution.py:214
  73.9 4.1 %collective-permute-done.9.right = bf16[128,1024]{1,0:T(8,128)(2,1)S(1)} collective-permute-done((bf16[128,1024]{1,0:T(8,128)(2,1)S(1)}, bf16[128,1024]{1,0:T(8,128)(2,1)S(1)}, u32[]{:S(2)}, u32[]{:S(2)}) %collective-permute-start.9) | collective-permute-done | bytes 262176 | tf_op jit(solution)/shard_map/ppermute | solution.py:215
  78.0 7.7 %collective-permute-done.8.left = bf16[128,1024]{1,0:T(8,128)(2,1)S(1)} collective-permute-done((bf16[128,1024]{1,0:T(8,128)(2,1)S(1)}, bf16[128,1024]{1,0:T(8,128)(2,1)S(1)}, u32[]{:S(2)}, u32[]{:S(2)}) %collective-permute-start.8) | collective-permute-done | bytes 262176 | tf_op jit(solution)/shard_map/ppermute | solution.py:214
  85.6 3.5 %grads.1 = f32[8,8,384]{2,1,0:T(8,128)S(1)} custom-call(bf16[128,1024]{1,0:T(8,128)(2,1)S(1)} %collective-permute-done.8.left, bf16[128,1024]{1,0:T(8,128)(2,1)S(1)} %get-tuple-element.15.own, bf16[128,1024]{1,0:T(8,128)(2,1)S(1)} %collective-permute-done.9.right, bf16[256,128]{1,0:T(8,128)(2,1)S(1)} %copy-done, f32[64,1024]{1,0:T(8,128)S(1)} %get-tuple-element.16.pre_own, ...), custom_call_target="tpu_custom_call" | custom-call | tf_op jit(solution)/shard_map/grads/pallas_call | solution.py:201
  89.1 9.2 %all_to_all.15.parts = f32[8,8,384]{2,1,0:T(8,128)S(1)} all-to-all(f32[8,8,384]{2,1,0:T(8,128)S(1)} %grads.1), channel_id=1, replica_groups=mesh['yh'=2,'z'=16,'x'=4,'yl'=2,'co'=2] {'yh','x'}, dimensions={0} | all-to-all | bytes 196608 | tf_op jit(solution)/shard_map/all_to_all | solution.py:282
  98.3 14.9 %all_to_all.16.parts = f32[16,8,384]{2,1,0:T(8,128)S(1)} all-to-all(f32[16,8,384]{2,1,0:T(8,128)S(1)} %sum_plane.1), channel_id=1, replica_groups=mesh['yh'=2,'z'=16,'x'=4,'yl'=2,'co'=2] {'z'}, dimensions={0} | all-to-all | bytes 393216 | tf_op jit(solution)/shard_map/all_to_all | solution.py:284
  113.2 18.6 %all_to_all.17.parts = f32[32,8,384]{2,1,0:T(8,128)S(1)} all-to-all(f32[32,8,384]{2,1,0:T(8,128)S(1)} %sum_z.1), channel_id=1, replica_groups=mesh['yh'=2,'z'=16,'x'=4,'yl'=2,'co'=2] {'yh','x','yl','co'}, dimensions={0} | all-to-all | bytes 786432 | tf_op jit(solution)/shard_map/all_to_all | solution.py:286
  131.9 0.8 collect.1
  (2 shorter events, 0.1 us)
Async XLA Ops:
  0.6 28.0 %copy-start.1 = (bf16[64,1024]{1,0:T(8,128)(2,1)S(1)}, bf16[64,1024]{1,0:T(8,128)(2,1)}, u32[]{:S(2)}) copy-start(bf16[64,1024]{1,0:T(8,128)(2,1)} %own.1) | copy-start | bytes 393220
  0.6 28.0 %copy-start.3 = (s32[256]{0:T(256)S(1)}, s32[256]{0:T(256)}, u32[]{:S(2)}) copy-start(s32[256]{0:T(256)} %param.13) | copy-start | bytes 3076
  0.7 28.0 %collective-permute-start = (bf16[64,1024]{1,0:T(8,128)(2,1)}, bf16[64,1024]{1,0:T(8,128)(2,1)S(1)}, u32[]{:S(2)}, u32[]{:S(2)}) collective-permute-start(bf16[64,1024]{1,0:T(8,128)(2,1)} %own.1), channel_id=1, source_target_pairs={{0,4},{4,8},{8,12},{12,16},{16,20},{20,24},{24,28},{28,32},{32,36}... | collective-permute-start | bytes 393224 | tf_op jit(solution)/shard_map/ppermute | solution.py:214
  4.7 23.9 %collective-permute-start.1 = (bf16[64,1024]{1,0:T(8,128)(2,1)}, bf16[64,1024]{1,0:T(8,128)(2,1)S(1)}, u32[]{:S(2)}, u32[]{:S(2)}) collective-permute-start(bf16[64,1024]{1,0:T(8,128)(2,1)} %own.1), channel_id=1, source_target_pairs={{4,0},{8,4},{12,8},{16,12},{20,16},{24,20},{28,24},{32,28},{36,32}... | collective-permute-start | bytes 393224 | tf_op jit(solution)/shard_map/ppermute | solution.py:215
  20.1 0.7 copy-start.4
  20.8 0.7 copy-start.5
  28.6 13.5 %copy-start.2 = (bf16[256,256]{1,0:T(8,128)(2,1)S(1)}, bf16[256,256]{1,0:T(8,128)(2,1)}, u32[]{:S(2)}) copy-start(bf16[256,256]{1,0:T(8,128)(2,1)} %w_in.1) | copy-start | bytes 393220
  28.7 38.7 %copy-start = (bf16[256,128]{1,0:T(8,128)(2,1)S(1)}, bf16[256,128]{1,0:T(8,128)(2,1)}, u32[]{:S(2)}) copy-start(bf16[256,128]{1,0:T(8,128)(2,1)} %w_out.3) | copy-start | bytes 196612
  30.2 8.4 %collective-permute-start.4 = (bf16[80,1024]{1,0:T(8,128)(2,1)S(1)}, bf16[80,1024]{1,0:T(8,128)(2,1)S(1)}, u32[]{:S(2)}, u32[]{:S(2)}) collective-permute-start(bf16[80,1024]{1,0:T(8,128)(2,1)S(1)} %prop_in.1.first), channel_id=1, source_target_pairs={{0,3},{1,2},{2,1},{3,0},{4,7},{5,6},{6,5},{7,4},{8,11},{9,10},{10,... | collective-permute-start | bytes 491528 | tf_op jit(solution)/shard_map/ppermute | solution.py:221
  33.4 8.8 %collective-permute-start.3 = (bf16[80,1024]{1,0:T(8,128)(2,1)S(1)}, bf16[80,1024]{1,0:T(8,128)(2,1)S(1)}, u32[]{:S(2)}, u32[]{:S(2)}) collective-permute-start(bf16[80,1024]{1,0:T(8,128)(2,1)S(1)} %prop_in.1.first), channel_id=1, source_target_pairs={{0,2},{1,3},{2,0},{3,1},{4,6},{5,7},{6,4},{7,5},{8,10},{9,11},{10,... | collective-permute-start | bytes 491528 | tf_op jit(solution)/shard_map/ppermute | solution.py:221
  36.4 5.8 %collective-permute-start.2 = (bf16[80,1024]{1,0:T(8,128)(2,1)S(1)}, bf16[80,1024]{1,0:T(8,128)(2,1)S(1)}, u32[]{:S(2)}, u32[]{:S(2)}) collective-permute-start(bf16[80,1024]{1,0:T(8,128)(2,1)S(1)} %prop_in.1.first), channel_id=1, source_target_pairs={{0,1},{1,0},{2,3},{3,2},{4,5},{5,4},{6,7},{7,6},{8,9},{9,8},{10,11... | collective-permute-start | bytes 491528 | tf_op jit(solution)/shard_map/ppermute | solution.py:221
  42.6 9.4 %collective-permute-start.6 = (bf16[128,1024]{1,0:T(8,128)(2,1)S(1)}, bf16[128,1024]{1,0:T(8,128)(2,1)S(1)}, u32[]{:S(2)}, u32[]{:S(2)}) collective-permute-start(bf16[128,1024]{1,0:T(8,128)(2,1)S(1)} %get-tuple-element.12.own), channel_id=1, source_target_pairs={{4,0},{8,4},{12,8},{16,12},{20,16},{24,20},{28,24},{32,28},{36,32}... | collective-permute-start | bytes 786440 | tf_op jit(solution)/shard_map/ppermute | solution.py:215
  46.4 14.8 %collective-permute-start.5 = (bf16[128,1024]{1,0:T(8,128)(2,1)S(1)}, bf16[128,1024]{1,0:T(8,128)(2,1)S(1)}, u32[]{:S(2)}, u32[]{:S(2)}) collective-permute-start(bf16[128,1024]{1,0:T(8,128)(2,1)S(1)} %get-tuple-element.12.own), channel_id=1, source_target_pairs={{0,4},{4,8},{8,12},{12,16},{16,20},{20,24},{24,28},{28,32},{32,36}... | collective-permute-start | bytes 786440 | tf_op jit(solution)/shard_map/ppermute | solution.py:214
  62.8 4.6 %collective-permute-start.7 = (bf16[128,1024]{1,0:T(8,128)(2,1)S(1)}, bf16[128,1024]{1,0:T(8,128)(2,1)S(1)}, u32[]{:S(2)}, u32[]{:S(2)}) collective-permute-start(bf16[128,1024]{1,0:T(8,128)(2,1)S(1)} %prop_hid.1.own), channel_id=1, source_target_pairs={{0,1},{1,0},{2,3},{3,2},{4,5},{5,4},{6,7},{7,6},{8,9},{9,8},{10,11... | collective-permute-start | bytes 786440 | tf_op jit(solution)/shard_map/ppermute | solution.py:221
  68.6 9.4 %collective-permute-start.9 = (bf16[128,1024]{1,0:T(8,128)(2,1)S(1)}, bf16[128,1024]{1,0:T(8,128)(2,1)S(1)}, u32[]{:S(2)}, u32[]{:S(2)}) collective-permute-start(bf16[128,1024]{1,0:T(8,128)(2,1)S(1)} %get-tuple-element.15.own), channel_id=1, source_target_pairs={{4,0},{8,4},{12,8},{16,12},{20,16},{24,20},{28,24},{32,28},{36,32}... | collective-permute-start | bytes 786440 | tf_op jit(solution)/shard_map/ppermute | solution.py:215
  70.5 15.1 %collective-permute-start.8 = (bf16[128,1024]{1,0:T(8,128)(2,1)S(1)}, bf16[128,1024]{1,0:T(8,128)(2,1)S(1)}, u32[]{:S(2)}, u32[]{:S(2)}) collective-permute-start(bf16[128,1024]{1,0:T(8,128)(2,1)S(1)} %get-tuple-element.15.own), channel_id=1, source_target_pairs={{0,4},{4,8},{8,12},{12,16},{16,20},{20,24},{24,28},{28,32},{32,36}... | collective-permute-start | bytes 786440 | tf_op jit(solution)/shard_map/ppermute | solution.py:214

commit v2 on v1

--- a/solution.py
+++ b/solution.py
@@ -8,6 +8,7 @@
 from jax.experimental.pallas import tpu as pltpu
 from jax.sharding import Mesh
 from jax.sharding import PartitionSpec as P
+
 
 BLK = ("yh", "z", "x")
 FEAT = ("yl", "co")
@@ -17,8 +18,8 @@
 BS = 128
 WIDTH = 18 * BS
 TILE = 2 * BS
+TAG = 8
 NT = (((1,), (1,)), ((), ()))
-NN = (((1,), (0,)), ((), ()))
 TN = (((0,), (0,)), ((), ()))
 GELU_A = math.sqrt(2.0 / math.pi)
 GELU_B = 0.044715
@@ -40,70 +41,122 @@
     return jax.ShapeDtypeStruct(shape, dtype)
 
 
-def assemble_kernel(per_step, rows_ref, cols_ref, count_ref, blocks_ref, dense_ref):
-    step = pl.program_id(0)
-    stripe_blocks = dense_ref.shape[0] // BS
-    total_blocks = stripe_blocks * lax.axis_size(BLK)
-    first = (lax.axis_index(BLK) - 1) * stripe_blocks - total_blocks
-
-    @pl.when(step == 0)
-    def _():
-        dense_ref[...] = jnp.zeros_like(dense_ref)
-
-    for j in range(per_step):
-        slot = step * per_step + j
-
-        @pl.when(slot < count_ref[0])
-        def _():
+def assemble_kernel(chunks, rows_ref, cols_ref, count_ref, blocks_hbm, dense_ref, blocks, sems):
+    slots = blocks.shape[0]
+    each = slots // chunks
+    copies = [
+        pltpu.make_async_copy(
+            blocks_hbm.at[pl.ds(i * each, each)], blocks.at[pl.ds(i * each, each)], sems.at[i]
+        )
+        for i in range(chunks)
+    ]
+    for copy in copies:
+        copy.start()
+    spare = dense_ref.shape[0] - BS
+    total_blocks = spare // BS * lax.axis_size(BLK)
+    first = (lax.axis_index(BLK) - 1) * (spare // BS)
+    count = count_ref[0]
+    dense_ref[...] = jnp.zeros_like(dense_ref)
+    for i in range(chunks):
+        copies[i].wait()
+
+        def place(slot, carry):
             row = rows_ref[slot]
-            local = lax.rem(cols_ref[slot] - first, total_blocks)
-            col = local - (row // 2) * 2
-            row = pl.multiple_of(row * BS, BS)
+            local = cols_ref[slot] - first
+            local = jnp.where(local < 0, local + total_blocks, local)
+            local = jnp.where(local >= total_blocks, local - total_blocks, local)
+            col = local - row + lax.bitwise_and(row, 1)
+            row = jnp.where(slot < count, row * BS, spare)
+            row = pl.multiple_of(row, BS)
             col = pl.multiple_of(col * BS, BS)
-            dense_ref[pl.ds(row, BS), pl.ds(col, BS)] = blocks_ref[j]
+            dense_ref[pl.ds(row, BS), pl.ds(col, BS)] = blocks[slot]
+            return carry
+
+        lax.fori_loop(i * each, (i + 1) * each, place, 0, unroll=True)
 
 
 def assemble(block_values, rows, cols, count, stripe_rows):
-    slots = block_values.shape[0]
-    per_step = 17
+    chunks = 4
+    shape = (stripe_rows + BS, WIDTH)
+    smem = pl.BlockSpec(memory_space=pltpu.SMEM)
     return pl.pallas_call(
-        functools.partial(assemble_kernel, per_step),
-        grid_spec=pltpu.PrefetchScalarGridSpec(
-            num_scalar_prefetch=3,
-            grid=(slots // per_step,),
-            in_specs=[pl.BlockSpec((per_step, BS, BS), lambda i, *_: (i, 0, 0))],
-            out_specs=pl.BlockSpec((stripe_rows, WIDTH), lambda i, *_: (0, 0)),
-        ),
-        out_shape=sds((stripe_rows, WIDTH), BF16),
+        functools.partial(assemble_kernel, chunks),
+        in_specs=[smem, smem, smem, pl.BlockSpec(memory_space=pltpu.HBM)],
+        out_specs=whole(),
+        out_shape=sds(shape, BF16),
+        scratch_shapes=[
+            pltpu.VMEM(block_values.shape, BF16),
+            pltpu.SemaphoreType.DMA((chunks,)),
+        ],
         compiler_params=params(24),
         name="assemble",
-    )(rows, cols, count, pltpu.with_memory_space_constraint(block_values, pltpu.HBM))
-
-
-def band_product(left, own, right, dense, t):
-    stripe = own.shape[1]
-    band = dense.at[pl.ds(t * TILE, TILE)]
-    cut = stripe - t * TILE
-    acc = dot(left[:, t * TILE :], band[:, :cut], NT)
-    acc = acc + dot(own[...], band[:, cut : cut + stripe], NT)
-    return acc + dot(right[:, : (t + 1) * TILE], band[:, cut + stripe :], NT)
+    )(in_hbm(rows), in_hbm(cols), count, in_hbm(block_values))
+
+
+def in_hbm(value):
+    return pltpu.with_memory_space_constraint(value, pltpu.HBM)
 
 
 def tiles_of(stripe):
     return [(t, slice(t * TILE, (t + 1) * TILE)) for t in range(stripe // TILE)]
 
 
-def prop_in_kernel(left, own, right, labels, dense, out):
-    channels = own.shape[0]
-    tag = jnp.broadcast_to(labels[...].astype(F32), (16, labels.shape[1])).astype(BF16)
-    for t, at in tiles_of(own.shape[1]):
-        out[:channels, at] = band_product(left, own, right, dense, t).astype(BF16)
+def on_sides(near, body):
+    odd = lax.bitwise_and(lax.axis_index("x"), 1) == 1
+    to_left = odd if near else jnp.logical_not(odd)
+
+    @pl.when(to_left)
+    def _():
+        body(left_product)
+
+    @pl.when(jnp.logical_not(to_left))
+    def _():
+        body(right_product)
+
+
+def left_product(dense, piece, t, at):
+    return dot(dense[at, : piece.shape[1] - t * TILE], piece[:, t * TILE :], NT)
+
+
+def right_product(dense, piece, t, at):
+    start = 2 * piece.shape[1] - t * TILE
+    return dot(dense[at, start:], piece[:, : (t + 1) * TILE], NT)
+
+
+def own_product(dense, piece, t, at):
+    start = piece.shape[1] - t * TILE
+    return dot(dense[at, start : start + piece.shape[1]], piece[...], NT)
+
+
+def near_kernel(own, near, dense, acc):
+    def body(product):
+        for t, at in tiles_of(own.shape[1]):
+            acc[at, :] = own_product(dense, own, t, at) + product(dense, near, t, at)
+
+    on_sides(True, body)
+
+
+def prop_in_kernel(far, acc, labels, dense, out):
+    channels = far.shape[0]
+    tag = jnp.broadcast_to(labels[...].astype(F32), (TAG, labels.shape[1])).astype(BF16)
+    for t, at in tiles_of(far.shape[1]):
         out[channels:, at] = tag if t == 0 else jnp.zeros_like(tag)
 
-
-def prop_kernel(left, own, right, dense, out):
-    for t, at in tiles_of(own.shape[1]):
-        out[:, at] = band_product(left, own, right, dense, t).astype(BF16)
+    def body(product):
+        for t, at in tiles_of(far.shape[1]):
+            total = acc[at, :] + product(dense, far, t, at)
+            out[:channels, at] = total.T.astype(BF16)
+
+    on_sides(False, body)
+
+
+def prop_kernel(far, acc, dense, out):
+    def body(product):
+        for t, at in tiles_of(far.shape[1]):
+            total = acc[at, :] + product(dense, far, t, at)
+            out[:, at] = total.T.astype(BF16)
+
+    on_sides(False, body)
 
 
 def hidden_kernel(first, second, third, fourth, w_in, hidden, pre_own, prop_in, labels):
@@ -117,7 +170,7 @@
         rows = pl.ds(pl.multiple_of(place * depth, depth), depth)
         prop_in[rows, :] = part[:depth, :]
         labels[:, pl.ds(pl.multiple_of(place * TILE, TILE), TILE)] = part[
-            depth : depth + 8, :TILE
+            depth : depth + TAG, :TILE
         ].astype(F32)
     weight = w_in[:, pl.ds(pl.multiple_of(co * hid, hid), hid)]
     pre = dot(weight, prop_in[...], TN)
@@ -148,19 +201,24 @@
     share[...] = dot(mine, dlogits, NT)
 
 
-def grads_kernel(left, own, right, w_out, pre_own, prop_in, share_out, dense, out):
+def grads_kernel(far, acc, w_out, pre_own, prop_in, share_out, dense, out, total):
+    def body(product):
+        for t, at in tiles_of(far.shape[1]):
+            total[at, :] = acc[at, :] + product(dense, far, t, at)
+
+    on_sides(False, body)
     yl = lax.axis_index("yl")
     co = lax.axis_index("co")
     half = pre_own.shape[0]
     w = w_out[pl.ds(pl.multiple_of((co * 2 + yl) * half, half), half), :]
     share = None
-    for t, at in tiles_of(own.shape[1]):
-        acc = band_product(left, own, right, dense, t)
-        high = acc.astype(BF16)
-        rest = acc - high.astype(F32)
+    for t, at in tiles_of(far.shape[1]):
+        spread = total[at, :]
+        high = spread.astype(BF16)
+        rest = spread - high.astype(F32)
         middle = rest.astype(BF16)
         low = (rest - middle.astype(F32)).astype(BF16)
-        back = dot(w, high, NN) + (dot(w, middle, NN) + dot(w, low, NN))
+        back = dot(w, high, NT) + (dot(w, middle, NT) + dot(w, low, NT))
         v = pre_own[:, at]
         th = jnp.tanh(GELU_A * (v + GELU_B * (v * v * v)))
         slope = 0.5 * (1.0 + th) + (0.5 * v) * (1.0 - th * th) * (
@@ -196,7 +254,7 @@
     grad_out[...] = rows_ref[:, width:]
 
 
-def call(kernel, args, out_shape, name, mib=16, scratch=()):
+def call(kernel, args, out_shape, mib=16, scratch=()):
     many = isinstance(out_shape, (tuple, list))
     return pl.pallas_call(
         kernel,
@@ -205,15 +263,20 @@
         out_shape=out_shape,
         scratch_shapes=list(scratch),
         compiler_params=params(mib),
-        name=name,
     )(*args)
 
 
-def neighbours(value):
+def halo(value):
     count = lax.axis_size(BLK)
-    left = lax.ppermute(value, BLK, [(i, (i + 1) % count) for i in range(count)])
-    right = lax.ppermute(value, BLK, [((i + 1) % count, i) for i in range(count)])
-    return left, value, right
+    far = [(i, (i + 1 if i % 2 else i - 1) % count) for i in range(count)]
+    far = lax.ppermute(value, BLK, far)
+    near = lax.ppermute(value, BLK, [(i, i ^ 1) for i in range(count)])
+    return near, far
+
+
+def near_part(value, near, dense):
+    shape = (value.shape[1], value.shape[0])
+    return call(near_kernel, (value, near, dense), sds(shape, F32))
 
 
 def flipped(value, axes):
@@ -231,13 +294,12 @@
     classes = weight_out.shape[1]
     mine = labels.shape[0]
 
-    x_pieces = neighbours(features)
+    near, far = halo(features)
     dense = assemble(block_values, block_rows, block_cols, block_count, stripe)
     first = call(
         prop_in_kernel,
-        (*x_pieces, labels.reshape(1, mine), dense),
-        sds((depth + 16, stripe), BF16),
-        "prop_in",
+        (far, near_part(features, near, dense), labels.reshape(1, mine), dense),
+        sds((depth + TAG, stripe), BF16),
     )
     fourth = flipped(first, ("yl", "co"))
     third = flipped(first, ("yl",))
@@ -251,11 +313,11 @@
             sds((4 * depth, stripe), BF16),
             sds((8, stripe), F32),
         ),
-        "hidden",
-    )
-
+    )
+
+    near, far = halo(hidden)
     prop_own = call(
-        prop_kernel, (*neighbours(hidden), dense), sds((hid // 2, stripe), BF16), "prop_hid"
+        prop_kernel, (far, near_part(hidden, near, dense), dense), sds((hid // 2, stripe), BF16)
     )
     prop_other = flipped(prop_own, ("co",))
     logits, dl, share_out = call(
@@ -266,29 +328,36 @@
             sds((classes, stripe), BF16),
             sds((hid // 4, classes), F32),
         ),
-        "logits",
         scratch=[pltpu.VMEM((classes, stripe), F32)],
     )
 
     plane = lax.axis_size(PLANE)
     rows = hid // 4 // plane
     width = 4 * depth + classes
+    near, far = halo(dl)
     share = call(
         grads_kernel,
-        (*neighbours(dl), weight_out, pre_own, prop_in, share_out, dense),
+        (
+            far,
+            near_part(dl, near, dense),
+            weight_out,
+            pre_own,
+            prop_in,
+            share_out,
+            dense,
+        ),
         sds((plane, rows, width), F32),
-        "grads",
+        scratch=[pltpu.VMEM((stripe, classes), F32)],
     )
     parts = lax.all_to_all(share, PLANE, 0, 0, tiled=True)
-    parts = call(sum_kernel, (parts,), sds((lax.axis_size("z"), rows, width), F32), "sum_plane")
+    parts = call(sum_kernel, (parts,), sds((lax.axis_size("z"), rows, width), F32))
     parts = lax.all_to_all(parts, "z", 0, 0, tiled=True)
-    parts = call(sum_kernel, (parts,), sds((plane * 4, rows, width), F32), "sum_z")
+    parts = call(sum_kernel, (parts,), sds((plane * 4, rows, width), F32))
     parts = lax.all_to_all(parts, PLANE + FEAT, 0, 0, tiled=True)
     grad_in, grad_out = call(
         collect_kernel,
         (parts,),
         (sds((4 * depth, hid), F32), sds((hid, classes), F32)),
-        "collect",
         scratch=[pltpu.VMEM((hid, width), F32)],
     )
     return (logits, grad_in, grad_out)

time: 133 us -> 127 us (0.955)
  waiting for transfers between devices: 29.6 us -> 16.6 us
  starting transfers between devices: 41.3 us -> 50.5 us
  Pallas kernels: 16.3 us -> 11.1 us
  blocking collectives: 42.7 us -> 46.4 us
  local copies, waits for them, and re-layouts: 1.37 us -> 0.02 us
    ppermute x6, waiting for transfers between devices: 24.6 us -> 12.4 us  [the longest x3 12.4 us: halo(): far = lax.ppermute(value, BLK, far)]
    ppermute x6, starting transfers between devices: 29.8 us -> 39 us  [the longest x3 31 us: halo(): far = lax.ppermute(value, BLK, far)]
    pallas_call x1, Pallas kernels: 7.14 us -> 3.24 us  [assemble(): pl.pallas_call(functools.partial(assemble_kernel, chunks), in_specs=[smem...]
    all_to_all x1, blocking collectives: 14.9 us -> 18.4 us  [on_device(): parts = lax.all_to_all(parts, 'z', 0, 0, tiled=True)]
    unnamed x12 -> x8, local copies, waits for them, and re-layouts: 1.37 us -> 0.02 us
    pallas_call x8 -> x11, Pallas kernels: 9.14 us -> 7.87 us  [call(): pl.pallas_call(kernel, in_specs=[whole()] * len(args), out_specs=[whole()...]
  transfers between devices with their start and end apart: 10 -> 10, of which waited for: 7 -> 4; matrix products, arithmetic and copies ran while one was open for 0% -> 0% of each run, Pallas kernels for 5% -> 5%
where the time goes in v2:
time: 127 us; the launch traced here: 126 us
  starting transfers between devices  50.5 us (40%)
  blocking collectives  46.4 us (37%)
  waiting for transfers between devices  16.6 us (13%)
  Pallas kernels  11.1 us (9%)
  between operations  1.51 us (1%)
    ppermute x3, starting transfers between devices, halo(): far = lax.ppermute(value, BLK, far)  31 us
    all_to_all x1, blocking collectives, on_device(): parts = lax.all_to_all(parts, PLANE + FEAT, 0, 0, tiled=True)  18.9 us
    all_to_all x1, blocking collectives, on_device(): parts = lax.all_to_all(parts, 'z', 0, 0, tiled=True)  18.4 us
    ppermute x3, waiting for transfers between devices, halo(): far = lax.ppermute(value, BLK, far)  12.4 us
    ppermute x4, starting transfers between devices, flipped(): return lax.ppermute(value, FEAT, [(i, i ^ shift) for i in range(4)])  11.5 us
    all_to_all x1, blocking collectives, on_device(): parts = lax.all_to_all(share, PLANE, 0, 0, tiled=True)  9.18 us
    ppermute x3, starting transfers between devices, halo(): near = lax.ppermute(value, BLK, [(i, i ^ 1) for i in range(count)])  8.03 us
    pallas_call x11, Pallas kernels, call(): pl.pallas_call(kernel, in_specs=[whole()] * len(args), out_specs=[whole()...  7.87 us
  transfers between devices with their start and end apart: 10, of which 4 were waited for; matrix products, arithmetic and copies ran while one was open for 0% of the time, Pallas kernels for 5%

profile of v2, /device:TPU:1, one launch (start us, length us, event | category | flops | bytes accessed | tf_op | source)
XLA Modules:
  0.0 126.1 jit_solution(14275625890968231652)
XLA Ops:
  0.6 0.0 copy-start.1
  0.6 4.1 %collective-permute-start.1 = (bf16[64,1024]{1,0:T(8,128)(2,1)}, bf16[64,1024]{1,0:T(8,128)(2,1)S(1)}, u32[]{:S(2)}, u32[]{:S(2)}) collective-permute-start(bf16[64,1024]{1,0:T(8,128)(2,1)} %own.1), channel_id=1, source_target_pairs={{0,4},{4,0},{8,12},{12,8},{16,20},{20,16},{24,28},{28,24},{32,36},... | collective-permute-start | bytes 393224 | tf_op jit(solution)/shard_map/ppermute | solution.py:273
  4.7 15.3 %collective-permute-start = (bf16[64,1024]{1,0:T(8,128)(2,1)}, bf16[64,1024]{1,0:T(8,128)(2,1)S(1)}, u32[]{:S(2)}, u32[]{:S(2)}) collective-permute-start(bf16[64,1024]{1,0:T(8,128)(2,1)} %own.1), channel_id=1, source_target_pairs={{0,508},{4,8},{8,4},{12,16},{16,12},{20,24},{24,20},{28,32},{32,28... | collective-permute-start | bytes 393224 | tf_op jit(solution)/shard_map/ppermute | solution.py:272
  20.7 3.2 %assemble.1.dense = bf16[1152,2304]{1,0:T(8,128)(2,1)S(1)} custom-call(s32[136]{0:T(256)} %rows_ref.1, s32[136]{0:T(256)} %cols_ref.1, s32[1]{0:T(128)S(6)} %copy.11.count_ref, bf16[136,128,128]{2,1,0:T(8,128)(2,1)} %blocks_hbm.1), custom_call_target="tpu_custom_call" | custom-call | tf_op jit(solution)/shard_map/assemble/pallas_call | solution.py:82
  23.9 0.0 copy-start.3
  23.9 0.0 copy-start.2
  23.9 0.0 collective-permute-done.1.near
  23.9 0.0 copy-done.1
  23.9 1.0 shard_map.103.acc
  25.0 0.0 collective-permute-done.far
  25.0 0.0 copy-done.3
  25.0 0.6 shard_map.104.first
  25.6 3.4 %collective-permute-start.4 = (bf16[72,1024]{1,0:T(8,128)(2,1)S(1)}, bf16[72,1024]{1,0:T(8,128)(2,1)S(1)}, u32[]{:S(2)}, u32[]{:S(2)}) collective-permute-start(bf16[72,1024]{1,0:T(8,128)(2,1)S(1)} %shard_map.104.first), channel_id=1, source_target_pairs={{0,3},{1,2},{2,1},{3,0},{4,7},{5,6},{6,5},{7,4},{8,11},{9,10},{10,... | collective-permute-start | bytes 442376 | tf_op jit(solution)/shard_map/ppermute | solution.py:284
  29.0 3.0 %collective-permute-start.3 = (bf16[72,1024]{1,0:T(8,128)(2,1)S(1)}, bf16[72,1024]{1,0:T(8,128)(2,1)S(1)}, u32[]{:S(2)}, u32[]{:S(2)}) collective-permute-start(bf16[72,1024]{1,0:T(8,128)(2,1)S(1)} %shard_map.104.first), channel_id=1, source_target_pairs={{0,2},{1,3},{2,0},{3,1},{4,6},{5,7},{6,4},{7,5},{8,10},{9,11},{10,... | collective-permute-start | bytes 442376 | tf_op jit(solution)/shard_map/ppermute | solution.py:284
  32.0 1.9 %collective-permute-start.2 = (bf16[72,1024]{1,0:T(8,128)(2,1)S(1)}, bf16[72,1024]{1,0:T(8,128)(2,1)S(1)}, u32[]{:S(2)}, u32[]{:S(2)}) collective-permute-start(bf16[72,1024]{1,0:T(8,128)(2,1)S(1)} %shard_map.104.first), channel_id=1, source_target_pairs={{0,1},{1,0},{2,3},{3,2},{4,5},{5,4},{6,7},{7,6},{8,9},{9,8},{10,11... | collective-permute-start | bytes 442376 | tf_op jit(solution)/shard_map/ppermute | solution.py:284
  33.9 0.0 collective-permute-done.4.fourth
  33.9 3.0 %collective-permute-done.3.third = bf16[72,1024]{1,0:T(8,128)(2,1)S(1)} collective-permute-done((bf16[72,1024]{1,0:T(8,128)(2,1)S(1)}, bf16[72,1024]{1,0:T(8,128)(2,1)S(1)}, u32[]{:S(2)}, u32[]{:S(2)}) %collective-permute-start.3) | collective-permute-done | bytes 147488 | tf_op jit(solution)/shard_map/ppermute | solution.py:284
  37.0 0.0 collective-permute-done.2.second
  37.0 0.0 copy-done.2
  37.0 0.4 shard_map.105
  37.4 0.0 copy-start
  37.4 2.1 %collective-permute-start.6 = (bf16[128,1024]{1,0:T(8,128)(2,1)S(1)}, bf16[128,1024]{1,0:T(8,128)(2,1)S(1)}, u32[]{:S(2)}, u32[]{:S(2)}) collective-permute-start(bf16[128,1024]{1,0:T(8,128)(2,1)S(1)} %get-tuple-element.12.own), channel_id=1, source_target_pairs={{0,4},{4,0},{8,12},{12,8},{16,20},{20,16},{24,28},{28,24},{32,36},... | collective-permute-start | bytes 786440 | tf_op jit(solution)/shard_map/ppermute | solution.py:273
  39.4 7.8 %collective-permute-start.5 = (bf16[128,1024]{1,0:T(8,128)(2,1)S(1)}, bf16[128,1024]{1,0:T(8,128)(2,1)S(1)}, u32[]{:S(2)}, u32[]{:S(2)}) collective-permute-start(bf16[128,1024]{1,0:T(8,128)(2,1)S(1)} %get-tuple-element.12.own), channel_id=1, source_target_pairs={{0,508},{4,8},{8,4},{12,16},{16,12},{20,24},{24,20},{28,32},{32,28... | collective-permute-start | bytes 786440 | tf_op jit(solution)/shard_map/ppermute | solution.py:272
  47.3 0.0 collective-permute-done.6.near
  47.3 1.0 shard_map.106.acc
  48.3 6.2 %collective-permute-done.5.far = bf16[128,1024]{1,0:T(8,128)(2,1)S(1)} collective-permute-done((bf16[128,1024]{1,0:T(8,128)(2,1)S(1)}, bf16[128,1024]{1,0:T(8,128)(2,1)S(1)}, u32[]{:S(2)}, u32[]{:S(2)}) %collective-permute-start.5) | collective-permute-done | bytes 262176 | tf_op jit(solution)/shard_map/ppermute | solution.py:272
  54.5 0.6 shard_map.107.own
  55.1 3.2 %collective-permute-start.7 = (bf16[128,1024]{1,0:T(8,128)(2,1)S(1)}, bf16[128,1024]{1,0:T(8,128)(2,1)S(1)}, u32[]{:S(2)}, u32[]{:S(2)}) collective-permute-start(bf16[128,1024]{1,0:T(8,128)(2,1)S(1)} %shard_map.107.own), channel_id=1, source_target_pairs={{0,1},{1,0},{2,3},{3,2},{4,5},{5,4},{6,7},{7,6},{8,9},{9,8},{10,11... | collective-permute-start | bytes 786440 | tf_op jit(solution)/shard_map/ppermute | solution.py:284
  58.3 1.1 collective-permute-done.7.other
  59.4 0.0 copy-done
  59.4 1.2 shard_map.108
  60.6 1.9 %collective-permute-start.9 = (bf16[128,1024]{1,0:T(8,128)(2,1)S(1)}, bf16[128,1024]{1,0:T(8,128)(2,1)S(1)}, u32[]{:S(2)}, u32[]{:S(2)}) collective-permute-start(bf16[128,1024]{1,0:T(8,128)(2,1)S(1)} %get-tuple-element.15.own), channel_id=1, source_target_pairs={{0,4},{4,0},{8,12},{12,8},{16,20},{20,16},{24,28},{28,24},{32,36},... | collective-permute-start | bytes 786440 | tf_op jit(solution)/shard_map/ppermute | solution.py:273
  62.5 7.8 %collective-permute-start.8 = (bf16[128,1024]{1,0:T(8,128)(2,1)S(1)}, bf16[128,1024]{1,0:T(8,128)(2,1)S(1)}, u32[]{:S(2)}, u32[]{:S(2)}) collective-permute-start(bf16[128,1024]{1,0:T(8,128)(2,1)S(1)} %get-tuple-element.15.own), channel_id=1, source_target_pairs={{0,508},{4,8},{8,4},{12,16},{16,12},{20,24},{24,20},{28,32},{32,28... | collective-permute-start | bytes 786440 | tf_op jit(solution)/shard_map/ppermute | solution.py:272
  70.3 0.0 collective-permute-done.9.near
  70.4 1.1 shard_map.109.acc
  71.4 6.2 %collective-permute-done.8.far = bf16[128,1024]{1,0:T(8,128)(2,1)S(1)} collective-permute-done((bf16[128,1024]{1,0:T(8,128)(2,1)S(1)}, bf16[128,1024]{1,0:T(8,128)(2,1)S(1)}, u32[]{:S(2)}, u32[]{:S(2)}) %collective-permute-start.8) | collective-permute-done | bytes 262176 | tf_op jit(solution)/shard_map/ppermute | solution.py:272
  77.6 1.1 shard_map.110
  78.8 9.2 %all_to_all.15.parts = f32[8,8,384]{2,1,0:T(8,128)S(1)} all-to-all(f32[8,8,384]{2,1,0:T(8,128)S(1)} %shard_map.110), channel_id=1, replica_groups=mesh['yh'=2,'z'=16,'x'=4,'yl'=2,'co'=2] {'yh','x'}, dimensions={0} | all-to-all | bytes 196608 | tf_op jit(solution)/shard_map/all_to_all | solution.py:352
  88.0 18.4 %all_to_all.16.parts = f32[16,8,384]{2,1,0:T(8,128)S(1)} all-to-all(f32[16,8,384]{2,1,0:T(8,128)S(1)} %shard_map.111), channel_id=1, replica_groups=mesh['yh'=2,'z'=16,'x'=4,'yl'=2,'co'=2] {'z'}, dimensions={0} | all-to-all | bytes 393216 | tf_op jit(solution)/shard_map/all_to_all | solution.py:354
  106.4 18.9 %all_to_all.17.parts = f32[32,8,384]{2,1,0:T(8,128)S(1)} all-to-all(f32[32,8,384]{2,1,0:T(8,128)S(1)} %shard_map.112), channel_id=1, replica_groups=mesh['yh'=2,'z'=16,'x'=4,'yl'=2,'co'=2] {'yh','x','yl','co'}, dimensions={0} | all-to-all | bytes 786432 | tf_op jit(solution)/shard_map/all_to_all | solution.py:356
  125.3 0.8 shard_map.113
  (2 shorter events, 0.1 us)
Async XLA Ops:
  0.6 23.3 %copy-start.1 = (bf16[64,1024]{1,0:T(8,128)(2,1)S(1)}, bf16[64,1024]{1,0:T(8,128)(2,1)}, u32[]{:S(2)}) copy-start(bf16[64,1024]{1,0:T(8,128)(2,1)} %own.1) | copy-start | bytes 393220
  0.6 23.3 %collective-permute-start.1 = (bf16[64,1024]{1,0:T(8,128)(2,1)}, bf16[64,1024]{1,0:T(8,128)(2,1)S(1)}, u32[]{:S(2)}, u32[]{:S(2)}) collective-permute-start(bf16[64,1024]{1,0:T(8,128)(2,1)} %own.1), channel_id=1, source_target_pairs={{0,4},{4,0},{8,12},{12,8},{16,20},{20,16},{24,28},{28,24},{32,36},... | collective-permute-start | bytes 393224 | tf_op jit(solution)/shard_map/ppermute | solution.py:273
  4.7 20.3 %collective-permute-start = (bf16[64,1024]{1,0:T(8,128)(2,1)}, bf16[64,1024]{1,0:T(8,128)(2,1)S(1)}, u32[]{:S(2)}, u32[]{:S(2)}) collective-permute-start(bf16[64,1024]{1,0:T(8,128)(2,1)} %own.1), channel_id=1, source_target_pairs={{0,508},{4,8},{8,4},{12,16},{16,12},{20,24},{24,20},{28,32},{32,28... | collective-permute-start | bytes 393224 | tf_op jit(solution)/shard_map/ppermute | solution.py:272
  23.9 1.1 copy-start.3
  23.9 13.0 %copy-start.2 = (bf16[256,256]{1,0:T(8,128)(2,1)S(1)}, bf16[256,256]{1,0:T(8,128)(2,1)}, u32[]{:S(2)}) copy-start(bf16[256,256]{1,0:T(8,128)(2,1)} %w_in.1) | copy-start | bytes 393220
  25.6 8.3 %collective-permute-start.4 = (bf16[72,1024]{1,0:T(8,128)(2,1)S(1)}, bf16[72,1024]{1,0:T(8,128)(2,1)S(1)}, u32[]{:S(2)}, u32[]{:S(2)}) collective-permute-start(bf16[72,1024]{1,0:T(8,128)(2,1)S(1)} %shard_map.104.first), channel_id=1, source_target_pairs={{0,3},{1,2},{2,1},{3,0},{4,7},{5,6},{6,5},{7,4},{8,11},{9,10},{10,... | collective-permute-start | bytes 442376 | tf_op jit(solution)/shard_map/ppermute | solution.py:284
  29.0 8.0 %collective-permute-start.3 = (bf16[72,1024]{1,0:T(8,128)(2,1)S(1)}, bf16[72,1024]{1,0:T(8,128)(2,1)S(1)}, u32[]{:S(2)}, u32[]{:S(2)}) collective-permute-start(bf16[72,1024]{1,0:T(8,128)(2,1)S(1)} %shard_map.104.first), channel_id=1, source_target_pairs={{0,2},{1,3},{2,0},{3,1},{4,6},{5,7},{6,4},{7,5},{8,10},{9,11},{10,... | collective-permute-start | bytes 442376 | tf_op jit(solution)/shard_map/ppermute | solution.py:284
  32.0 5.0 %collective-permute-start.2 = (bf16[72,1024]{1,0:T(8,128)(2,1)S(1)}, bf16[72,1024]{1,0:T(8,128)(2,1)S(1)}, u32[]{:S(2)}, u32[]{:S(2)}) collective-permute-start(bf16[72,1024]{1,0:T(8,128)(2,1)S(1)} %shard_map.104.first), channel_id=1, source_target_pairs={{0,1},{1,0},{2,3},{3,2},{4,5},{5,4},{6,7},{7,6},{8,9},{9,8},{10,11... | collective-permute-start | bytes 442376 | tf_op jit(solution)/shard_map/ppermute | solution.py:284
  37.4 22.1 %copy-start = (bf16[256,128]{1,0:T(8,128)(2,1)S(1)}, bf16[256,128]{1,0:T(8,128)(2,1)}, u32[]{:S(2)}) copy-start(bf16[256,128]{1,0:T(8,128)(2,1)} %w_out.3) | copy-start | bytes 196612
  37.4 9.9 %collective-permute-start.6 = (bf16[128,1024]{1,0:T(8,128)(2,1)S(1)}, bf16[128,1024]{1,0:T(8,128)(2,1)S(1)}, u32[]{:S(2)}, u32[]{:S(2)}) collective-permute-start(bf16[128,1024]{1,0:T(8,128)(2,1)S(1)} %get-tuple-element.12.own), channel_id=1, source_target_pairs={{0,4},{4,0},{8,12},{12,8},{16,20},{20,16},{24,28},{28,24},{32,36},... | collective-permute-start | bytes 786440 | tf_op jit(solution)/shard_map/ppermute | solution.py:273
  39.4 15.1 %collective-permute-start.5 = (bf16[128,1024]{1,0:T(8,128)(2,1)S(1)}, bf16[128,1024]{1,0:T(8,128)(2,1)S(1)}, u32[]{:S(2)}, u32[]{:S(2)}) collective-permute-start(bf16[128,1024]{1,0:T(8,128)(2,1)S(1)} %get-tuple-element.12.own), channel_id=1, source_target_pairs={{0,508},{4,8},{8,4},{12,16},{16,12},{20,24},{24,20},{28,32},{32,28... | collective-permute-start | bytes 786440 | tf_op jit(solution)/shard_map/ppermute | solution.py:272
  55.1 4.3 %collective-permute-start.7 = (bf16[128,1024]{1,0:T(8,128)(2,1)S(1)}, bf16[128,1024]{1,0:T(8,128)(2,1)S(1)}, u32[]{:S(2)}, u32[]{:S(2)}) collective-permute-start(bf16[128,1024]{1,0:T(8,128)(2,1)S(1)} %shard_map.107.own), channel_id=1, source_target_pairs={{0,1},{1,0},{2,3},{3,2},{4,5},{5,4},{6,7},{7,6},{8,9},{9,8},{10,11... | collective-permute-start | bytes 786440 | tf_op jit(solution)/shard_map/ppermute | solution.py:284
  60.6 9.8 %collective-permute-start.9 = (bf16[128,1024]{1,0:T(8,128)(2,1)S(1)}, bf16[128,1024]{1,0:T(8,128)(2,1)S(1)}, u32[]{:S(2)}, u32[]{:S(2)}) collective-permute-start(bf16[128,1024]{1,0:T(8,128)(2,1)S(1)} %get-tuple-element.15.own), channel_id=1, source_target_pairs={{0,4},{4,0},{8,12},{12,8},{16,20},{20,16},{24,28},{28,24},{32,36},... | collective-permute-start | bytes 786440 | tf_op jit(solution)/shard_map/ppermute | solution.py:273
  62.5 15.1 %collective-permute-start.8 = (bf16[128,1024]{1,0:T(8,128)(2,1)S(1)}, bf16[128,1024]{1,0:T(8,128)(2,1)S(1)}, u32[]{:S(2)}, u32[]{:S(2)}) collective-permute-start(bf16[128,1024]{1,0:T(8,128)(2,1)S(1)} %get-tuple-element.15.own), channel_id=1, source_target_pairs={{0,508},{4,8},{8,4},{12,16},{16,12},{20,24},{24,20},{28,32},{32,28... | collective-permute-start | bytes 786440 | tf_op jit(solution)/shard_map/ppermute | solution.py:272

commit v3 on v2

--- a/solution.py
+++ b/solution.py
@@ -20,6 +20,7 @@
 TILE = 2 * BS
 TAG = 8
 NT = (((1,), (1,)), ((), ()))
+NN = (((1,), (0,)), ((), ()))
 TN = (((0,), (0,)), ((), ()))
 GELU_A = math.sqrt(2.0 / math.pi)
 GELU_B = 0.044715
@@ -128,12 +129,12 @@
     return dot(dense[at, start : start + piece.shape[1]], piece[...], NT)
 
 
-def near_kernel(own, near, dense, acc):
+def start_kernel(near, own, piece, dense, acc):
     def body(product):
         for t, at in tiles_of(own.shape[1]):
-            acc[at, :] = own_product(dense, own, t, at) + product(dense, near, t, at)
-
-    on_sides(True, body)
+            acc[at, :] = own_product(dense, own, t, at) + product(dense, piece, t, at)
+
+    on_sides(near, body)
 
 
 def prop_in_kernel(far, acc, labels, dense, out):
@@ -150,20 +151,9 @@
     on_sides(False, body)
 
 
-def prop_kernel(far, acc, dense, out):
-    def body(product):
-        for t, at in tiles_of(far.shape[1]):
-            total = acc[at, :] + product(dense, far, t, at)
-            out[:, at] = total.T.astype(BF16)
-
-    on_sides(False, body)
-
-
-def hidden_kernel(first, second, third, fourth, w_in, hidden, pre_own, prop_in, labels):
+def gather_kernel(first, second, third, fourth, prop_in, half, labels):
     yl = lax.axis_index("yl")
     co = lax.axis_index("co")
-    hid = hidden.shape[0]
-    half = hid // 2
     depth = prop_in.shape[0] // 4
     for part, dy, dc in ((first, 0, 0), (second, 0, 1), (third, 1, 0), (fourth, 1, 1)):
         place = (yl + dy - 2 * yl * dy) * 2 + (co + dc - 2 * co * dc)
@@ -172,11 +162,55 @@
         labels[:, pl.ds(pl.multiple_of(place * TILE, TILE), TILE)] = part[
             depth : depth + TAG, :TILE
         ].astype(F32)
+    rows = half.shape[0]
+    half[...] = prop_in[pl.ds(pl.multiple_of(co * rows, rows), rows), :]
+
+
+def hidden_of(prop_in, w_in, hidden, pre_part):
+    yl = lax.axis_index("yl")
+    co = lax.axis_index("co")
+    hid = hidden.shape[0]
     weight = w_in[:, pl.ds(pl.multiple_of(co * hid, hid), hid)]
     pre = dot(weight, prop_in[...], TN)
     inner = GELU_A * (pre + GELU_B * (pre * pre * pre))
     hidden[...] = (pre * (0.5 * (1.0 + jnp.tanh(inner)))).astype(BF16)
-    pre_own[...] = jnp.where(yl == 0, pre[:half], pre[half:])
+    pre_part[...] = jnp.where(yl == 0, pre[: hid // 2], pre[hid // 2 :])
+
+
+def own_hidden_kernel(prop_in, w_in, dense, acc, pre_part, hidden):
+    hidden_of(prop_in, w_in, hidden, pre_part)
+    for t, at in tiles_of(hidden.shape[1]):
+        acc[at, :] = own_product(dense, hidden, t, at)
+
+
+def join_halves(mine, other, out):
+    co = lax.axis_index("co")
+    half = mine.shape[0]
+    out[pl.ds(pl.multiple_of(co * half, half), half), :] = mine[...]
+    out[pl.ds(pl.multiple_of((1 - co) * half, half), half), :] = other[...]
+
+
+def prop_hidden_kernel(
+    near, near_other, far, far_other, w_in, acc, dense,
+    out, near_in, far_in, pre_near, pre_far,
+    hidden, total,
+):
+    join_halves(near, near_other, near_in)
+    hidden_of(near_in, w_in, hidden, pre_near)
+
+    def add_near(product):
+        for t, at in tiles_of(out.shape[1]):
+            total[at, :] = acc[at, :] + product(dense, hidden, t, at)
+
+    on_sides(True, add_near)
+    join_halves(far, far_other, far_in)
+    hidden_of(far_in, w_in, hidden, pre_far)
+
+    def add_far(product):
+        for t, at in tiles_of(out.shape[1]):
+            out[:, at] = (total[at, :] + product(dense, hidden, t, at)).T.astype(BF16)
+
+    on_sides(False, add_far)
 
 
 def logits_kernel(scale, own, other, w_out, labels, out, dl, share, scores):
@@ -201,30 +235,44 @@
     share[...] = dot(mine, dlogits, NT)
 
 
-def grads_kernel(far, acc, w_out, pre_own, prop_in, share_out, dense, out, total):
-    def body(product):
-        for t, at in tiles_of(far.shape[1]):
-            total[at, :] = acc[at, :] + product(dense, far, t, at)
-
-    on_sides(False, body)
+def grads_kernel(
+    dl, dense, w_out, pre_own, pre_near, pre_far, own_in, near_in, far_in, share_out, out
+):
+    odd = lax.bitwise_and(lax.axis_index("x"), 1) == 1
     yl = lax.axis_index("yl")
     co = lax.axis_index("co")
     half = pre_own.shape[0]
     w = w_out[pl.ds(pl.multiple_of((co * 2 + yl) * half, half), half), :]
+    tiles = tiles_of(dl.shape[1])
+    reach = dense.shape[1] // TILE
     share = None
-    for t, at in tiles_of(far.shape[1]):
-        spread = total[at, :]
+    for block in range(3 * len(tiles)):
+        spread = None
+        for t, at in tiles:
+            if 0 <= block - t < reach:
+                part = dot(dl[:, at], dense[at, (block - t) * TILE : (block - t + 1) * TILE], NN)
+                spread = part if spread is None else spread + part
         high = spread.astype(BF16)
         rest = spread - high.astype(F32)
         middle = rest.astype(BF16)
         low = (rest - middle.astype(F32)).astype(BF16)
-        back = dot(w, high, NT) + (dot(w, middle, NT) + dot(w, low, NT))
-        v = pre_own[:, at]
+        back = dot(w, high, NN) + (dot(w, middle, NN) + dot(w, low, NN))
+        stripe, tile = divmod(block, len(tiles))
+        at = tiles[tile][1]
+        if stripe == 1:
+            v, prop_in = pre_own[:, at], own_in[:, at]
+        else:
+            is_near = odd if stripe == 0 else jnp.logical_not(odd)
+            v = jnp.where(is_near, pre_near[:, at], pre_far[:, at])
+            prop_in = jnp.where(is_near, near_in[:, at], far_in[:, at])
         th = jnp.tanh(GELU_A * (v + GELU_B * (v * v * v)))
         slope = 0.5 * (1.0 + th) + (0.5 * v) * (1.0 - th * th) * (
             GELU_A * (1.0 + (3.0 * GELU_B) * (v * v))
         )
-        part = dot((back * slope).astype(BF16), prop_in[:, at], NT)
+        grad = back * slope
+        high = grad.astype(BF16)
+        low = (grad - high.astype(F32)).astype(BF16)
+        part = dot(high, prop_in, NT) + dot(low, prop_in, NT)
         share = part if share is None else share + part
     pieces, rows, _ = out.shape
     width = share.shape[1]
@@ -274,13 +322,13 @@
     return near, far
 
 
-def near_part(value, near, dense):
-    shape = (value.shape[1], value.shape[0])
-    return call(near_kernel, (value, near, dense), sds(shape, F32))
+def start_part(own, piece, dense, near):
+    shape = (own.shape[1], own.shape[0])
+    return call(functools.partial(start_kernel, near), (own, piece, dense), sds(shape, F32))
 
 
 def flipped(value, axes):
-    shift = {("co",): 1, ("yl",): 2, ("yl", "co"): 3}[axes]
+    shift = {("co",): 1, ("yl",): 2}[axes]
     return lax.ppermute(value, FEAT, [(i, i ^ shift) for i in range(4)])
 
 
@@ -298,26 +346,37 @@
     dense = assemble(block_values, block_rows, block_cols, block_count, stripe)
     first = call(
         prop_in_kernel,
-        (far, near_part(features, near, dense), labels.reshape(1, mine), dense),
+        (far, start_part(features, near, dense, True), labels.reshape(1, mine), dense),
         sds((depth + TAG, stripe), BF16),
     )
-    fourth = flipped(first, ("yl", "co"))
     third = flipped(first, ("yl",))
     second = flipped(first, ("co",))
-    hidden, pre_own, prop_in, label_rows = call(
-        hidden_kernel,
-        (first, second, third, fourth, weight_in),
+    fourth = flipped(third, ("co",))
+    half_rows = 2 * depth
+    prop_in, half_in, label_rows = call(
+        gather_kernel,
+        (first, second, third, fourth),
         (
-            sds((hid // 2, stripe), BF16),
-            sds((hid // 4, stripe), F32),
             sds((4 * depth, stripe), BF16),
-            sds((8, stripe), F32),
+            sds((half_rows, stripe), BF16),
+            sds((TAG, stripe), F32),
         ),
     )
-
-    near, far = halo(hidden)
-    prop_own = call(
-        prop_kernel, (far, near_part(hidden, near, dense), dense), sds((hid // 2, stripe), BF16)
+    near, far = halo(half_in)
+    pre = sds((hid // 4, stripe), F32)
+    hidden = pltpu.VMEM((hid // 2, stripe), BF16)
+    acc, pre_own = call(
+        own_hidden_kernel,
+        (prop_in, weight_in, dense),
+        (sds((stripe, hid // 2), F32), pre),
+        scratch=[hidden],
+    )
+    whole_in = sds((4 * depth, stripe), BF16)
+    prop_own, near_in, far_in, pre_near, pre_far = call(
+        prop_hidden_kernel,
+        (near, flipped(near, ("co",)), far, flipped(far, ("co",)), weight_in, acc, dense),
+        (sds((hid // 2, stripe), BF16), whole_in, whole_in, pre, pre),
+        scratch=[hidden, pltpu.VMEM((stripe, hid // 2), F32)],
     )
     prop_other = flipped(prop_own, ("co",))
     logits, dl, share_out = call(
@@ -334,20 +393,21 @@
     plane = lax.axis_size(PLANE)
     rows = hid // 4 // plane
     width = 4 * depth + classes
-    near, far = halo(dl)
     share = call(
         grads_kernel,
         (
-            far,
-            near_part(dl, near, dense),
+            dl,
+            dense,
             weight_out,
             pre_own,
+            pre_near,
+            pre_far,
             prop_in,
+            near_in,
+            far_in,
             share_out,
-            dense,
         ),
         sds((plane, rows, width), F32),
-        scratch=[pltpu.VMEM((stripe, classes), F32)],
     )
     parts = lax.all_to_all(share, PLANE, 0, 0, tiled=True)
     parts = call(sum_kernel, (parts,), sds((lax.axis_size("z"), rows, width), F32))

time: 127 us -> 115 us (0.906)
  waiting for transfers between devices: 16.6 us -> 8.66 us
  starting transfers between devices: 50.5 us -> 45.9 us
  Pallas kernels: 11.1 us -> 13.2 us
    ppermute x3 -> x2, starting transfers between devices: 31 us -> 22.8 us  [halo(): far = lax.ppermute(value, BLK, far)]
    ppermute x3 -> x2, waiting for transfers between devices: 12.4 us -> 5.68 us  [halo(): far = lax.ppermute(value, BLK, far)]
    ppermute x4 -> x6, starting transfers between devices: 11.5 us -> 17.1 us  [flipped(): return lax.ppermute(value, FEAT, [(i, i ^ shift) for i in range(4)])]
    pallas_call x11 -> x10, Pallas kernels: 7.87 us -> 9.94 us  [call(): pl.pallas_call(kernel, in_specs=[whole()] * len(args), out_specs=[whole()...]
    ppermute x3 -> x2, starting transfers between devices: 8.03 us -> 5.99 us  [halo(): near = lax.ppermute(value, BLK, [(i, i ^ 1) for i in range(count)])]
    ppermute x4 -> x6, waiting for transfers between devices: 4.17 us -> 2.98 us  [flipped(): return lax.ppermute(value, FEAT, [(i, i ^ shift) for i in range(4)])]
  transfers between devices with their start and end apart: 10 -> 10, of which waited for: 4 -> 5; matrix products, arithmetic and copies ran while one was open for 0% -> 0% of each run, Pallas kernels for 5% -> 5%
where the time goes in v3:
time: 115 us
  starting transfers between devices  45.9 us (40%)
  blocking collectives  45.5 us (40%)
  Pallas kernels  13.2 us (11%)
  waiting for transfers between devices  8.66 us (8%)
  between operations  1.51 us (1%)
    ppermute x2, starting transfers between devices, halo(): far = lax.ppermute(value, BLK, far)  22.8 us
    all_to_all x1, blocking collectives, on_device(): parts = lax.all_to_all(parts, PLANE + FEAT, 0, 0, tiled=True)  18.3 us
    all_to_all x1, blocking collectives, on_device(): parts = lax.all_to_all(parts, 'z', 0, 0, tiled=True)  18 us
    ppermute x6, starting transfers between devices, flipped(): return lax.ppermute(value, FEAT, [(i, i ^ shift) for i in range(4)])  17.1 us
    pallas_call x10, Pallas kernels, call(): pl.pallas_call(kernel, in_specs=[whole()] * len(args), out_specs=[whole()...  9.94 us
    all_to_all x1, blocking collectives, on_device(): parts = lax.all_to_all(share, PLANE, 0, 0, tiled=True)  9.18 us
    ppermute x2, starting transfers between devices, halo(): near = lax.ppermute(value, BLK, [(i, i ^ 1) for i in range(count)])  5.99 us
    ppermute x2, waiting for transfers between devices, halo(): far = lax.ppermute(value, BLK, far)  5.68 us
  transfers between devices with their start and end apart: 10, of which 5 were waited for; matrix products, arithmetic and copies ran while one was open for 0% of the time, Pallas kernels for 5%

profile of v3, /device:TPU:1, one launch (start us, length us, event | category | flops | bytes accessed | tf_op | source)
XLA Modules:
  0.0 114.7 jit_solution(8734130498699851123)
XLA Ops:
  0.6 0.0 copy-start.2
  0.6 4.1 %collective-permute-start.1 = (bf16[64,1024]{1,0:T(8,128)(2,1)}, bf16[64,1024]{1,0:T(8,128)(2,1)S(1)}, u32[]{:S(2)}, u32[]{:S(2)}) collective-permute-start(bf16[64,1024]{1,0:T(8,128)(2,1)} %own.1), channel_id=1, source_target_pairs={{0,4},{4,0},{8,12},{12,8},{16,20},{20,16},{24,28},{28,24},{32,36},... | collective-permute-start | bytes 393224 | tf_op jit(solution)/shard_map/ppermute | solution.py:321
  4.7 15.3 %collective-permute-start = (bf16[64,1024]{1,0:T(8,128)(2,1)}, bf16[64,1024]{1,0:T(8,128)(2,1)S(1)}, u32[]{:S(2)}, u32[]{:S(2)}) collective-permute-start(bf16[64,1024]{1,0:T(8,128)(2,1)} %own.1), channel_id=1, source_target_pairs={{0,508},{4,8},{8,4},{12,16},{16,12},{20,24},{24,20},{28,32},{32,28... | collective-permute-start | bytes 393224 | tf_op jit(solution)/shard_map/ppermute | solution.py:320
  20.7 3.2 %assemble.1.dense = bf16[1152,2304]{1,0:T(8,128)(2,1)S(1)} custom-call(s32[136]{0:T(256)} %rows_ref.1, s32[136]{0:T(256)} %cols_ref.1, s32[1]{0:T(128)S(6)} %copy.11.count_ref, bf16[136,128,128]{2,1,0:T(8,128)(2,1)} %blocks_hbm.1), custom_call_target="tpu_custom_call" | custom-call | tf_op jit(solution)/shard_map/assemble/pallas_call | solution.py:83
  23.9 0.0 copy-start.3
  23.9 0.0 copy-start
  23.9 0.0 collective-permute-done.1.piece
  23.9 0.0 copy-done.2
  23.9 1.0 shard_map.103.acc
  25.0 0.0 collective-permute-done.far
  25.0 0.0 copy-done.3
  25.0 0.6 shard_map.104.first
  25.6 2.3 %collective-permute-start.3 = (bf16[72,1024]{1,0:T(8,128)(2,1)S(1)}, bf16[72,1024]{1,0:T(8,128)(2,1)S(1)}, u32[]{:S(2)}, u32[]{:S(2)}) collective-permute-start(bf16[72,1024]{1,0:T(8,128)(2,1)S(1)} %shard_map.104.first), channel_id=1, source_target_pairs={{0,2},{1,3},{2,0},{3,1},{4,6},{5,7},{6,4},{7,5},{8,10},{9,11},{10,... | collective-permute-start | bytes 442376 | tf_op jit(solution)/shard_map/ppermute | solution.py:332
  27.9 3.4 %collective-permute-start.2 = (bf16[72,1024]{1,0:T(8,128)(2,1)S(1)}, bf16[72,1024]{1,0:T(8,128)(2,1)S(1)}, u32[]{:S(2)}, u32[]{:S(2)}) collective-permute-start(bf16[72,1024]{1,0:T(8,128)(2,1)S(1)} %shard_map.104.first), channel_id=1, source_target_pairs={{0,1},{1,0},{2,3},{3,2},{4,5},{5,4},{6,7},{7,6},{8,9},{9,8},{10,11... | collective-permute-start | bytes 442376 | tf_op jit(solution)/shard_map/ppermute | solution.py:332
  31.3 0.2 collective-permute-done.3.third
  31.5 4.3 %collective-permute-start.4 = (bf16[72,1024]{1,0:T(8,128)(2,1)S(1)}, bf16[72,1024]{1,0:T(8,128)(2,1)S(1)}, u32[]{:S(2)}, u32[]{:S(2)}) collective-permute-start(bf16[72,1024]{1,0:T(8,128)(2,1)S(1)} %collective-permute-done.3.third), channel_id=1, source_target_pairs={{0,1},{1,0},{2,3},{3,2},{4,5},{5,4},{6,7},{7,6},{8,9},{9,8},{10,11... | collective-permute-start | bytes 442376 | tf_op jit(solution)/shard_map/ppermute | solution.py:332
  35.7 0.0 collective-permute-done.2.second
  35.8 1.0 collective-permute-done.4.fourth
  36.7 0.1 shard_map.105
  36.8 7.5 %collective-permute-start.7 = (bf16[128,1024]{1,0:T(8,128)(2,1)S(1)}, bf16[128,1024]{1,0:T(8,128)(2,1)S(1)}, u32[]{:S(2)}, u32[]{:S(2)}) collective-permute-start(bf16[128,1024]{1,0:T(8,128)(2,1)S(1)} %get-tuple-element.18), channel_id=1, source_target_pairs={{0,508},{4,8},{8,4},{12,16},{16,12},{20,24},{24,20},{28,32},{32,28... | collective-permute-start | bytes 786440 | tf_op jit(solution)/shard_map/ppermute | solution.py:320
  44.3 1.9 %collective-permute-start.5 = (bf16[128,1024]{1,0:T(8,128)(2,1)S(1)}, bf16[128,1024]{1,0:T(8,128)(2,1)S(1)}, u32[]{:S(2)}, u32[]{:S(2)}) collective-permute-start(bf16[128,1024]{1,0:T(8,128)(2,1)S(1)} %get-tuple-element.18), channel_id=1, source_target_pairs={{0,4},{4,0},{8,12},{12,8},{16,20},{20,16},{24,28},{28,24},{32,36},... | collective-permute-start | bytes 786440 | tf_op jit(solution)/shard_map/ppermute | solution.py:321
  46.2 5.7 %collective-permute-done.7.far = bf16[128,1024]{1,0:T(8,128)(2,1)S(1)} collective-permute-done((bf16[128,1024]{1,0:T(8,128)(2,1)S(1)}, bf16[128,1024]{1,0:T(8,128)(2,1)S(1)}, u32[]{:S(2)}, u32[]{:S(2)}) %collective-permute-start.7) | collective-permute-done | bytes 262176 | tf_op jit(solution)/shard_map/ppermute | solution.py:320
  51.9 3.1 %collective-permute-start.8 = (bf16[128,1024]{1,0:T(8,128)(2,1)S(1)}, bf16[128,1024]{1,0:T(8,128)(2,1)S(1)}, u32[]{:S(2)}, u32[]{:S(2)}) collective-permute-start(bf16[128,1024]{1,0:T(8,128)(2,1)S(1)} %collective-permute-done.7.far), channel_id=1, source_target_pairs={{0,1},{1,0},{2,3},{3,2},{4,5},{5,4},{6,7},{7,6},{8,9},{9,8},{10,11... | collective-permute-start | bytes 786440 | tf_op jit(solution)/shard_map/ppermute | solution.py:332
  55.0 0.0 collective-permute-done.5.near
  55.1 1.9 %collective-permute-start.6 = (bf16[128,1024]{1,0:T(8,128)(2,1)S(1)}, bf16[128,1024]{1,0:T(8,128)(2,1)S(1)}, u32[]{:S(2)}, u32[]{:S(2)}) collective-permute-start(bf16[128,1024]{1,0:T(8,128)(2,1)S(1)} %collective-permute-done.5.near), channel_id=1, source_target_pairs={{0,1},{1,0},{2,3},{3,2},{4,5},{5,4},{6,7},{7,6},{8,9},{9,8},{10,11... | collective-permute-start | bytes 786440 | tf_op jit(solution)/shard_map/ppermute | solution.py:332
  57.0 0.0 copy-done
  57.0 0.0 copy-start.1
  57.0 1.0 shard_map.106
  58.0 0.0 collective-permute-done.8.far_other
  58.0 0.5 collective-permute-done.6.near_other
  58.5 1.9 %shard_map.107 = (bf16[128,1024]{1,0:T(8,128)(2,1)S(1)}, bf16[256,1024]{1,0:T(8,128)(2,1)S(1)}, bf16[256,1024]{1,0:T(8,128)(2,1)S(1)}, f32[64,1024]{1,0:T(8,128)S(1)}, f32[64,1024]{1,0:T(8,128)S(1)}) custom-call(bf16[128,1024]{1,0:T(8,128)(2,1)S(1)} %collective-permute-done.5.near, bf16[128,1024]{1,0:T(8,128)(2,1)S(1)} %collective-permute-done.6.near_other, ...), custom_call_target="tpu_custom_call" | custom-call | tf_op jit(solution)/shard_map/pallas_call | solution.py:307
  60.4 2.0 %collective-permute-start.9 = (bf16[128,1024]{1,0:T(8,128)(2,1)S(1)}, bf16[128,1024]{1,0:T(8,128)(2,1)S(1)}, u32[]{:S(2)}, u32[]{:S(2)}) collective-permute-start(bf16[128,1024]{1,0:T(8,128)(2,1)S(1)} %get-tuple-element.21.own), channel_id=1, source_target_pairs={{0,1},{1,0},{2,3},{3,2},{4,5},{5,4},{6,7},{7,6},{8,9},{9,8},{10,11... | collective-permute-start | bytes 786440 | tf_op jit(solution)/shard_map/ppermute | solution.py:332
  62.5 1.4 %collective-permute-done.9.other = bf16[128,1024]{1,0:T(8,128)(2,1)S(1)} collective-permute-done((bf16[128,1024]{1,0:T(8,128)(2,1)S(1)}, bf16[128,1024]{1,0:T(8,128)(2,1)S(1)}, u32[]{:S(2)}, u32[]{:S(2)}) %collective-permute-start.9) | collective-permute-done | bytes 262176 | tf_op jit(solution)/shard_map/ppermute | solution.py:332
  63.9 0.0 copy-done.1
  63.9 1.2 %shard_map.108 = (f32[128,256]{1,0:T(8,128)}, bf16[128,1024]{1,0:T(8,128)(2,1)S(1)}, f32[64,128]{1,0:T(8,128)S(1)}) custom-call(bf16[128,1024]{1,0:T(8,128)(2,1)S(1)} %get-tuple-element.21.own, bf16[128,1024]{1,0:T(8,128)(2,1)S(1)} %collective-permute-done.9.other, bf16[256,128]{1,0:T(8,128)(2,1)S(1)} %copy-done.1, f32[8,1024]{1,0:T(8,128)S(1)} %get-tuple-element.22.labels), custom_call_target="tpu_custom_call" | custom-call | tf_op jit(solution)/shard_map/pallas_call | solution.py:307
  65.0 3.3 %shard_map.109 = f32[8,8,384]{2,1,0:T(8,128)S(1)} custom-call(bf16[128,1024]{1,0:T(8,128)(2,1)S(1)} %get-tuple-element.24.dl, bf16[1152,2304]{1,0:T(8,128)(2,1)S(1)} %assemble.1.dense, bf16[256,128]{1,0:T(8,128)(2,1)S(1)} %copy-done.1, f32[64,1024]{1,0:T(8,128)S(1)} %get-tuple-element.25.pre_own, f32[64,1024]{1,0:T(8,128)S(1)} %get-tuple-element.26.pre_near, ...), custom_call_target="tpu_custom_call" | custom-call | tf_op jit(solution)/shard_map/pallas_call | solution.py:307
  68.3 9.2 %all_to_all.15.parts = f32[8,8,384]{2,1,0:T(8,128)S(1)} all-to-all(f32[8,8,384]{2,1,0:T(8,128)S(1)} %shard_map.109), channel_id=1, replica_groups=mesh['yh'=2,'z'=16,'x'=4,'yl'=2,'co'=2] {'yh','x'}, dimensions={0} | all-to-all | bytes 196608 | tf_op jit(solution)/shard_map/all_to_all | solution.py:412
  77.5 18.0 %all_to_all.16.parts = f32[16,8,384]{2,1,0:T(8,128)S(1)} all-to-all(f32[16,8,384]{2,1,0:T(8,128)S(1)} %shard_map.110), channel_id=1, replica_groups=mesh['yh'=2,'z'=16,'x'=4,'yl'=2,'co'=2] {'z'}, dimensions={0} | all-to-all | bytes 393216 | tf_op jit(solution)/shard_map/all_to_all | solution.py:414
  95.6 18.3 %all_to_all.17.parts = f32[32,8,384]{2,1,0:T(8,128)S(1)} all-to-all(f32[32,8,384]{2,1,0:T(8,128)S(1)} %shard_map.111), channel_id=1, replica_groups=mesh['yh'=2,'z'=16,'x'=4,'yl'=2,'co'=2] {'yh','x','yl','co'}, dimensions={0} | all-to-all | bytes 786432 | tf_op jit(solution)/shard_map/all_to_all | solution.py:416
  113.9 0.8 shard_map.112
  (2 shorter events, 0.1 us)
Async XLA Ops:
  0.6 23.3 %copy-start.2 = (bf16[64,1024]{1,0:T(8,128)(2,1)S(1)}, bf16[64,1024]{1,0:T(8,128)(2,1)}, u32[]{:S(2)}) copy-start(bf16[64,1024]{1,0:T(8,128)(2,1)} %own.1) | copy-start | bytes 393220
  0.6 23.3 %collective-permute-start.1 = (bf16[64,1024]{1,0:T(8,128)(2,1)}, bf16[64,1024]{1,0:T(8,128)(2,1)S(1)}, u32[]{:S(2)}, u32[]{:S(2)}) collective-permute-start(bf16[64,1024]{1,0:T(8,128)(2,1)} %own.1), channel_id=1, source_target_pairs={{0,4},{4,0},{8,12},{12,8},{16,20},{20,16},{24,28},{28,24},{32,36},... | collective-permute-start | bytes 393224 | tf_op jit(solution)/shard_map/ppermute | solution.py:321
  4.7 20.3 %collective-permute-start = (bf16[64,1024]{1,0:T(8,128)(2,1)}, bf16[64,1024]{1,0:T(8,128)(2,1)S(1)}, u32[]{:S(2)}, u32[]{:S(2)}) collective-permute-start(bf16[64,1024]{1,0:T(8,128)(2,1)} %own.1), channel_id=1, source_target_pairs={{0,508},{4,8},{8,4},{12,16},{16,12},{20,24},{24,20},{28,32},{32,28... | collective-permute-start | bytes 393224 | tf_op jit(solution)/shard_map/ppermute | solution.py:320
  23.9 1.1 copy-start.3
  23.9 33.1 %copy-start = (bf16[256,256]{1,0:T(8,128)(2,1)S(1)}, bf16[256,256]{1,0:T(8,128)(2,1)}, u32[]{:S(2)}) copy-start(bf16[256,256]{1,0:T(8,128)(2,1)} %w_in.3) | copy-start | bytes 393220
  25.6 5.9 %collective-permute-start.3 = (bf16[72,1024]{1,0:T(8,128)(2,1)S(1)}, bf16[72,1024]{1,0:T(8,128)(2,1)S(1)}, u32[]{:S(2)}, u32[]{:S(2)}) collective-permute-start(bf16[72,1024]{1,0:T(8,128)(2,1)S(1)} %shard_map.104.first), channel_id=1, source_target_pairs={{0,2},{1,3},{2,0},{3,1},{4,6},{5,7},{6,4},{7,5},{8,10},{9,11},{10,... | collective-permute-start | bytes 442376 | tf_op jit(solution)/shard_map/ppermute | solution.py:332
  27.9 7.9 %collective-permute-start.2 = (bf16[72,1024]{1,0:T(8,128)(2,1)S(1)}, bf16[72,1024]{1,0:T(8,128)(2,1)S(1)}, u32[]{:S(2)}, u32[]{:S(2)}) collective-permute-start(bf16[72,1024]{1,0:T(8,128)(2,1)S(1)} %shard_map.104.first), channel_id=1, source_target_pairs={{0,1},{1,0},{2,3},{3,2},{4,5},{5,4},{6,7},{7,6},{8,9},{9,8},{10,11... | collective-permute-start | bytes 442376 | tf_op jit(solution)/shard_map/ppermute | solution.py:332
  31.5 5.3 %collective-permute-start.4 = (bf16[72,1024]{1,0:T(8,128)(2,1)S(1)}, bf16[72,1024]{1,0:T(8,128)(2,1)S(1)}, u32[]{:S(2)}, u32[]{:S(2)}) collective-permute-start(bf16[72,1024]{1,0:T(8,128)(2,1)S(1)} %collective-permute-done.3.third), channel_id=1, source_target_pairs={{0,1},{1,0},{2,3},{3,2},{4,5},{5,4},{6,7},{7,6},{8,9},{9,8},{10,11... | collective-permute-start | bytes 442376 | tf_op jit(solution)/shard_map/ppermute | solution.py:332
  36.8 15.1 %collective-permute-start.7 = (bf16[128,1024]{1,0:T(8,128)(2,1)S(1)}, bf16[128,1024]{1,0:T(8,128)(2,1)S(1)}, u32[]{:S(2)}, u32[]{:S(2)}) collective-permute-start(bf16[128,1024]{1,0:T(8,128)(2,1)S(1)} %get-tuple-element.18), channel_id=1, source_target_pairs={{0,508},{4,8},{8,4},{12,16},{16,12},{20,24},{24,20},{28,32},{32,28... | collective-permute-start | bytes 786440 | tf_op jit(solution)/shard_map/ppermute | solution.py:320
  44.3 10.7 %collective-permute-start.5 = (bf16[128,1024]{1,0:T(8,128)(2,1)S(1)}, bf16[128,1024]{1,0:T(8,128)(2,1)S(1)}, u32[]{:S(2)}, u32[]{:S(2)}) collective-permute-start(bf16[128,1024]{1,0:T(8,128)(2,1)S(1)} %get-tuple-element.18), channel_id=1, source_target_pairs={{0,4},{4,0},{8,12},{12,8},{16,20},{20,16},{24,28},{28,24},{32,36},... | collective-permute-start | bytes 786440 | tf_op jit(solution)/shard_map/ppermute | solution.py:321
  51.9 6.1 %collective-permute-start.8 = (bf16[128,1024]{1,0:T(8,128)(2,1)S(1)}, bf16[128,1024]{1,0:T(8,128)(2,1)S(1)}, u32[]{:S(2)}, u32[]{:S(2)}) collective-permute-start(bf16[128,1024]{1,0:T(8,128)(2,1)S(1)} %collective-permute-done.7.far), channel_id=1, source_target_pairs={{0,1},{1,0},{2,3},{3,2},{4,5},{5,4},{6,7},{7,6},{8,9},{9,8},{10,11... | collective-permute-start | bytes 786440 | tf_op jit(solution)/shard_map/ppermute | solution.py:332
  55.1 3.4 %collective-permute-start.6 = (bf16[128,1024]{1,0:T(8,128)(2,1)S(1)}, bf16[128,1024]{1,0:T(8,128)(2,1)S(1)}, u32[]{:S(2)}, u32[]{:S(2)}) collective-permute-start(bf16[128,1024]{1,0:T(8,128)(2,1)S(1)} %collective-permute-done.5.near), channel_id=1, source_target_pairs={{0,1},{1,0},{2,3},{3,2},{4,5},{5,4},{6,7},{7,6},{8,9},{9,8},{10,11... | collective-permute-start | bytes 786440 | tf_op jit(solution)/shard_map/ppermute | solution.py:332
  57.0 6.9 %copy-start.1 = (bf16[256,128]{1,0:T(8,128)(2,1)S(1)}, bf16[256,128]{1,0:T(8,128)(2,1)}, u32[]{:S(2)}) copy-start(bf16[256,128]{1,0:T(8,128)(2,1)} %w_out.3) | copy-start | bytes 196612
  60.4 3.4 %collective-permute-start.9 = (bf16[128,1024]{1,0:T(8,128)(2,1)S(1)}, bf16[128,1024]{1,0:T(8,128)(2,1)S(1)}, u32[]{:S(2)}, u32[]{:S(2)}) collective-permute-start(bf16[128,1024]{1,0:T(8,128)(2,1)S(1)} %get-tuple-element.21.own), channel_id=1, source_target_pairs={{0,1},{1,0},{2,3},{3,2},{4,5},{5,4},{6,7},{7,6},{8,9},{9,8},{10,11... | collective-permute-start | bytes 786440 | tf_op jit(solution)/shard_map/ppermute | solution.py:332

commit v4 on v3

--- a/solution.py
+++ b/solution.py
@@ -137,7 +137,7 @@
     on_sides(near, body)
 
 
-def prop_in_kernel(far, acc, labels, dense, out):
+def prop_in_kernel(far, acc, labels, dense, out, plain):
     channels = far.shape[0]
     tag = jnp.broadcast_to(labels[...].astype(F32), (TAG, labels.shape[1])).astype(BF16)
     for t, at in tiles_of(far.shape[1]):
@@ -146,24 +146,24 @@
     def body(product):
         for t, at in tiles_of(far.shape[1]):
             total = acc[at, :] + product(dense, far, t, at)
-            out[:channels, at] = total.T.astype(BF16)
+            value = total.T.astype(BF16)
+            out[:channels, at] = value
+            plain[:, at] = value
 
     on_sides(False, body)
 
 
-def gather_kernel(first, second, third, fourth, prop_in, half, labels):
+def stack_kernel(near, far, both):
+    rows = near.shape[0]
+    both[:rows, :] = near[...]
+    both[rows:, :] = far[...]
+
+
+def gather(parts, place_part):
     yl = lax.axis_index("yl")
     co = lax.axis_index("co")
-    depth = prop_in.shape[0] // 4
-    for part, dy, dc in ((first, 0, 0), (second, 0, 1), (third, 1, 0), (fourth, 1, 1)):
-        place = (yl + dy - 2 * yl * dy) * 2 + (co + dc - 2 * co * dc)
-        rows = pl.ds(pl.multiple_of(place * depth, depth), depth)
-        prop_in[rows, :] = part[:depth, :]
-        labels[:, pl.ds(pl.multiple_of(place * TILE, TILE), TILE)] = part[
-            depth : depth + TAG, :TILE
-        ].astype(F32)
-    rows = half.shape[0]
-    half[...] = prop_in[pl.ds(pl.multiple_of(co * rows, rows), rows), :]
+    for part, (dy, dc) in zip(parts, ((0, 0), (0, 1), (1, 0), (1, 1))):
+        place_part(part, (yl + dy - 2 * yl * dy) * 2 + (co + dc - 2 * co * dc))
 
 
 def hidden_of(prop_in, w_in, hidden, pre_part):
@@ -177,25 +177,36 @@
     pre_part[...] = jnp.where(yl == 0, pre[: hid // 2], pre[hid // 2 :])
 
 
-def own_hidden_kernel(prop_in, w_in, dense, acc, pre_part, hidden):
+def own_hidden_kernel(
+    first, second, third, fourth, w_in, dense, acc, pre_part, prop_in, labels, hidden
+):
+    depth = prop_in.shape[0] // 4
+
+    def place_part(part, place):
+        prop_in[pl.ds(pl.multiple_of(place * depth, depth), depth), :] = part[:depth, :]
+        labels[:, pl.ds(pl.multiple_of(place * TILE, TILE), TILE)] = part[
+            depth : depth + TAG, :TILE
+        ].astype(F32)
+
+    gather((first, second, third, fourth), place_part)
     hidden_of(prop_in, w_in, hidden, pre_part)
     for t, at in tiles_of(hidden.shape[1]):
         acc[at, :] = own_product(dense, hidden, t, at)
 
 
-def join_halves(mine, other, out):
-    co = lax.axis_index("co")
-    half = mine.shape[0]
-    out[pl.ds(pl.multiple_of(co * half, half), half), :] = mine[...]
-    out[pl.ds(pl.multiple_of((1 - co) * half, half), half), :] = other[...]
-
-
 def prop_hidden_kernel(
-    near, near_other, far, far_other, w_in, acc, dense,
+    first, second, third, fourth, w_in, acc, dense,
     out, near_in, far_in, pre_near, pre_far,
     hidden, total,
 ):
-    join_halves(near, near_other, near_in)
+    depth = near_in.shape[0] // 4
+
+    def place_part(part, place):
+        rows = pl.ds(pl.multiple_of(place * depth, depth), depth)
+        near_in[rows, :] = part[:depth, :]
+        far_in[rows, :] = part[depth:, :]
+
+    gather((first, second, third, fourth), place_part)
     hidden_of(near_in, w_in, hidden, pre_near)
 
     def add_near(product):
@@ -203,7 +214,6 @@
             total[at, :] = acc[at, :] + product(dense, hidden, t, at)
 
     on_sides(True, add_near)
-    join_halves(far, far_other, far_in)
     hidden_of(far_in, w_in, hidden, pre_far)
 
     def add_far(product):
@@ -327,8 +337,8 @@
     return call(functools.partial(start_kernel, near), (own, piece, dense), sds(shape, F32))
 
 
-def flipped(value, axes):
-    shift = {("co",): 1, ("yl",): 2}[axes]
+def flipped(value, axis):
+    shift = {"co": 1, "yl": 2}[axis]
     return lax.ppermute(value, FEAT, [(i, i ^ shift) for i in range(4)])
 
 
@@ -344,41 +354,36 @@
 
     near, far = halo(features)
     dense = assemble(block_values, block_rows, block_cols, block_count, stripe)
-    first = call(
+    first, plain = call(
         prop_in_kernel,
         (far, start_part(features, near, dense, True), labels.reshape(1, mine), dense),
-        sds((depth + TAG, stripe), BF16),
-    )
-    third = flipped(first, ("yl",))
-    second = flipped(first, ("co",))
-    fourth = flipped(third, ("co",))
-    half_rows = 2 * depth
-    prop_in, half_in, label_rows = call(
-        gather_kernel,
-        (first, second, third, fourth),
-        (
-            sds((4 * depth, stripe), BF16),
-            sds((half_rows, stripe), BF16),
-            sds((TAG, stripe), F32),
-        ),
-    )
-    near, far = halo(half_in)
+        (sds((depth + TAG, stripe), BF16), sds((depth, stripe), BF16)),
+    )
+    near, far = halo(plain)
+    third = flipped(first, "yl")
+    second = flipped(first, "co")
+    fourth = flipped(third, "co")
+    both = call(stack_kernel, (near, far), sds((2 * depth, stripe), BF16))
+    both_third = flipped(both, "yl")
+    both_second = flipped(both, "co")
+    both_fourth = flipped(both_third, "co")
+
     pre = sds((hid // 4, stripe), F32)
     hidden = pltpu.VMEM((hid // 2, stripe), BF16)
-    acc, pre_own = call(
+    whole_in = sds((4 * depth, stripe), BF16)
+    acc, pre_own, prop_in, label_rows = call(
         own_hidden_kernel,
-        (prop_in, weight_in, dense),
-        (sds((stripe, hid // 2), F32), pre),
+        (first, second, third, fourth, weight_in, dense),
+        (sds((stripe, hid // 2), F32), pre, whole_in, sds((TAG, stripe), F32)),
         scratch=[hidden],
     )
-    whole_in = sds((4 * depth, stripe), BF16)
     prop_own, near_in, far_in, pre_near, pre_far = call(
         prop_hidden_kernel,
-        (near, flipped(near, ("co",)), far, flipped(far, ("co",)), weight_in, acc, dense),
+        (both, both_second, both_third, both_fourth, weight_in, acc, dense),
         (sds((hid // 2, stripe), BF16), whole_in, whole_in, pre, pre),
         scratch=[hidden, pltpu.VMEM((stripe, hid // 2), F32)],
     )
-    prop_other = flipped(prop_own, ("co",))
+    prop_other = flipped(prop_own, "co")
     logits, dl, share_out = call(
         functools.partial(logits_kernel, node_scale),
         (prop_own, prop_other, weight_out, label_rows),

time: 115 us -> 114 us (level)
  starting transfers between devices: 45.9 us -> 48.5 us
  waiting for transfers between devices: 8.66 us -> 6.22 us
  blocking collectives: 45.5 us -> 43.9 us
    ppermute x6 -> x7, starting transfers between devices: 17.1 us -> 20.6 us  [flipped(): return lax.ppermute(value, FEAT, [(i, i ^ shift) for i in range(4)])]
    ppermute x2, waiting for transfers between devices: 5.68 us -> 2.88 us  [halo(): far = lax.ppermute(value, BLK, far)]
    all_to_all x1, blocking collectives: 18 us -> 16.2 us  [on_device(): parts = lax.all_to_all(parts, 'z', 0, 0, tiled=True)]
    ppermute x2, waiting for transfers between devices: 0.01 us -> 1.2 us  [halo(): near = lax.ppermute(value, BLK, [(i, i ^ 1) for i in range(count)])]
    ppermute x6 -> x7, waiting for transfers between devices: 2.98 us -> 2.14 us  [flipped(): return lax.ppermute(value, FEAT, [(i, i ^ shift) for i in range(4)])]
  transfers between devices with their start and end apart: 10 -> 11, of which waited for: 5 -> 4; matrix products, arithmetic and copies ran while one was open for 0% -> 0% of each run, Pallas kernels for 5% -> 5%
where the time goes in v4:
time: 114 us; the launch traced here: 113 us
  starting transfers between devices  48.5 us (43%)
  blocking collectives  43.9 us (39%)
  Pallas kernels  13.1 us (11%)
  waiting for transfers between devices  6.22 us (5%)
  between operations  1.53 us (1%)
    ppermute x2, starting transfers between devices, halo(): far = lax.ppermute(value, BLK, far)  21.9 us
    ppermute x7, starting transfers between devices, flipped(): return lax.ppermute(value, FEAT, [(i, i ^ shift) for i in range(4)])  20.6 us
    all_to_all x1, blocking collectives, on_device(): parts = lax.all_to_all(parts, PLANE + FEAT, 0, 0, tiled=True)  18.5 us
    all_to_all x1, blocking collectives, on_device(): parts = lax.all_to_all(parts, 'z', 0, 0, tiled=True)  16.2 us
    pallas_call x10, Pallas kernels, call(): pl.pallas_call(kernel, in_specs=[whole()] * len(args), out_specs=[whole()...  9.86 us
    all_to_all x1, blocking collectives, on_device(): parts = lax.all_to_all(share, PLANE, 0, 0, tiled=True)  9.18 us
    ppermute x2, starting transfers between devices, halo(): near = lax.ppermute(value, BLK, [(i, i ^ 1) for i in range(count)])  5.99 us
    pallas_call x1, Pallas kernels, assemble(): pl.pallas_call(functools.partial(assemble_kernel, chunks), in_specs=[smem...  3.24 us
  transfers between devices with their start and end apart: 11, of which 4 were waited for; matrix products, arithmetic and copies ran while one was open for 0% of the time, Pallas kernels for 5%

profile of v4, /device:TPU:1, one launch (start us, length us, event | category | flops | bytes accessed | tf_op | source)
XLA Modules:
  0.0 113.3 jit_solution(8533773037329554785)
XLA Ops:
  0.6 0.0 copy-start.2
  0.6 4.1 %collective-permute-start.1 = (bf16[64,1024]{1,0:T(8,128)(2,1)}, bf16[64,1024]{1,0:T(8,128)(2,1)S(1)}, u32[]{:S(2)}, u32[]{:S(2)}) collective-permute-start(bf16[64,1024]{1,0:T(8,128)(2,1)} %own.1), channel_id=1, source_target_pairs={{0,4},{4,0},{8,12},{12,8},{16,20},{20,16},{24,28},{28,24},{32,36},... | collective-permute-start | bytes 393224 | tf_op jit(solution)/shard_map/ppermute | solution.py:331
  4.7 15.3 %collective-permute-start = (bf16[64,1024]{1,0:T(8,128)(2,1)}, bf16[64,1024]{1,0:T(8,128)(2,1)S(1)}, u32[]{:S(2)}, u32[]{:S(2)}) collective-permute-start(bf16[64,1024]{1,0:T(8,128)(2,1)} %own.1), channel_id=1, source_target_pairs={{0,508},{4,8},{8,4},{12,16},{16,12},{20,24},{24,20},{28,32},{32,28... | collective-permute-start | bytes 393224 | tf_op jit(solution)/shard_map/ppermute | solution.py:330
  20.7 3.2 %assemble.1.dense = bf16[1152,2304]{1,0:T(8,128)(2,1)S(1)} custom-call(s32[136]{0:T(256)} %rows_ref.1, s32[136]{0:T(256)} %cols_ref.1, s32[1]{0:T(128)S(6)} %copy.11.count_ref, bf16[136,128,128]{2,1,0:T(8,128)(2,1)} %blocks_hbm.1), custom_call_target="tpu_custom_call" | custom-call | tf_op jit(solution)/shard_map/assemble/pallas_call | solution.py:83
  23.9 0.0 copy-start.3
  23.9 0.0 copy-start
  23.9 0.0 collective-permute-done.1.piece
  23.9 0.0 copy-done.2
  23.9 1.0 shard_map.103.acc
  25.0 0.0 collective-permute-done.far
  25.0 0.0 copy-done.3
  25.0 0.6 shard_map.104
  25.6 6.6 %collective-permute-start.3 = (bf16[64,1024]{1,0:T(8,128)(2,1)S(1)}, bf16[64,1024]{1,0:T(8,128)(2,1)S(1)}, u32[]{:S(2)}, u32[]{:S(2)}) collective-permute-start(bf16[64,1024]{1,0:T(8,128)(2,1)S(1)} %get-tuple-element.19), channel_id=1, source_target_pairs={{0,508},{4,8},{8,4},{12,16},{16,12},{20,24},{24,20},{28,32},{32,28... | collective-permute-start | bytes 393224 | tf_op jit(solution)/shard_map/ppermute | solution.py:330
  32.2 1.9 %collective-permute-start.2 = (bf16[64,1024]{1,0:T(8,128)(2,1)S(1)}, bf16[64,1024]{1,0:T(8,128)(2,1)S(1)}, u32[]{:S(2)}, u32[]{:S(2)}) collective-permute-start(bf16[64,1024]{1,0:T(8,128)(2,1)S(1)} %get-tuple-element.19), channel_id=1, source_target_pairs={{0,4},{4,0},{8,12},{12,8},{16,20},{20,16},{24,28},{28,24},{32,36},... | collective-permute-start | bytes 393224 | tf_op jit(solution)/shard_map/ppermute | solution.py:331
  34.1 2.9 %collective-permute-done.3.far = bf16[64,1024]{1,0:T(8,128)(2,1)S(1)} collective-permute-done((bf16[64,1024]{1,0:T(8,128)(2,1)S(1)}, bf16[64,1024]{1,0:T(8,128)(2,1)S(1)}, u32[]{:S(2)}, u32[]{:S(2)}) %collective-permute-start.3) | collective-permute-done | bytes 131104 | tf_op jit(solution)/shard_map/ppermute | solution.py:330
  37.0 1.2 %collective-permute-done.2.near = bf16[64,1024]{1,0:T(8,128)(2,1)S(1)} collective-permute-done((bf16[64,1024]{1,0:T(8,128)(2,1)S(1)}, bf16[64,1024]{1,0:T(8,128)(2,1)S(1)}, u32[]{:S(2)}, u32[]{:S(2)}) %collective-permute-start.2) | collective-permute-done | bytes 131104 | tf_op jit(solution)/shard_map/ppermute | solution.py:331
  38.2 2.3 %collective-permute-start.5 = (bf16[128,1024]{1,0:T(8,128)(2,1)S(1)}, bf16[128,1024]{1,0:T(8,128)(2,1)S(1)}, u32[]{:S(2)}, u32[]{:S(2)}) collective-permute-start(bf16[128,1024]{1,0:T(8,128)(2,1)S(1)} %shard_map.105.first), channel_id=1, source_target_pairs={{0,2},{1,3},{2,0},{3,1},{4,6},{5,7},{6,4},{7,5},{8,10},{9,11},{10,... | collective-permute-start | bytes 786440 | tf_op jit(solution)/shard_map/ppermute | solution.py:342
  40.5 0.0 copy-start.1
  40.6 3.1 %collective-permute-start.8 = (bf16[72,1024]{1,0:T(8,128)(2,1)S(1)}, bf16[72,1024]{1,0:T(8,128)(2,1)S(1)}, u32[]{:S(2)}, u32[]{:S(2)}) collective-permute-start(bf16[72,1024]{1,0:T(8,128)(2,1)S(1)} %get-tuple-element.20.first), channel_id=1, source_target_pairs={{0,2},{1,3},{2,0},{3,1},{4,6},{5,7},{6,4},{7,5},{8,10},{9,11},{10,... | collective-permute-start | bytes 442376 | tf_op jit(solution)/shard_map/ppermute | solution.py:342
  43.7 5.7 %collective-permute-start.4 = (bf16[128,1024]{1,0:T(8,128)(2,1)S(1)}, bf16[128,1024]{1,0:T(8,128)(2,1)S(1)}, u32[]{:S(2)}, u32[]{:S(2)}) collective-permute-start(bf16[128,1024]{1,0:T(8,128)(2,1)S(1)} %shard_map.105.first), channel_id=1, source_target_pairs={{0,1},{1,0},{2,3},{3,2},{4,5},{5,4},{6,7},{7,6},{8,9},{9,8},{10,11... | collective-permute-start | bytes 786440 | tf_op jit(solution)/shard_map/ppermute | solution.py:342
  49.4 0.0 collective-permute-done.5.third
  49.4 2.9 %collective-permute-start.6 = (bf16[128,1024]{1,0:T(8,128)(2,1)S(1)}, bf16[128,1024]{1,0:T(8,128)(2,1)S(1)}, u32[]{:S(2)}, u32[]{:S(2)}) collective-permute-start(bf16[128,1024]{1,0:T(8,128)(2,1)S(1)} %collective-permute-done.5.third), channel_id=1, source_target_pairs={{0,1},{1,0},{2,3},{3,2},{4,5},{5,4},{6,7},{7,6},{8,9},{9,8},{10,11... | collective-permute-start | bytes 786440 | tf_op jit(solution)/shard_map/ppermute | solution.py:342
  52.3 1.9 %collective-permute-start.7 = (bf16[72,1024]{1,0:T(8,128)(2,1)S(1)}, bf16[72,1024]{1,0:T(8,128)(2,1)S(1)}, u32[]{:S(2)}, u32[]{:S(2)}) collective-permute-start(bf16[72,1024]{1,0:T(8,128)(2,1)S(1)} %get-tuple-element.20.first), channel_id=1, source_target_pairs={{0,1},{1,0},{2,3},{3,2},{4,5},{5,4},{6,7},{7,6},{8,9},{9,8},{10,11... | collective-permute-start | bytes 442376 | tf_op jit(solution)/shard_map/ppermute | solution.py:342
  54.3 0.0 collective-permute-done.8.third
  54.3 2.4 %collective-permute-start.9 = (bf16[72,1024]{1,0:T(8,128)(2,1)S(1)}, bf16[72,1024]{1,0:T(8,128)(2,1)S(1)}, u32[]{:S(2)}, u32[]{:S(2)}) collective-permute-start(bf16[72,1024]{1,0:T(8,128)(2,1)S(1)} %collective-permute-done.8.third), channel_id=1, source_target_pairs={{0,1},{1,0},{2,3},{3,2},{4,5},{5,4},{6,7},{7,6},{8,9},{9,8},{10,11... | collective-permute-start | bytes 442376 | tf_op jit(solution)/shard_map/ppermute | solution.py:342
  56.7 0.0 collective-permute-done.7.second
  56.7 1.0 collective-permute-done.9.fourth
  57.7 0.0 copy-done
  57.7 1.0 shard_map.106
  58.7 0.0 collective-permute-done.4.second
  58.7 0.0 collective-permute-done.6.fourth
  58.7 1.9 %shard_map.107 = (bf16[128,1024]{1,0:T(8,128)(2,1)S(1)}, bf16[256,1024]{1,0:T(8,128)(2,1)S(1)}, bf16[256,1024]{1,0:T(8,128)(2,1)S(1)}, f32[64,1024]{1,0:T(8,128)S(1)}, f32[64,1024]{1,0:T(8,128)S(1)}) custom-call(bf16[128,1024]{1,0:T(8,128)(2,1)S(1)} %shard_map.105.first, bf16[128,1024]{1,0:T(8,128)(2,1)S(1)} %collective-permute-done.4.second, ...), custom_call_target="tpu_custom_call" | custom-call | tf_op jit(solution)/shard_map/pallas_call | solution.py:317
  60.6 2.3 %collective-permute-start.10 = (bf16[128,1024]{1,0:T(8,128)(2,1)S(1)}, bf16[128,1024]{1,0:T(8,128)(2,1)S(1)}, u32[]{:S(2)}, u32[]{:S(2)}) collective-permute-start(bf16[128,1024]{1,0:T(8,128)(2,1)S(1)} %get-tuple-element.22.own), channel_id=1, source_target_pairs={{0,1},{1,0},{2,3},{3,2},{4,5},{5,4},{6,7},{7,6},{8,9},{9,8},{10,11... | collective-permute-start | bytes 786440 | tf_op jit(solution)/shard_map/ppermute | solution.py:342
  62.9 1.2 %collective-permute-done.10.other = bf16[128,1024]{1,0:T(8,128)(2,1)S(1)} collective-permute-done((bf16[128,1024]{1,0:T(8,128)(2,1)S(1)}, bf16[128,1024]{1,0:T(8,128)(2,1)S(1)}, u32[]{:S(2)}, u32[]{:S(2)}) %collective-permute-start.10) | collective-permute-done | bytes 262176 | tf_op jit(solution)/shard_map/ppermute | solution.py:342
  64.0 0.0 copy-done.1
  64.0 1.2 %shard_map.108 = (f32[128,256]{1,0:T(8,128)}, bf16[128,1024]{1,0:T(8,128)(2,1)S(1)}, f32[64,128]{1,0:T(8,128)S(1)}) custom-call(bf16[128,1024]{1,0:T(8,128)(2,1)S(1)} %get-tuple-element.22.own, bf16[128,1024]{1,0:T(8,128)(2,1)S(1)} %collective-permute-done.10.other, bf16[256,128]{1,0:T(8,128)(2,1)S(1)} %copy-done.1, f32[8,1024]{1,0:T(8,128)S(1)} %get-tuple-element.23.labels), custom_call_target="tpu_custom_call" | custom-call | tf_op jit(solution)/shard_map/pallas_call | solution.py:317
  65.2 3.3 %shard_map.109 = f32[8,8,384]{2,1,0:T(8,128)S(1)} custom-call(bf16[128,1024]{1,0:T(8,128)(2,1)S(1)} %get-tuple-element.25.dl, bf16[1152,2304]{1,0:T(8,128)(2,1)S(1)} %assemble.1.dense, bf16[256,128]{1,0:T(8,128)(2,1)S(1)} %copy-done.1, f32[64,1024]{1,0:T(8,128)S(1)} %get-tuple-element.26.pre_own, f32[64,1024]{1,0:T(8,128)S(1)} %get-tuple-element.27.pre_near, ...), custom_call_target="tpu_custom_call" | custom-call | tf_op jit(solution)/shard_map/pallas_call | solution.py:317
  68.5 9.2 %all_to_all.15.parts = f32[8,8,384]{2,1,0:T(8,128)S(1)} all-to-all(f32[8,8,384]{2,1,0:T(8,128)S(1)} %shard_map.109), channel_id=1, replica_groups=mesh['yh'=2,'z'=16,'x'=4,'yl'=2,'co'=2] {'yh','x'}, dimensions={0} | all-to-all | bytes 196608 | tf_op jit(solution)/shard_map/all_to_all | solution.py:417
  77.7 16.2 %all_to_all.16.parts = f32[16,8,384]{2,1,0:T(8,128)S(1)} all-to-all(f32[16,8,384]{2,1,0:T(8,128)S(1)} %shard_map.110), channel_id=1, replica_groups=mesh['yh'=2,'z'=16,'x'=4,'yl'=2,'co'=2] {'z'}, dimensions={0} | all-to-all | bytes 393216 | tf_op jit(solution)/shard_map/all_to_all | solution.py:419
  94.0 18.5 %all_to_all.17.parts = f32[32,8,384]{2,1,0:T(8,128)S(1)} all-to-all(f32[32,8,384]{2,1,0:T(8,128)S(1)} %shard_map.111), channel_id=1, replica_groups=mesh['yh'=2,'z'=16,'x'=4,'yl'=2,'co'=2] {'yh','x','yl','co'}, dimensions={0} | all-to-all | bytes 786432 | tf_op jit(solution)/shard_map/all_to_all | solution.py:421
  112.4 0.8 shard_map.112
  (3 shorter events, 0.1 us)
Async XLA Ops:
  0.6 23.3 %copy-start.2 = (bf16[64,1024]{1,0:T(8,128)(2,1)S(1)}, bf16[64,1024]{1,0:T(8,128)(2,1)}, u32[]{:S(2)}) copy-start(bf16[64,1024]{1,0:T(8,128)(2,1)} %own.1) | copy-start | bytes 393220
  0.6 23.3 %collective-permute-start.1 = (bf16[64,1024]{1,0:T(8,128)(2,1)}, bf16[64,1024]{1,0:T(8,128)(2,1)S(1)}, u32[]{:S(2)}, u32[]{:S(2)}) collective-permute-start(bf16[64,1024]{1,0:T(8,128)(2,1)} %own.1), channel_id=1, source_target_pairs={{0,4},{4,0},{8,12},{12,8},{16,20},{20,16},{24,28},{28,24},{32,36},... | collective-permute-start | bytes 393224 | tf_op jit(solution)/shard_map/ppermute | solution.py:331
  4.7 20.3 %collective-permute-start = (bf16[64,1024]{1,0:T(8,128)(2,1)}, bf16[64,1024]{1,0:T(8,128)(2,1)S(1)}, u32[]{:S(2)}, u32[]{:S(2)}) collective-permute-start(bf16[64,1024]{1,0:T(8,128)(2,1)} %own.1), channel_id=1, source_target_pairs={{0,508},{4,8},{8,4},{12,16},{16,12},{20,24},{24,20},{28,32},{32,28... | collective-permute-start | bytes 393224 | tf_op jit(solution)/shard_map/ppermute | solution.py:330
  23.9 1.1 copy-start.3
  23.9 33.8 %copy-start = (bf16[256,256]{1,0:T(8,128)(2,1)S(1)}, bf16[256,256]{1,0:T(8,128)(2,1)}, u32[]{:S(2)}) copy-start(bf16[256,256]{1,0:T(8,128)(2,1)} %w_in.3) | copy-start | bytes 393220
  25.6 11.4 %collective-permute-start.3 = (bf16[64,1024]{1,0:T(8,128)(2,1)S(1)}, bf16[64,1024]{1,0:T(8,128)(2,1)S(1)}, u32[]{:S(2)}, u32[]{:S(2)}) collective-permute-start(bf16[64,1024]{1,0:T(8,128)(2,1)S(1)} %get-tuple-element.19), channel_id=1, source_target_pairs={{0,508},{4,8},{8,4},{12,16},{16,12},{20,24},{24,20},{28,32},{32,28... | collective-permute-start | bytes 393224 | tf_op jit(solution)/shard_map/ppermute | solution.py:330
  32.2 6.0 %collective-permute-start.2 = (bf16[64,1024]{1,0:T(8,128)(2,1)S(1)}, bf16[64,1024]{1,0:T(8,128)(2,1)S(1)}, u32[]{:S(2)}, u32[]{:S(2)}) collective-permute-start(bf16[64,1024]{1,0:T(8,128)(2,1)S(1)} %get-tuple-element.19), channel_id=1, source_target_pairs={{0,4},{4,0},{8,12},{12,8},{16,20},{20,16},{24,28},{28,24},{32,36},... | collective-permute-start | bytes 393224 | tf_op jit(solution)/shard_map/ppermute | solution.py:331
  38.2 11.2 %collective-permute-start.5 = (bf16[128,1024]{1,0:T(8,128)(2,1)S(1)}, bf16[128,1024]{1,0:T(8,128)(2,1)S(1)}, u32[]{:S(2)}, u32[]{:S(2)}) collective-permute-start(bf16[128,1024]{1,0:T(8,128)(2,1)S(1)} %shard_map.105.first), channel_id=1, source_target_pairs={{0,2},{1,3},{2,0},{3,1},{4,6},{5,7},{6,4},{7,5},{8,10},{9,11},{10,... | collective-permute-start | bytes 786440 | tf_op jit(solution)/shard_map/ppermute | solution.py:342
  40.5 23.5 %copy-start.1 = (bf16[256,128]{1,0:T(8,128)(2,1)S(1)}, bf16[256,128]{1,0:T(8,128)(2,1)}, u32[]{:S(2)}) copy-start(bf16[256,128]{1,0:T(8,128)(2,1)} %w_out.3) | copy-start | bytes 196612
  40.6 13.7 %collective-permute-start.8 = (bf16[72,1024]{1,0:T(8,128)(2,1)S(1)}, bf16[72,1024]{1,0:T(8,128)(2,1)S(1)}, u32[]{:S(2)}, u32[]{:S(2)}) collective-permute-start(bf16[72,1024]{1,0:T(8,128)(2,1)S(1)} %get-tuple-element.20.first), channel_id=1, source_target_pairs={{0,2},{1,3},{2,0},{3,1},{4,6},{5,7},{6,4},{7,5},{8,10},{9,11},{10,... | collective-permute-start | bytes 442376 | tf_op jit(solution)/shard_map/ppermute | solution.py:342
  43.7 15.0 %collective-permute-start.4 = (bf16[128,1024]{1,0:T(8,128)(2,1)S(1)}, bf16[128,1024]{1,0:T(8,128)(2,1)S(1)}, u32[]{:S(2)}, u32[]{:S(2)}) collective-permute-start(bf16[128,1024]{1,0:T(8,128)(2,1)S(1)} %shard_map.105.first), channel_id=1, source_target_pairs={{0,1},{1,0},{2,3},{3,2},{4,5},{5,4},{6,7},{7,6},{8,9},{9,8},{10,11... | collective-permute-start | bytes 786440 | tf_op jit(solution)/shard_map/ppermute | solution.py:342
  49.4 9.3 %collective-permute-start.6 = (bf16[128,1024]{1,0:T(8,128)(2,1)S(1)}, bf16[128,1024]{1,0:T(8,128)(2,1)S(1)}, u32[]{:S(2)}, u32[]{:S(2)}) collective-permute-start(bf16[128,1024]{1,0:T(8,128)(2,1)S(1)} %collective-permute-done.5.third), channel_id=1, source_target_pairs={{0,1},{1,0},{2,3},{3,2},{4,5},{5,4},{6,7},{7,6},{8,9},{9,8},{10,11... | collective-permute-start | bytes 786440 | tf_op jit(solution)/shard_map/ppermute | solution.py:342
  52.3 4.4 %collective-permute-start.7 = (bf16[72,1024]{1,0:T(8,128)(2,1)S(1)}, bf16[72,1024]{1,0:T(8,128)(2,1)S(1)}, u32[]{:S(2)}, u32[]{:S(2)}) collective-permute-start(bf16[72,1024]{1,0:T(8,128)(2,1)S(1)} %get-tuple-element.20.first), channel_id=1, source_target_pairs={{0,1},{1,0},{2,3},{3,2},{4,5},{5,4},{6,7},{7,6},{8,9},{9,8},{10,11... | collective-permute-start | bytes 442376 | tf_op jit(solution)/shard_map/ppermute | solution.py:342
  54.3 3.4 %collective-permute-start.9 = (bf16[72,1024]{1,0:T(8,128)(2,1)S(1)}, bf16[72,1024]{1,0:T(8,128)(2,1)S(1)}, u32[]{:S(2)}, u32[]{:S(2)}) collective-permute-start(bf16[72,1024]{1,0:T(8,128)(2,1)S(1)} %collective-permute-done.8.third), channel_id=1, source_target_pairs={{0,1},{1,0},{2,3},{3,2},{4,5},{5,4},{6,7},{7,6},{8,9},{9,8},{10,11... | collective-permute-start | bytes 442376 | tf_op jit(solution)/shard_map/ppermute | solution.py:342
  60.6 3.4 %collective-permute-start.10 = (bf16[128,1024]{1,0:T(8,128)(2,1)S(1)}, bf16[128,1024]{1,0:T(8,128)(2,1)S(1)}, u32[]{:S(2)}, u32[]{:S(2)}) collective-permute-start(bf16[128,1024]{1,0:T(8,128)(2,1)S(1)} %get-tuple-element.22.own), channel_id=1, source_target_pairs={{0,1},{1,0},{2,3},{3,2},{4,5},{5,4},{6,7},{7,6},{8,9},{9,8},{10,11... | collective-permute-start | bytes 786440 | tf_op jit(solution)/shard_map/ppermute | solution.py:342

commit v5 on v4

--- a/solution.py
+++ b/solution.py
@@ -166,19 +166,19 @@
         place_part(part, (yl + dy - 2 * yl * dy) * 2 + (co + dc - 2 * co * dc))
 
 
-def hidden_of(prop_in, w_in, hidden, pre_part):
+def hidden_of(prop_in, w_in, hidden, pre_part, whole_pre):
     yl = lax.axis_index("yl")
     co = lax.axis_index("co")
-    hid = hidden.shape[0]
-    weight = w_in[:, pl.ds(pl.multiple_of(co * hid, hid), hid)]
-    pre = dot(weight, prop_in[...], TN)
+    pre = dot(w_in[...], prop_in[...], TN)
     inner = GELU_A * (pre + GELU_B * (pre * pre * pre))
     hidden[...] = (pre * (0.5 * (1.0 + jnp.tanh(inner)))).astype(BF16)
-    pre_part[...] = jnp.where(yl == 0, pre[: hid // 2], pre[hid // 2 :])
+    whole_pre[...] = pre
+    rows = pre_part.shape[0]
+    pre_part[...] = whole_pre[pl.ds(pl.multiple_of((co * 2 + yl) * rows, rows), rows), :]
 
 
 def own_hidden_kernel(
-    first, second, third, fourth, w_in, dense, acc, pre_part, prop_in, labels, hidden
+    first, second, third, fourth, w_in, dense, acc, pre_part, prop_in, labels, hidden, whole_pre
 ):
     depth = prop_in.shape[0] // 4
 
@@ -189,7 +189,7 @@
         ].astype(F32)
 
     gather((first, second, third, fourth), place_part)
-    hidden_of(prop_in, w_in, hidden, pre_part)
+    hidden_of(prop_in, w_in, hidden, pre_part, whole_pre)
     for t, at in tiles_of(hidden.shape[1]):
         acc[at, :] = own_product(dense, hidden, t, at)
 
@@ -197,7 +197,7 @@
 def prop_hidden_kernel(
     first, second, third, fourth, w_in, acc, dense,
     out, near_in, far_in, pre_near, pre_far,
-    hidden, total,
+    hidden, whole_pre, total,
 ):
     depth = near_in.shape[0] // 4
 
@@ -207,14 +207,14 @@
         far_in[rows, :] = part[depth:, :]
 
     gather((first, second, third, fourth), place_part)
-    hidden_of(near_in, w_in, hidden, pre_near)
+    hidden_of(near_in, w_in, hidden, pre_near, whole_pre)
 
     def add_near(product):
         for t, at in tiles_of(out.shape[1]):
             total[at, :] = acc[at, :] + product(dense, hidden, t, at)
 
     on_sides(True, add_near)
-    hidden_of(far_in, w_in, hidden, pre_far)
+    hidden_of(far_in, w_in, hidden, pre_far, whole_pre)
 
     def add_far(product):
         for t, at in tiles_of(out.shape[1]):
@@ -223,13 +223,10 @@
     on_sides(False, add_far)
 
 
-def logits_kernel(scale, own, other, w_out, labels, out, dl, share, scores):
+def logits_kernel(scale, prop_hid, w_out, labels, out, dl, share, scores):
     yl = lax.axis_index("yl")
     co = lax.axis_index("co")
-    hid = own.shape[0]
-    w_own = w_out[pl.ds(pl.multiple_of(co * hid, hid), hid), :]
-    w_other = w_out[pl.ds(pl.multiple_of((1 - co) * hid, hid), hid), :]
-    logit = dot(w_own, own[...], TN) + dot(w_other, other[...], TN)
+    logit = dot(w_out[...], prop_hid[...], TN)
     scores[...] = logit
     start = pl.multiple_of((yl * 2 + co) * out.shape[1], out.shape[1])
     out[...] = scores[:, pl.ds(start, out.shape[1])]
@@ -241,18 +238,25 @@
     dlogits = ((probability - onehot) * scale).astype(BF16)
     dl[...] = dlogits
     rows = share.shape[0]
-    mine = own[pl.ds(pl.multiple_of(yl * rows, rows), rows), :]
+    mine = prop_hid[pl.ds(pl.multiple_of((co * 2 + yl) * rows, rows), rows), :]
     share[...] = dot(mine, dlogits, NT)
 
 
 def grads_kernel(
-    dl, dense, w_out, pre_own, pre_near, pre_far, own_in, near_in, far_in, share_out, out
+    dl, dense, w_out, pre_own, pre_near, pre_far, own_in, near_in, far_in, share_out, out, terms
 ):
     odd = lax.bitwise_and(lax.axis_index("x"), 1) == 1
     yl = lax.axis_index("yl")
     co = lax.axis_index("co")
     half = pre_own.shape[0]
     w = w_out[pl.ds(pl.multiple_of((co * 2 + yl) * half, half), half), :]
+    unspread = dot(w, dl[...], NN)
+    high = unspread.astype(BF16)
+    rest = unspread - high.astype(F32)
+    middle = rest.astype(BF16)
+    terms[:half, :] = high
+    terms[half : 2 * half, :] = middle
+    terms[2 * half :, :] = (rest - middle.astype(F32)).astype(BF16)
     tiles = tiles_of(dl.shape[1])
     reach = dense.shape[1] // TILE
     share = None
@@ -260,13 +264,9 @@
         spread = None
         for t, at in tiles:
             if 0 <= block - t < reach:
-                part = dot(dl[:, at], dense[at, (block - t) * TILE : (block - t + 1) * TILE], NN)
+                part = dot(terms[:, at], dense[at, (block - t) * TILE : (block - t + 1) * TILE], NN)
                 spread = part if spread is None else spread + part
-        high = spread.astype(BF16)
-        rest = spread - high.astype(F32)
-        middle = rest.astype(BF16)
-        low = (rest - middle.astype(F32)).astype(BF16)
-        back = dot(w, high, NN) + (dot(w, middle, NN) + dot(w, low, NN))
+        back = spread[:half] + (spread[half : 2 * half] + spread[2 * half :])
         stripe, tile = divmod(block, len(tiles))
         at = tiles[tile][1]
         if stripe == 1:
@@ -282,8 +282,9 @@
         grad = back * slope
         high = grad.astype(BF16)
         low = (grad - high.astype(F32)).astype(BF16)
-        part = dot(high, prop_in, NT) + dot(low, prop_in, NT)
+        part = dot(jnp.concatenate([high, low], axis=0), prop_in, NT)
         share = part if share is None else share + part
+    share = share[:half] + share[half:]
     pieces, rows, _ = out.shape
     width = share.shape[1]
     for p in range(pieces):
@@ -369,24 +370,25 @@
     both_fourth = flipped(both_third, "co")
 
     pre = sds((hid // 4, stripe), F32)
-    hidden = pltpu.VMEM((hid // 2, stripe), BF16)
+    hidden = pltpu.VMEM((hid, stripe), BF16)
+    whole_pre = pltpu.VMEM((hid, stripe), F32)
     whole_in = sds((4 * depth, stripe), BF16)
     acc, pre_own, prop_in, label_rows = call(
         own_hidden_kernel,
         (first, second, third, fourth, weight_in, dense),
-        (sds((stripe, hid // 2), F32), pre, whole_in, sds((TAG, stripe), F32)),
-        scratch=[hidden],
-    )
-    prop_own, near_in, far_in, pre_near, pre_far = call(
+        (sds((stripe, hid), F32), pre, whole_in, sds((TAG, stripe), F32)),
+        scratch=[hidden, whole_pre],
+    )
+    prop_hid, near_in, far_in, pre_near, pre_far = call(
         prop_hidden_kernel,
         (both, both_second, both_third, both_fourth, weight_in, acc, dense),
-        (sds((hid // 2, stripe), BF16), whole_in, whole_in, pre, pre),
-        scratch=[hidden, pltpu.VMEM((stripe, hid // 2), F32)],
-    )
-    prop_other = flipped(prop_own, "co")
+        (sds((hid, stripe), BF16), whole_in, whole_in, pre, pre),
+        scratch=[hidden, whole_pre, pltpu.VMEM((stripe, hid), F32)],
+        mib=24,
+    )
     logits, dl, share_out = call(
         functools.partial(logits_kernel, node_scale),
-        (prop_own, prop_other, weight_out, label_rows),
+        (prop_hid, weight_out, label_rows),
         (
             sds((classes, mine), F32),
             sds((classes, stripe), BF16),
@@ -413,6 +415,7 @@
             share_out,
         ),
         sds((plane, rows, width), F32),
+        scratch=[pltpu.VMEM((3 * hid // 4, stripe), BF16)],
     )
     parts = lax.all_to_all(share, PLANE, 0, 0, tiled=True)
     parts = call(sum_kernel, (parts,), sds((lax.axis_size("z"), rows, width), F32))

time: 114 us -> 110 us (0.965)
  starting transfers between devices: 48.5 us -> 46.3 us
  waiting for transfers between devices: 6.22 us -> 5.07 us
    ppermute x7 -> x6, starting transfers between devices: 20.6 us -> 18.4 us  [flipped(): return lax.ppermute(value, FEAT, [(i, i ^ shift) for i in range(4)])]
    ppermute x7 -> x6, waiting for transfers between devices: 2.14 us -> 0.99 us  [flipped(): return lax.ppermute(value, FEAT, [(i, i ^ shift) for i in range(4)])]
  transfers between devices with their start and end apart: 11 -> 10, of which waited for: 4 -> 3; matrix products, arithmetic and copies ran while one was open for 0% -> 0% of each run, Pallas kernels for 5% -> 5%
where the time goes in v5:
time: 110 us; the launch traced here: 109 us
  starting transfers between devices  46.3 us (42%)
  blocking collectives  43.9 us (40%)
  Pallas kernels  12.7 us (12%)
  waiting for transfers between devices  5.07 us (5%)
  between operations  1.53 us (1%)
    ppermute x2, starting transfers between devices, halo(): far = lax.ppermute(value, BLK, far)  21.9 us
    all_to_all x1, blocking collectives, on_device(): parts = lax.all_to_all(parts, PLANE + FEAT, 0, 0, tiled=True)  18.5 us
    ppermute x6, starting transfers between devices, flipped(): return lax.ppermute(value, FEAT, [(i, i ^ shift) for i in range(4)])  18.4 us
    all_to_all x1, blocking collectives, on_device(): parts = lax.all_to_all(parts, 'z', 0, 0, tiled=True)  16.2 us
    pallas_call x10, Pallas kernels, call(): pl.pallas_call(kernel, in_specs=[whole()] * len(args), out_specs=[whole()...  9.48 us
    all_to_all x1, blocking collectives, on_device(): parts = lax.all_to_all(share, PLANE, 0, 0, tiled=True)  9.18 us
    ppermute x2, starting transfers between devices, halo(): near = lax.ppermute(value, BLK, [(i, i ^ 1) for i in range(count)])  5.99 us
    pallas_call x1, Pallas kernels, assemble(): pl.pallas_call(functools.partial(assemble_kernel, chunks), in_specs=[smem...  3.24 us
  transfers between devices with their start and end apart: 10, of which 3 were waited for; matrix products, arithmetic and copies ran while one was open for 0% of the time, Pallas kernels for 5%

profile of v5, /device:TPU:1, one launch (start us, length us, event | category | flops | bytes accessed | tf_op | source)
XLA Modules:
  0.0 109.5 jit_solution(5014294254710587758)
XLA Ops:
  0.6 0.0 copy-start.2
  0.6 4.1 %collective-permute-start.1 = (bf16[64,1024]{1,0:T(8,128)(2,1)}, bf16[64,1024]{1,0:T(8,128)(2,1)S(1)}, u32[]{:S(2)}, u32[]{:S(2)}) collective-permute-start(bf16[64,1024]{1,0:T(8,128)(2,1)} %own.1), channel_id=1, source_target_pairs={{0,4},{4,0},{8,12},{12,8},{16,20},{20,16},{24,28},{28,24},{32,36},... | collective-permute-start | bytes 393224 | tf_op jit(solution)/shard_map/ppermute | solution.py:332
  4.7 15.3 %collective-permute-start = (bf16[64,1024]{1,0:T(8,128)(2,1)}, bf16[64,1024]{1,0:T(8,128)(2,1)S(1)}, u32[]{:S(2)}, u32[]{:S(2)}) collective-permute-start(bf16[64,1024]{1,0:T(8,128)(2,1)} %own.1), channel_id=1, source_target_pairs={{0,508},{4,8},{8,4},{12,16},{16,12},{20,24},{24,20},{28,32},{32,28... | collective-permute-start | bytes 393224 | tf_op jit(solution)/shard_map/ppermute | solution.py:331
  20.7 3.2 %assemble.1.dense = bf16[1152,2304]{1,0:T(8,128)(2,1)S(1)} custom-call(s32[136]{0:T(256)} %rows_ref.1, s32[136]{0:T(256)} %cols_ref.1, s32[1]{0:T(128)S(6)} %copy.11.count_ref, bf16[136,128,128]{2,1,0:T(8,128)(2,1)} %blocks_hbm.1), custom_call_target="tpu_custom_call" | custom-call | tf_op jit(solution)/shard_map/assemble/pallas_call | solution.py:83
  23.9 0.0 copy-start.3
  23.9 0.0 copy-start
  23.9 0.0 collective-permute-done.1.piece
  23.9 0.0 copy-done.2
  23.9 1.0 shard_map.103.acc
  25.0 0.0 collective-permute-done.far
  25.0 0.0 copy-done.3
  25.0 0.6 shard_map.104
  25.6 6.6 %collective-permute-start.3 = (bf16[64,1024]{1,0:T(8,128)(2,1)S(1)}, bf16[64,1024]{1,0:T(8,128)(2,1)S(1)}, u32[]{:S(2)}, u32[]{:S(2)}) collective-permute-start(bf16[64,1024]{1,0:T(8,128)(2,1)S(1)} %get-tuple-element.19), channel_id=1, source_target_pairs={{0,508},{4,8},{8,4},{12,16},{16,12},{20,24},{24,20},{28,32},{32,28... | collective-permute-start | bytes 393224 | tf_op jit(solution)/shard_map/ppermute | solution.py:331
  32.2 1.9 %collective-permute-start.2 = (bf16[64,1024]{1,0:T(8,128)(2,1)S(1)}, bf16[64,1024]{1,0:T(8,128)(2,1)S(1)}, u32[]{:S(2)}, u32[]{:S(2)}) collective-permute-start(bf16[64,1024]{1,0:T(8,128)(2,1)S(1)} %get-tuple-element.19), channel_id=1, source_target_pairs={{0,4},{4,0},{8,12},{12,8},{16,20},{20,16},{24,28},{28,24},{32,36},... | collective-permute-start | bytes 393224 | tf_op jit(solution)/shard_map/ppermute | solution.py:332
  34.1 2.9 %collective-permute-done.3.far = bf16[64,1024]{1,0:T(8,128)(2,1)S(1)} collective-permute-done((bf16[64,1024]{1,0:T(8,128)(2,1)S(1)}, bf16[64,1024]{1,0:T(8,128)(2,1)S(1)}, u32[]{:S(2)}, u32[]{:S(2)}) %collective-permute-start.3) | collective-permute-done | bytes 131104 | tf_op jit(solution)/shard_map/ppermute | solution.py:331
  37.0 1.2 %collective-permute-done.2.near = bf16[64,1024]{1,0:T(8,128)(2,1)S(1)} collective-permute-done((bf16[64,1024]{1,0:T(8,128)(2,1)S(1)}, bf16[64,1024]{1,0:T(8,128)(2,1)S(1)}, u32[]{:S(2)}, u32[]{:S(2)}) %collective-permute-start.2) | collective-permute-done | bytes 131104 | tf_op jit(solution)/shard_map/ppermute | solution.py:332
  38.2 2.3 %collective-permute-start.5 = (bf16[128,1024]{1,0:T(8,128)(2,1)S(1)}, bf16[128,1024]{1,0:T(8,128)(2,1)S(1)}, u32[]{:S(2)}, u32[]{:S(2)}) collective-permute-start(bf16[128,1024]{1,0:T(8,128)(2,1)S(1)} %shard_map.105.first), channel_id=1, source_target_pairs={{0,2},{1,3},{2,0},{3,1},{4,6},{5,7},{6,4},{7,5},{8,10},{9,11},{10,... | collective-permute-start | bytes 786440 | tf_op jit(solution)/shard_map/ppermute | solution.py:343
  40.5 0.0 copy-start.1
  40.6 3.1 %collective-permute-start.8 = (bf16[72,1024]{1,0:T(8,128)(2,1)S(1)}, bf16[72,1024]{1,0:T(8,128)(2,1)S(1)}, u32[]{:S(2)}, u32[]{:S(2)}) collective-permute-start(bf16[72,1024]{1,0:T(8,128)(2,1)S(1)} %get-tuple-element.20.first), channel_id=1, source_target_pairs={{0,2},{1,3},{2,0},{3,1},{4,6},{5,7},{6,4},{7,5},{8,10},{9,11},{10,... | collective-permute-start | bytes 442376 | tf_op jit(solution)/shard_map/ppermute | solution.py:343
  43.7 5.7 %collective-permute-start.4 = (bf16[128,1024]{1,0:T(8,128)(2,1)S(1)}, bf16[128,1024]{1,0:T(8,128)(2,1)S(1)}, u32[]{:S(2)}, u32[]{:S(2)}) collective-permute-start(bf16[128,1024]{1,0:T(8,128)(2,1)S(1)} %shard_map.105.first), channel_id=1, source_target_pairs={{0,1},{1,0},{2,3},{3,2},{4,5},{5,4},{6,7},{7,6},{8,9},{9,8},{10,11... | collective-permute-start | bytes 786440 | tf_op jit(solution)/shard_map/ppermute | solution.py:343
  49.4 0.0 collective-permute-done.5.third
  49.4 2.9 %collective-permute-start.6 = (bf16[128,1024]{1,0:T(8,128)(2,1)S(1)}, bf16[128,1024]{1,0:T(8,128)(2,1)S(1)}, u32[]{:S(2)}, u32[]{:S(2)}) collective-permute-start(bf16[128,1024]{1,0:T(8,128)(2,1)S(1)} %collective-permute-done.5.third), channel_id=1, source_target_pairs={{0,1},{1,0},{2,3},{3,2},{4,5},{5,4},{6,7},{7,6},{8,9},{9,8},{10,11... | collective-permute-start | bytes 786440 | tf_op jit(solution)/shard_map/ppermute | solution.py:343
  52.3 1.9 %collective-permute-start.7 = (bf16[72,1024]{1,0:T(8,128)(2,1)S(1)}, bf16[72,1024]{1,0:T(8,128)(2,1)S(1)}, u32[]{:S(2)}, u32[]{:S(2)}) collective-permute-start(bf16[72,1024]{1,0:T(8,128)(2,1)S(1)} %get-tuple-element.20.first), channel_id=1, source_target_pairs={{0,1},{1,0},{2,3},{3,2},{4,5},{5,4},{6,7},{7,6},{8,9},{9,8},{10,11... | collective-permute-start | bytes 442376 | tf_op jit(solution)/shard_map/ppermute | solution.py:343
  54.3 0.0 collective-permute-done.8.third
  54.3 2.4 %collective-permute-start.9 = (bf16[72,1024]{1,0:T(8,128)(2,1)S(1)}, bf16[72,1024]{1,0:T(8,128)(2,1)S(1)}, u32[]{:S(2)}, u32[]{:S(2)}) collective-permute-start(bf16[72,1024]{1,0:T(8,128)(2,1)S(1)} %collective-permute-done.8.third), channel_id=1, source_target_pairs={{0,1},{1,0},{2,3},{3,2},{4,5},{5,4},{6,7},{7,6},{8,9},{9,8},{10,11... | collective-permute-start | bytes 442376 | tf_op jit(solution)/shard_map/ppermute | solution.py:343
  56.7 0.0 collective-permute-done.7.second
  56.7 1.0 collective-permute-done.9.fourth
  57.7 0.0 copy-done
  57.7 1.2 %shard_map.106 = (f32[1024,256]{1,0:T(8,128)S(1)}, f32[64,1024]{1,0:T(8,128)S(1)}, bf16[256,1024]{1,0:T(8,128)(2,1)S(1)}, f32[8,1024]{1,0:T(8,128)S(1)}) custom-call(bf16[72,1024]{1,0:T(8,128)(2,1)S(1)} %get-tuple-element.20.first, bf16[72,1024]{1,0:T(8,128)(2,1)S(1)} %collective-permute-done.7.second, bf16[72,1024]{1,0:T(8,128)(2,1)S(1)} %collective-permute-done.8.third, ...), custom_call_target="tpu_custom_call" | custom-call | tf_op jit(solution)/shard_map/pallas_call | solution.py:318
  58.9 0.0 collective-permute-done.4.second
  58.9 0.0 collective-permute-done.6.fourth
  58.9 2.4 %shard_map.107 = (bf16[256,1024]{1,0:T(8,128)(2,1)S(1)}, bf16[256,1024]{1,0:T(8,128)(2,1)S(1)}, bf16[256,1024]{1,0:T(8,128)(2,1)S(1)}, f32[64,1024]{1,0:T(8,128)S(1)}, f32[64,1024]{1,0:T(8,128)S(1)}) custom-call(bf16[128,1024]{1,0:T(8,128)(2,1)S(1)} %shard_map.105.first, bf16[128,1024]{1,0:T(8,128)(2,1)S(1)} %collective-permute-done.4.second, ...), custom_call_target="tpu_custom_call" | custom-call | tf_op jit(solution)/shard_map/pallas_call | solution.py:318
  61.3 0.0 copy-done.1
  61.3 1.1 %shard_map.108 = (f32[128,256]{1,0:T(8,128)}, bf16[128,1024]{1,0:T(8,128)(2,1)S(1)}, f32[64,128]{1,0:T(8,128)S(1)}) custom-call(bf16[256,1024]{1,0:T(8,128)(2,1)S(1)} %get-tuple-element.22.prop_hid, bf16[256,128]{1,0:T(8,128)(2,1)S(1)} %copy-done.1, f32[8,1024]{1,0:T(8,128)S(1)} %get-tuple-element.23.labels), custom_call_target="tpu_custom_call" | custom-call | tf_op jit(solution)/shard_map/pallas_call | solution.py:318
  62.5 2.2 %shard_map.109 = f32[8,8,384]{2,1,0:T(8,128)S(1)} custom-call(bf16[128,1024]{1,0:T(8,128)(2,1)S(1)} %get-tuple-element.25.dl, bf16[1152,2304]{1,0:T(8,128)(2,1)S(1)} %assemble.1.dense, bf16[256,128]{1,0:T(8,128)(2,1)S(1)} %copy-done.1, f32[64,1024]{1,0:T(8,128)S(1)} %get-tuple-element.26.pre_own, f32[64,1024]{1,0:T(8,128)S(1)} %get-tuple-element.27.pre_near, ...), custom_call_target="tpu_custom_call" | custom-call | tf_op jit(solution)/shard_map/pallas_call | solution.py:318
  64.7 9.2 %all_to_all.15.parts = f32[8,8,384]{2,1,0:T(8,128)S(1)} all-to-all(f32[8,8,384]{2,1,0:T(8,128)S(1)} %shard_map.109), channel_id=1, replica_groups=mesh['yh'=2,'z'=16,'x'=4,'yl'=2,'co'=2] {'yh','x'}, dimensions={0} | all-to-all | bytes 196608 | tf_op jit(solution)/shard_map/all_to_all | solution.py:420
  73.9 16.2 %all_to_all.16.parts = f32[16,8,384]{2,1,0:T(8,128)S(1)} all-to-all(f32[16,8,384]{2,1,0:T(8,128)S(1)} %shard_map.110), channel_id=1, replica_groups=mesh['yh'=2,'z'=16,'x'=4,'yl'=2,'co'=2] {'z'}, dimensions={0} | all-to-all | bytes 393216 | tf_op jit(solution)/shard_map/all_to_all | solution.py:422
  90.2 18.5 %all_to_all.17.parts = f32[32,8,384]{2,1,0:T(8,128)S(1)} all-to-all(f32[32,8,384]{2,1,0:T(8,128)S(1)} %shard_map.111), channel_id=1, replica_groups=mesh['yh'=2,'z'=16,'x'=4,'yl'=2,'co'=2] {'yh','x','yl','co'}, dimensions={0} | all-to-all | bytes 786432 | tf_op jit(solution)/shard_map/all_to_all | solution.py:424
  108.7 0.8 shard_map.112
  (3 shorter events, 0.1 us)
Async XLA Ops:
  0.6 23.3 %copy-start.2 = (bf16[64,1024]{1,0:T(8,128)(2,1)S(1)}, bf16[64,1024]{1,0:T(8,128)(2,1)}, u32[]{:S(2)}) copy-start(bf16[64,1024]{1,0:T(8,128)(2,1)} %own.1) | copy-start | bytes 393220
  0.6 23.3 %collective-permute-start.1 = (bf16[64,1024]{1,0:T(8,128)(2,1)}, bf16[64,1024]{1,0:T(8,128)(2,1)S(1)}, u32[]{:S(2)}, u32[]{:S(2)}) collective-permute-start(bf16[64,1024]{1,0:T(8,128)(2,1)} %own.1), channel_id=1, source_target_pairs={{0,4},{4,0},{8,12},{12,8},{16,20},{20,16},{24,28},{28,24},{32,36},... | collective-permute-start | bytes 393224 | tf_op jit(solution)/shard_map/ppermute | solution.py:332
  4.7 20.3 %collective-permute-start = (bf16[64,1024]{1,0:T(8,128)(2,1)}, bf16[64,1024]{1,0:T(8,128)(2,1)S(1)}, u32[]{:S(2)}, u32[]{:S(2)}) collective-permute-start(bf16[64,1024]{1,0:T(8,128)(2,1)} %own.1), channel_id=1, source_target_pairs={{0,508},{4,8},{8,4},{12,16},{16,12},{20,24},{24,20},{28,32},{32,28... | collective-permute-start | bytes 393224 | tf_op jit(solution)/shard_map/ppermute | solution.py:331
  23.9 1.1 copy-start.3
  23.9 33.8 %copy-start = (bf16[256,256]{1,0:T(8,128)(2,1)S(1)}, bf16[256,256]{1,0:T(8,128)(2,1)}, u32[]{:S(2)}) copy-start(bf16[256,256]{1,0:T(8,128)(2,1)} %w_in.3) | copy-start | bytes 393220
  25.6 11.4 %collective-permute-start.3 = (bf16[64,1024]{1,0:T(8,128)(2,1)S(1)}, bf16[64,1024]{1,0:T(8,128)(2,1)S(1)}, u32[]{:S(2)}, u32[]{:S(2)}) collective-permute-start(bf16[64,1024]{1,0:T(8,128)(2,1)S(1)} %get-tuple-element.19), channel_id=1, source_target_pairs={{0,508},{4,8},{8,4},{12,16},{16,12},{20,24},{24,20},{28,32},{32,28... | collective-permute-start | bytes 393224 | tf_op jit(solution)/shard_map/ppermute | solution.py:331
  32.2 6.0 %collective-permute-start.2 = (bf16[64,1024]{1,0:T(8,128)(2,1)S(1)}, bf16[64,1024]{1,0:T(8,128)(2,1)S(1)}, u32[]{:S(2)}, u32[]{:S(2)}) collective-permute-start(bf16[64,1024]{1,0:T(8,128)(2,1)S(1)} %get-tuple-element.19), channel_id=1, source_target_pairs={{0,4},{4,0},{8,12},{12,8},{16,20},{20,16},{24,28},{28,24},{32,36},... | collective-permute-start | bytes 393224 | tf_op jit(solution)/shard_map/ppermute | solution.py:332
  38.2 11.2 %collective-permute-start.5 = (bf16[128,1024]{1,0:T(8,128)(2,1)S(1)}, bf16[128,1024]{1,0:T(8,128)(2,1)S(1)}, u32[]{:S(2)}, u32[]{:S(2)}) collective-permute-start(bf16[128,1024]{1,0:T(8,128)(2,1)S(1)} %shard_map.105.first), channel_id=1, source_target_pairs={{0,2},{1,3},{2,0},{3,1},{4,6},{5,7},{6,4},{7,5},{8,10},{9,11},{10,... | collective-permute-start | bytes 786440 | tf_op jit(solution)/shard_map/ppermute | solution.py:343
  40.5 20.8 %copy-start.1 = (bf16[256,128]{1,0:T(8,128)(2,1)S(1)}, bf16[256,128]{1,0:T(8,128)(2,1)}, u32[]{:S(2)}) copy-start(bf16[256,128]{1,0:T(8,128)(2,1)} %w_out.3) | copy-start | bytes 196612
  40.6 13.7 %collective-permute-start.8 = (bf16[72,1024]{1,0:T(8,128)(2,1)S(1)}, bf16[72,1024]{1,0:T(8,128)(2,1)S(1)}, u32[]{:S(2)}, u32[]{:S(2)}) collective-permute-start(bf16[72,1024]{1,0:T(8,128)(2,1)S(1)} %get-tuple-element.20.first), channel_id=1, source_target_pairs={{0,2},{1,3},{2,0},{3,1},{4,6},{5,7},{6,4},{7,5},{8,10},{9,11},{10,... | collective-permute-start | bytes 442376 | tf_op jit(solution)/shard_map/ppermute | solution.py:343
  43.7 15.3 %collective-permute-start.4 = (bf16[128,1024]{1,0:T(8,128)(2,1)S(1)}, bf16[128,1024]{1,0:T(8,128)(2,1)S(1)}, u32[]{:S(2)}, u32[]{:S(2)}) collective-permute-start(bf16[128,1024]{1,0:T(8,128)(2,1)S(1)} %shard_map.105.first), channel_id=1, source_target_pairs={{0,1},{1,0},{2,3},{3,2},{4,5},{5,4},{6,7},{7,6},{8,9},{9,8},{10,11... | collective-permute-start | bytes 786440 | tf_op jit(solution)/shard_map/ppermute | solution.py:343
  49.4 9.5 %collective-permute-start.6 = (bf16[128,1024]{1,0:T(8,128)(2,1)S(1)}, bf16[128,1024]{1,0:T(8,128)(2,1)S(1)}, u32[]{:S(2)}, u32[]{:S(2)}) collective-permute-start(bf16[128,1024]{1,0:T(8,128)(2,1)S(1)} %collective-permute-done.5.third), channel_id=1, source_target_pairs={{0,1},{1,0},{2,3},{3,2},{4,5},{5,4},{6,7},{7,6},{8,9},{9,8},{10,11... | collective-permute-start | bytes 786440 | tf_op jit(solution)/shard_map/ppermute | solution.py:343
  52.3 4.4 %collective-permute-start.7 = (bf16[72,1024]{1,0:T(8,128)(2,1)S(1)}, bf16[72,1024]{1,0:T(8,128)(2,1)S(1)}, u32[]{:S(2)}, u32[]{:S(2)}) collective-permute-start(bf16[72,1024]{1,0:T(8,128)(2,1)S(1)} %get-tuple-element.20.first), channel_id=1, source_target_pairs={{0,1},{1,0},{2,3},{3,2},{4,5},{5,4},{6,7},{7,6},{8,9},{9,8},{10,11... | collective-permute-start | bytes 442376 | tf_op jit(solution)/shard_map/ppermute | solution.py:343
  54.3 3.4 %collective-permute-start.9 = (bf16[72,1024]{1,0:T(8,128)(2,1)S(1)}, bf16[72,1024]{1,0:T(8,128)(2,1)S(1)}, u32[]{:S(2)}, u32[]{:S(2)}) collective-permute-start(bf16[72,1024]{1,0:T(8,128)(2,1)S(1)} %collective-permute-done.8.third), channel_id=1, source_target_pairs={{0,1},{1,0},{2,3},{3,2},{4,5},{5,4},{6,7},{7,6},{8,9},{9,8},{10,11... | collective-permute-start | bytes 442376 | tf_op jit(solution)/shard_map/ppermute | solution.py:343

commit v6 on v5

--- a/solution.py
+++ b/solution.py
@@ -292,6 +292,21 @@
         out[p, :, width:] = share_out[p * rows : (p + 1) * rows]
 
 
+def tail_kernel(
+    scale, first, second, third, fourth, w_in, acc, dense, w_out, labels, pre_own, own_in,
+    logits, out,
+    prop_hid, near_in, far_in, pre_near, pre_far, hidden, whole_pre, total, dl, share, scores, terms,
+):
+    prop_hidden_kernel(
+        first, second, third, fourth, w_in, acc, dense,
+        prop_hid, near_in, far_in, pre_near, pre_far, hidden, whole_pre, total,
+    )
+    logits_kernel(scale, prop_hid, w_out, labels, logits, dl, share, scores)
+    grads_kernel(
+        dl, dense, w_out, pre_own, pre_near, pre_far, own_in, near_in, far_in, share, out, terms
+    )
+
+
 def sum_kernel(parts, out):
     total = parts[0]
     for p in range(1, parts.shape[0]):
@@ -379,43 +394,29 @@
         (sds((stripe, hid), F32), pre, whole_in, sds((TAG, stripe), F32)),
         scratch=[hidden, whole_pre],
     )
-    prop_hid, near_in, far_in, pre_near, pre_far = call(
-        prop_hidden_kernel,
-        (both, both_second, both_third, both_fourth, weight_in, acc, dense),
-        (sds((hid, stripe), BF16), whole_in, whole_in, pre, pre),
-        scratch=[hidden, whole_pre, pltpu.VMEM((stripe, hid), F32)],
-        mib=24,
-    )
-    logits, dl, share_out = call(
-        functools.partial(logits_kernel, node_scale),
-        (prop_hid, weight_out, label_rows),
-        (
-            sds((classes, mine), F32),
-            sds((classes, stripe), BF16),
-            sds((hid // 4, classes), F32),
-        ),
-        scratch=[pltpu.VMEM((classes, stripe), F32)],
-    )
-
     plane = lax.axis_size(PLANE)
     rows = hid // 4 // plane
     width = 4 * depth + classes
-    share = call(
-        grads_kernel,
-        (
-            dl,
-            dense,
-            weight_out,
-            pre_own,
-            pre_near,
-            pre_far,
-            prop_in,
-            near_in,
-            far_in,
-            share_out,
-        ),
-        sds((plane, rows, width), F32),
-        scratch=[pltpu.VMEM((3 * hid // 4, stripe), BF16)],
+    tail_inputs = (both, both_second, both_third, both_fourth, weight_in, acc, dense)
+    logits, share = call(
+        functools.partial(tail_kernel, node_scale),
+        (*tail_inputs, weight_out, label_rows, pre_own, prop_in),
+        (sds((classes, mine), F32), sds((plane, rows, width), F32)),
+        mib=32,
+        scratch=[
+            pltpu.VMEM((hid, stripe), BF16),
+            pltpu.VMEM(whole_in.shape, BF16),
+            pltpu.VMEM(whole_in.shape, BF16),
+            pltpu.VMEM(pre.shape, F32),
+            pltpu.VMEM(pre.shape, F32),
+            hidden,
+            whole_pre,
+            pltpu.VMEM((stripe, hid), F32),
+            pltpu.VMEM((classes, stripe), BF16),
+            pltpu.VMEM((hid // 4, classes), F32),
+            pltpu.VMEM((classes, stripe), F32),
+            pltpu.VMEM((3 * hid // 4, stripe), BF16),
+        ],
     )
     parts = lax.all_to_all(share, PLANE, 0, 0, tiled=True)
     parts = call(sum_kernel, (parts,), sds((lax.axis_size("z"), rows, width), F32))

time: 110 us -> 111 us (level)
    ppermute x2, waiting for transfers between devices: 2.88 us -> 4.8 us  [halo(): far = lax.ppermute(value, BLK, far)]
    ppermute x2, waiting for transfers between devices: 1.2 us -> 0.01 us  [halo(): near = lax.ppermute(value, BLK, [(i, i ^ 1) for i in range(count)])]
    pallas_call x10 -> x8, Pallas kernels: 9.48 us -> 8.83 us  [call(): pl.pallas_call(kernel, in_specs=[whole()] * len(args), out_specs=[whole()...]
  transfers between devices with their start and end apart: 10 -> 10, of which waited for: 3 -> 2; matrix products, arithmetic and copies ran while one was open for 0% -> 0% of each run, Pallas kernels for 5% -> 5%
where the time goes in v6:
time: 111 us
  starting transfers between devices  46.3 us (42%)
  blocking collectives  44.9 us (40%)
  Pallas kernels  12.1 us (11%)
  waiting for transfers between devices  5.79 us (5%)
  between operations  1.52 us (1%)
    ppermute x2, starting transfers between devices, halo(): far = lax.ppermute(value, BLK, far)  21.9 us
    all_to_all x1, blocking collectives, on_device(): parts = lax.all_to_all(parts, PLANE + FEAT, 0, 0, tiled=True)  18.5 us
    ppermute x6, starting transfers between devices, flipped(): return lax.ppermute(value, FEAT, [(i, i ^ shift) for i in range(4)])  18.4 us
    all_to_all x1, blocking collectives, on_device(): parts = lax.all_to_all(parts, 'z', 0, 0, tiled=True)  17.3 us
    all_to_all x1, blocking collectives, on_device(): parts = lax.all_to_all(share, PLANE, 0, 0, tiled=True)  9.16 us
    pallas_call x8, Pallas kernels, call(): pl.pallas_call(kernel, in_specs=[whole()] * len(args), out_specs=[whole()...  8.83 us
    ppermute x2, starting transfers between devices, halo(): near = lax.ppermute(value, BLK, [(i, i ^ 1) for i in range(count)])  5.99 us
    ppermute x2, waiting for transfers between devices, halo(): far = lax.ppermute(value, BLK, far)  4.8 us
  transfers between devices with their start and end apart: 10, of which 2 were waited for; matrix products, arithmetic and copies ran while one was open for 0% of the time, Pallas kernels for 5%

profile of v6, /device:TPU:1, one launch (start us, length us, event | category | flops | bytes accessed | tf_op | source)
XLA Modules:
  0.0 110.6 jit_solution(12336976724261390248)
XLA Ops:
  0.6 0.0 copy-start.1
  0.6 4.1 %collective-permute-start.1 = (bf16[64,1024]{1,0:T(8,128)(2,1)}, bf16[64,1024]{1,0:T(8,128)(2,1)S(1)}, u32[]{:S(2)}, u32[]{:S(2)}) collective-permute-start(bf16[64,1024]{1,0:T(8,128)(2,1)} %own.1), channel_id=1, source_target_pairs={{0,4},{4,0},{8,12},{12,8},{16,20},{20,16},{24,28},{28,24},{32,36},... | collective-permute-start | bytes 393224 | tf_op jit(solution)/shard_map/ppermute | solution.py:347
  4.7 15.3 %collective-permute-start = (bf16[64,1024]{1,0:T(8,128)(2,1)}, bf16[64,1024]{1,0:T(8,128)(2,1)S(1)}, u32[]{:S(2)}, u32[]{:S(2)}) collective-permute-start(bf16[64,1024]{1,0:T(8,128)(2,1)} %own.1), channel_id=1, source_target_pairs={{0,508},{4,8},{8,4},{12,16},{16,12},{20,24},{24,20},{28,32},{32,28... | collective-permute-start | bytes 393224 | tf_op jit(solution)/shard_map/ppermute | solution.py:346
  20.7 3.2 %assemble.1.dense = bf16[1152,2304]{1,0:T(8,128)(2,1)S(1)} custom-call(s32[136]{0:T(256)} %rows_ref.1, s32[136]{0:T(256)} %cols_ref.1, s32[1]{0:T(128)S(6)} %copy.11.count_ref, bf16[136,128,128]{2,1,0:T(8,128)(2,1)} %blocks_hbm.1), custom_call_target="tpu_custom_call" | custom-call | tf_op jit(solution)/shard_map/assemble/pallas_call | solution.py:83
  23.9 0.0 copy-start.3
  23.9 0.0 copy-start
  23.9 0.0 collective-permute-done.1.piece
  23.9 0.0 copy-done.1
  23.9 1.0 shard_map.103.acc
  25.0 0.0 collective-permute-done.far
  25.0 0.0 copy-done.3
  25.0 0.0 copy-start.2
  25.0 0.6 shard_map.104
  25.6 1.9 %collective-permute-start.2 = (bf16[64,1024]{1,0:T(8,128)(2,1)S(1)}, bf16[64,1024]{1,0:T(8,128)(2,1)S(1)}, u32[]{:S(2)}, u32[]{:S(2)}) collective-permute-start(bf16[64,1024]{1,0:T(8,128)(2,1)S(1)} %get-tuple-element.13), channel_id=1, source_target_pairs={{0,4},{4,0},{8,12},{12,8},{16,20},{20,16},{24,28},{28,24},{32,36},... | collective-permute-start | bytes 393224 | tf_op jit(solution)/shard_map/ppermute | solution.py:347
  27.5 6.6 %collective-permute-start.3 = (bf16[64,1024]{1,0:T(8,128)(2,1)S(1)}, bf16[64,1024]{1,0:T(8,128)(2,1)S(1)}, u32[]{:S(2)}, u32[]{:S(2)}) collective-permute-start(bf16[64,1024]{1,0:T(8,128)(2,1)S(1)} %get-tuple-element.13), channel_id=1, source_target_pairs={{0,508},{4,8},{8,4},{12,16},{16,12},{20,24},{24,20},{28,32},{32,28... | collective-permute-start | bytes 393224 | tf_op jit(solution)/shard_map/ppermute | solution.py:346
  34.1 0.0 collective-permute-done.2.near
  34.2 4.8 %collective-permute-done.3.far = bf16[64,1024]{1,0:T(8,128)(2,1)S(1)} collective-permute-done((bf16[64,1024]{1,0:T(8,128)(2,1)S(1)}, bf16[64,1024]{1,0:T(8,128)(2,1)S(1)}, u32[]{:S(2)}, u32[]{:S(2)}) %collective-permute-start.3) | collective-permute-done | bytes 131104 | tf_op jit(solution)/shard_map/ppermute | solution.py:346
  39.0 2.3 %collective-permute-start.5 = (bf16[128,1024]{1,0:T(8,128)(2,1)S(1)}, bf16[128,1024]{1,0:T(8,128)(2,1)S(1)}, u32[]{:S(2)}, u32[]{:S(2)}) collective-permute-start(bf16[128,1024]{1,0:T(8,128)(2,1)S(1)} %shard_map.105.first), channel_id=1, source_target_pairs={{0,2},{1,3},{2,0},{3,1},{4,6},{5,7},{6,4},{7,5},{8,10},{9,11},{10,... | collective-permute-start | bytes 786440 | tf_op jit(solution)/shard_map/ppermute | solution.py:358
  41.3 3.0 %collective-permute-start.8 = (bf16[72,1024]{1,0:T(8,128)(2,1)S(1)}, bf16[72,1024]{1,0:T(8,128)(2,1)S(1)}, u32[]{:S(2)}, u32[]{:S(2)}) collective-permute-start(bf16[72,1024]{1,0:T(8,128)(2,1)S(1)} %get-tuple-element.14.first), channel_id=1, source_target_pairs={{0,2},{1,3},{2,0},{3,1},{4,6},{5,7},{6,4},{7,5},{8,10},{9,11},{10,... | collective-permute-start | bytes 442376 | tf_op jit(solution)/shard_map/ppermute | solution.py:358
  44.3 4.8 %collective-permute-start.4 = (bf16[128,1024]{1,0:T(8,128)(2,1)S(1)}, bf16[128,1024]{1,0:T(8,128)(2,1)S(1)}, u32[]{:S(2)}, u32[]{:S(2)}) collective-permute-start(bf16[128,1024]{1,0:T(8,128)(2,1)S(1)} %shard_map.105.first), channel_id=1, source_target_pairs={{0,1},{1,0},{2,3},{3,2},{4,5},{5,4},{6,7},{7,6},{8,9},{9,8},{10,11... | collective-permute-start | bytes 786440 | tf_op jit(solution)/shard_map/ppermute | solution.py:358
  49.1 0.0 collective-permute-done.5.third
  49.1 3.9 %collective-permute-start.6 = (bf16[128,1024]{1,0:T(8,128)(2,1)S(1)}, bf16[128,1024]{1,0:T(8,128)(2,1)S(1)}, u32[]{:S(2)}, u32[]{:S(2)}) collective-permute-start(bf16[128,1024]{1,0:T(8,128)(2,1)S(1)} %collective-permute-done.5.third), channel_id=1, source_target_pairs={{0,1},{1,0},{2,3},{3,2},{4,5},{5,4},{6,7},{7,6},{8,9},{9,8},{10,11... | collective-permute-start | bytes 786440 | tf_op jit(solution)/shard_map/ppermute | solution.py:358
  53.1 1.9 %collective-permute-start.7 = (bf16[72,1024]{1,0:T(8,128)(2,1)S(1)}, bf16[72,1024]{1,0:T(8,128)(2,1)S(1)}, u32[]{:S(2)}, u32[]{:S(2)}) collective-permute-start(bf16[72,1024]{1,0:T(8,128)(2,1)S(1)} %get-tuple-element.14.first), channel_id=1, source_target_pairs={{0,1},{1,0},{2,3},{3,2},{4,5},{5,4},{6,7},{7,6},{8,9},{9,8},{10,11... | collective-permute-start | bytes 442376 | tf_op jit(solution)/shard_map/ppermute | solution.py:358
  55.0 0.0 collective-permute-done.8.third
  55.0 2.4 %collective-permute-start.9 = (bf16[72,1024]{1,0:T(8,128)(2,1)S(1)}, bf16[72,1024]{1,0:T(8,128)(2,1)S(1)}, u32[]{:S(2)}, u32[]{:S(2)}) collective-permute-start(bf16[72,1024]{1,0:T(8,128)(2,1)S(1)} %collective-permute-done.8.third), channel_id=1, source_target_pairs={{0,1},{1,0},{2,3},{3,2},{4,5},{5,4},{6,7},{7,6},{8,9},{9,8},{10,11... | collective-permute-start | bytes 442376 | tf_op jit(solution)/shard_map/ppermute | solution.py:358
  57.4 0.0 collective-permute-done.7.second
  57.4 1.0 collective-permute-done.9.fourth
  58.4 0.0 copy-done
  58.4 1.2 %shard_map.106 = (f32[1024,256]{1,0:T(8,128)S(1)}, f32[64,1024]{1,0:T(8,128)S(1)}, bf16[256,1024]{1,0:T(8,128)(2,1)S(1)}, f32[8,1024]{1,0:T(8,128)S(1)}) custom-call(bf16[72,1024]{1,0:T(8,128)(2,1)S(1)} %get-tuple-element.14.first, bf16[72,1024]{1,0:T(8,128)(2,1)S(1)} %collective-permute-done.7.second, bf16[72,1024]{1,0:T(8,128)(2,1)S(1)} %collective-permute-done.8.third, ...), custom_call_target="tpu_custom_call" | custom-call | tf_op jit(solution)/shard_map/pallas_call | solution.py:333
  59.7 0.0 collective-permute-done.4.second
  59.7 0.0 collective-permute-done.6.fourth
  59.7 0.0 copy-done.2
  59.7 5.1 %shard_map.107 = (f32[128,256]{1,0:T(8,128)}, f32[8,8,384]{2,1,0:T(8,128)S(1)}) custom-call(bf16[128,1024]{1,0:T(8,128)(2,1)S(1)} %shard_map.105.first, bf16[128,1024]{1,0:T(8,128)(2,1)S(1)} %collective-permute-done.4.second, bf16[128,1024]{1,0:T(8,128)(2,1)S(1)} %collective-permute-done.5.third, bf16[128,1024]{1,0:T(8,128)(2,1)S(1)} %collective-permute-done.6.fourth, ...), custom_call_target="tpu_custom_call" | custom-call | tf_op jit(solution)/shard_map/pallas_call | solution.py:333
  64.8 9.2 %all_to_all.15.parts = f32[8,8,384]{2,1,0:T(8,128)S(1)} all-to-all(f32[8,8,384]{2,1,0:T(8,128)S(1)} %get-tuple-element.20), channel_id=1, replica_groups=mesh['yh'=2,'z'=16,'x'=4,'yl'=2,'co'=2] {'yh','x'}, dimensions={0} | all-to-all | bytes 196608 | tf_op jit(solution)/shard_map/all_to_all | solution.py:421
  74.0 17.3 %all_to_all.16.parts = f32[16,8,384]{2,1,0:T(8,128)S(1)} all-to-all(f32[16,8,384]{2,1,0:T(8,128)S(1)} %shard_map.108), channel_id=1, replica_groups=mesh['yh'=2,'z'=16,'x'=4,'yl'=2,'co'=2] {'z'}, dimensions={0} | all-to-all | bytes 393216 | tf_op jit(solution)/shard_map/all_to_all | solution.py:423
  91.3 18.5 %all_to_all.17.parts = f32[32,8,384]{2,1,0:T(8,128)S(1)} all-to-all(f32[32,8,384]{2,1,0:T(8,128)S(1)} %shard_map.109), channel_id=1, replica_groups=mesh['yh'=2,'z'=16,'x'=4,'yl'=2,'co'=2] {'yh','x','yl','co'}, dimensions={0} | all-to-all | bytes 786432 | tf_op jit(solution)/shard_map/all_to_all | solution.py:425
  109.8 0.8 shard_map.110
  (3 shorter events, 0.1 us)
Async XLA Ops:
  0.6 23.3 %copy-start.1 = (bf16[64,1024]{1,0:T(8,128)(2,1)S(1)}, bf16[64,1024]{1,0:T(8,128)(2,1)}, u32[]{:S(2)}) copy-start(bf16[64,1024]{1,0:T(8,128)(2,1)} %own.1) | copy-start | bytes 393220
  0.6 23.3 %collective-permute-start.1 = (bf16[64,1024]{1,0:T(8,128)(2,1)}, bf16[64,1024]{1,0:T(8,128)(2,1)S(1)}, u32[]{:S(2)}, u32[]{:S(2)}) collective-permute-start(bf16[64,1024]{1,0:T(8,128)(2,1)} %own.1), channel_id=1, source_target_pairs={{0,4},{4,0},{8,12},{12,8},{16,20},{20,16},{24,28},{28,24},{32,36},... | collective-permute-start | bytes 393224 | tf_op jit(solution)/shard_map/ppermute | solution.py:347
  4.7 20.3 %collective-permute-start = (bf16[64,1024]{1,0:T(8,128)(2,1)}, bf16[64,1024]{1,0:T(8,128)(2,1)S(1)}, u32[]{:S(2)}, u32[]{:S(2)}) collective-permute-start(bf16[64,1024]{1,0:T(8,128)(2,1)} %own.1), channel_id=1, source_target_pairs={{0,508},{4,8},{8,4},{12,16},{16,12},{20,24},{24,20},{28,32},{32,28... | collective-permute-start | bytes 393224 | tf_op jit(solution)/shard_map/ppermute | solution.py:346
  23.9 1.1 copy-start.3
  23.9 34.5 %copy-start = (bf16[256,256]{1,0:T(8,128)(2,1)S(1)}, bf16[256,256]{1,0:T(8,128)(2,1)}, u32[]{:S(2)}) copy-start(bf16[256,256]{1,0:T(8,128)(2,1)} %w_in.3) | copy-start | bytes 393220
  25.0 34.7 %copy-start.2 = (bf16[256,128]{1,0:T(8,128)(2,1)S(1)}, bf16[256,128]{1,0:T(8,128)(2,1)}, u32[]{:S(2)}) copy-start(bf16[256,128]{1,0:T(8,128)(2,1)} %w_out.1) | copy-start | bytes 196612
  25.6 8.6 %collective-permute-start.2 = (bf16[64,1024]{1,0:T(8,128)(2,1)S(1)}, bf16[64,1024]{1,0:T(8,128)(2,1)S(1)}, u32[]{:S(2)}, u32[]{:S(2)}) collective-permute-start(bf16[64,1024]{1,0:T(8,128)(2,1)S(1)} %get-tuple-element.13), channel_id=1, source_target_pairs={{0,4},{4,0},{8,12},{12,8},{16,20},{20,16},{24,28},{28,24},{32,36},... | collective-permute-start | bytes 393224 | tf_op jit(solution)/shard_map/ppermute | solution.py:347
  27.5 11.4 %collective-permute-start.3 = (bf16[64,1024]{1,0:T(8,128)(2,1)S(1)}, bf16[64,1024]{1,0:T(8,128)(2,1)S(1)}, u32[]{:S(2)}, u32[]{:S(2)}) collective-permute-start(bf16[64,1024]{1,0:T(8,128)(2,1)S(1)} %get-tuple-element.13), channel_id=1, source_target_pairs={{0,508},{4,8},{8,4},{12,16},{16,12},{20,24},{24,20},{28,32},{32,28... | collective-permute-start | bytes 393224 | tf_op jit(solution)/shard_map/ppermute | solution.py:346
  39.0 10.2 %collective-permute-start.5 = (bf16[128,1024]{1,0:T(8,128)(2,1)S(1)}, bf16[128,1024]{1,0:T(8,128)(2,1)S(1)}, u32[]{:S(2)}, u32[]{:S(2)}) collective-permute-start(bf16[128,1024]{1,0:T(8,128)(2,1)S(1)} %shard_map.105.first), channel_id=1, source_target_pairs={{0,2},{1,3},{2,0},{3,1},{4,6},{5,7},{6,4},{7,5},{8,10},{9,11},{10,... | collective-permute-start | bytes 786440 | tf_op jit(solution)/shard_map/ppermute | solution.py:358
  41.3 13.7 %collective-permute-start.8 = (bf16[72,1024]{1,0:T(8,128)(2,1)S(1)}, bf16[72,1024]{1,0:T(8,128)(2,1)S(1)}, u32[]{:S(2)}, u32[]{:S(2)}) collective-permute-start(bf16[72,1024]{1,0:T(8,128)(2,1)S(1)} %get-tuple-element.14.first), channel_id=1, source_target_pairs={{0,2},{1,3},{2,0},{3,1},{4,6},{5,7},{6,4},{7,5},{8,10},{9,11},{10,... | collective-permute-start | bytes 442376 | tf_op jit(solution)/shard_map/ppermute | solution.py:358
  44.3 15.4 %collective-permute-start.4 = (bf16[128,1024]{1,0:T(8,128)(2,1)S(1)}, bf16[128,1024]{1,0:T(8,128)(2,1)S(1)}, u32[]{:S(2)}, u32[]{:S(2)}) collective-permute-start(bf16[128,1024]{1,0:T(8,128)(2,1)S(1)} %shard_map.105.first), channel_id=1, source_target_pairs={{0,1},{1,0},{2,3},{3,2},{4,5},{5,4},{6,7},{7,6},{8,9},{9,8},{10,11... | collective-permute-start | bytes 786440 | tf_op jit(solution)/shard_map/ppermute | solution.py:358
  49.1 10.5 %collective-permute-start.6 = (bf16[128,1024]{1,0:T(8,128)(2,1)S(1)}, bf16[128,1024]{1,0:T(8,128)(2,1)S(1)}, u32[]{:S(2)}, u32[]{:S(2)}) collective-permute-start(bf16[128,1024]{1,0:T(8,128)(2,1)S(1)} %collective-permute-done.5.third), channel_id=1, source_target_pairs={{0,1},{1,0},{2,3},{3,2},{4,5},{5,4},{6,7},{7,6},{8,9},{9,8},{10,11... | collective-permute-start | bytes 786440 | tf_op jit(solution)/shard_map/ppermute | solution.py:358
  53.1 4.4 %collective-permute-start.7 = (bf16[72,1024]{1,0:T(8,128)(2,1)S(1)}, bf16[72,1024]{1,0:T(8,128)(2,1)S(1)}, u32[]{:S(2)}, u32[]{:S(2)}) collective-permute-start(bf16[72,1024]{1,0:T(8,128)(2,1)S(1)} %get-tuple-element.14.first), channel_id=1, source_target_pairs={{0,1},{1,0},{2,3},{3,2},{4,5},{5,4},{6,7},{7,6},{8,9},{9,8},{10,11... | collective-permute-start | bytes 442376 | tf_op jit(solution)/shard_map/ppermute | solution.py:358
  55.0 3.4 %collective-permute-start.9 = (bf16[72,1024]{1,0:T(8,128)(2,1)S(1)}, bf16[72,1024]{1,0:T(8,128)(2,1)S(1)}, u32[]{:S(2)}, u32[]{:S(2)}) collective-permute-start(bf16[72,1024]{1,0:T(8,128)(2,1)S(1)} %collective-permute-done.8.third), channel_id=1, source_target_pairs={{0,1},{1,0},{2,3},{3,2},{4,5},{5,4},{6,7},{7,6},{8,9},{9,8},{10,11... | collective-permute-start | bytes 442376 | tf_op jit(solution)/shard_map/ppermute | solution.py:358

commit v7 on v6

--- a/solution.py
+++ b/solution.py
@@ -10,9 +10,9 @@
 from jax.sharding import PartitionSpec as P
 
 
-BLK = ("yh", "z", "x")
+BLK = ("yh", "zh", "zp", "x")
 FEAT = ("yl", "co")
-PLANE = ("yh", "x")
+PLANE = ("yh", "zp", "x")
 F32 = jnp.float32
 BF16 = jnp.bfloat16
 BS = 128
@@ -419,8 +419,8 @@
         ],
     )
     parts = lax.all_to_all(share, PLANE, 0, 0, tiled=True)
-    parts = call(sum_kernel, (parts,), sds((lax.axis_size("z"), rows, width), F32))
-    parts = lax.all_to_all(parts, "z", 0, 0, tiled=True)
+    parts = call(sum_kernel, (parts,), sds((lax.axis_size("zh"), rows, width), F32))
+    parts = lax.all_to_all(parts, "zh", 0, 0, tiled=True)
     parts = call(sum_kernel, (parts,), sds((plane * 4, rows, width), F32))
     parts = lax.all_to_all(parts, PLANE + FEAT, 0, 0, tiled=True)
     grad_in, grad_out = call(
@@ -433,7 +433,7 @@
 
 
 def solution(mesh):
-    fine = Mesh(mesh.devices.reshape(2, 16, 4, 2, 2), BLK + FEAT)
+    fine = Mesh(mesh.devices.reshape(2, 8, 2, 4, 2, 2), BLK + FEAT)
     placed = (
         P(FEAT, BLK),
         P(BLK, None, None),

time: 111 us -> 112 us (level)
    all_to_all x1, blocking collectives: 9.16 us -> 10.4 us  [on_device(): parts = lax.all_to_all(share, PLANE, 0, 0, tiled=True)]
where the time goes in v7:
time: 112 us; the launch traced here: 111 us
  starting transfers between devices  46.3 us (41%)
  blocking collectives  45.6 us (41%)
  Pallas kernels  12.1 us (11%)
  waiting for transfers between devices  5.79 us (5%)
  between operations  1.52 us (1%)
    ppermute x2, starting transfers between devices, halo(): far = lax.ppermute(value, BLK, far)  21.9 us
    ppermute x6, starting transfers between devices, flipped(): return lax.ppermute(value, FEAT, [(i, i ^ shift) for i in range(4)])  18.4 us
    all_to_all x1, blocking collectives, on_device(): parts = lax.all_to_all(parts, 'zh', 0, 0, tiled=True)  17.7 us
    all_to_all x1, blocking collectives, on_device(): parts = lax.all_to_all(parts, PLANE + FEAT, 0, 0, tiled=True)  17.5 us
    all_to_all x1, blocking collectives, on_device(): parts = lax.all_to_all(share, PLANE, 0, 0, tiled=True)  10.4 us
    pallas_call x8, Pallas kernels, call(): pl.pallas_call(kernel, in_specs=[whole()] * len(args), out_specs=[whole()...  8.86 us
    ppermute x2, starting transfers between devices, halo(): near = lax.ppermute(value, BLK, [(i, i ^ 1) for i in range(count)])  5.99 us
    ppermute x2, waiting for transfers between devices, halo(): far = lax.ppermute(value, BLK, far)  4.8 us
  transfers between devices with their start and end apart: 10, of which 2 were waited for; matrix products, arithmetic and copies ran while one was open for 0% of the time, Pallas kernels for 5%

profile of v7, /device:TPU:1, one launch (start us, length us, event | category | flops | bytes accessed | tf_op | source)
XLA Modules:
  0.0 111.3 jit_solution(12288699073056653644)
XLA Ops:
  0.6 0.0 copy-start.1
  0.6 4.1 %collective-permute-start.1 = (bf16[64,1024]{1,0:T(8,128)(2,1)}, bf16[64,1024]{1,0:T(8,128)(2,1)S(1)}, u32[]{:S(2)}, u32[]{:S(2)}) collective-permute-start(bf16[64,1024]{1,0:T(8,128)(2,1)} %own.1), channel_id=1, source_target_pairs={{0,4},{4,0},{8,12},{12,8},{16,20},{20,16},{24,28},{28,24},{32,36},... | collective-permute-start | bytes 393224 | tf_op jit(solution)/shard_map/ppermute | solution.py:347
  4.7 15.3 %collective-permute-start = (bf16[64,1024]{1,0:T(8,128)(2,1)}, bf16[64,1024]{1,0:T(8,128)(2,1)S(1)}, u32[]{:S(2)}, u32[]{:S(2)}) collective-permute-start(bf16[64,1024]{1,0:T(8,128)(2,1)} %own.1), channel_id=1, source_target_pairs={{0,508},{4,8},{8,4},{12,16},{16,12},{20,24},{24,20},{28,32},{32,28... | collective-permute-start | bytes 393224 | tf_op jit(solution)/shard_map/ppermute | solution.py:346
  20.7 3.2 %assemble.1.dense = bf16[1152,2304]{1,0:T(8,128)(2,1)S(1)} custom-call(s32[136]{0:T(256)} %rows_ref.1, s32[136]{0:T(256)} %cols_ref.1, s32[1]{0:T(128)S(6)} %copy.11.count_ref, bf16[136,128,128]{2,1,0:T(8,128)(2,1)} %blocks_hbm.1), custom_call_target="tpu_custom_call" | custom-call | tf_op jit(solution)/shard_map/assemble/pallas_call | solution.py:83
  23.9 0.0 copy-start.3
  23.9 0.0 copy-start
  23.9 0.0 collective-permute-done.1.piece
  23.9 0.0 copy-done.1
  23.9 1.0 shard_map.103.acc
  25.0 0.0 collective-permute-done.far
  25.0 0.0 copy-done.3
  25.0 0.0 copy-start.2
  25.0 0.6 shard_map.104
  25.6 1.9 %collective-permute-start.2 = (bf16[64,1024]{1,0:T(8,128)(2,1)S(1)}, bf16[64,1024]{1,0:T(8,128)(2,1)S(1)}, u32[]{:S(2)}, u32[]{:S(2)}) collective-permute-start(bf16[64,1024]{1,0:T(8,128)(2,1)S(1)} %get-tuple-element.13), channel_id=1, source_target_pairs={{0,4},{4,0},{8,12},{12,8},{16,20},{20,16},{24,28},{28,24},{32,36},... | collective-permute-start | bytes 393224 | tf_op jit(solution)/shard_map/ppermute | solution.py:347
  27.5 6.6 %collective-permute-start.3 = (bf16[64,1024]{1,0:T(8,128)(2,1)S(1)}, bf16[64,1024]{1,0:T(8,128)(2,1)S(1)}, u32[]{:S(2)}, u32[]{:S(2)}) collective-permute-start(bf16[64,1024]{1,0:T(8,128)(2,1)S(1)} %get-tuple-element.13), channel_id=1, source_target_pairs={{0,508},{4,8},{8,4},{12,16},{16,12},{20,24},{24,20},{28,32},{32,28... | collective-permute-start | bytes 393224 | tf_op jit(solution)/shard_map/ppermute | solution.py:346
  34.1 0.0 collective-permute-done.2.near
  34.2 4.8 %collective-permute-done.3.far = bf16[64,1024]{1,0:T(8,128)(2,1)S(1)} collective-permute-done((bf16[64,1024]{1,0:T(8,128)(2,1)S(1)}, bf16[64,1024]{1,0:T(8,128)(2,1)S(1)}, u32[]{:S(2)}, u32[]{:S(2)}) %collective-permute-start.3) | collective-permute-done | bytes 131104 | tf_op jit(solution)/shard_map/ppermute | solution.py:346
  39.0 2.3 %collective-permute-start.5 = (bf16[128,1024]{1,0:T(8,128)(2,1)S(1)}, bf16[128,1024]{1,0:T(8,128)(2,1)S(1)}, u32[]{:S(2)}, u32[]{:S(2)}) collective-permute-start(bf16[128,1024]{1,0:T(8,128)(2,1)S(1)} %shard_map.105.first), channel_id=1, source_target_pairs={{0,2},{1,3},{2,0},{3,1},{4,6},{5,7},{6,4},{7,5},{8,10},{9,11},{10,... | collective-permute-start | bytes 786440 | tf_op jit(solution)/shard_map/ppermute | solution.py:358
  41.3 3.0 %collective-permute-start.8 = (bf16[72,1024]{1,0:T(8,128)(2,1)S(1)}, bf16[72,1024]{1,0:T(8,128)(2,1)S(1)}, u32[]{:S(2)}, u32[]{:S(2)}) collective-permute-start(bf16[72,1024]{1,0:T(8,128)(2,1)S(1)} %get-tuple-element.14.first), channel_id=1, source_target_pairs={{0,2},{1,3},{2,0},{3,1},{4,6},{5,7},{6,4},{7,5},{8,10},{9,11},{10,... | collective-permute-start | bytes 442376 | tf_op jit(solution)/shard_map/ppermute | solution.py:358
  44.3 4.8 %collective-permute-start.4 = (bf16[128,1024]{1,0:T(8,128)(2,1)S(1)}, bf16[128,1024]{1,0:T(8,128)(2,1)S(1)}, u32[]{:S(2)}, u32[]{:S(2)}) collective-permute-start(bf16[128,1024]{1,0:T(8,128)(2,1)S(1)} %shard_map.105.first), channel_id=1, source_target_pairs={{0,1},{1,0},{2,3},{3,2},{4,5},{5,4},{6,7},{7,6},{8,9},{9,8},{10,11... | collective-permute-start | bytes 786440 | tf_op jit(solution)/shard_map/ppermute | solution.py:358
  49.1 0.0 collective-permute-done.5.third
  49.1 3.9 %collective-permute-start.6 = (bf16[128,1024]{1,0:T(8,128)(2,1)S(1)}, bf16[128,1024]{1,0:T(8,128)(2,1)S(1)}, u32[]{:S(2)}, u32[]{:S(2)}) collective-permute-start(bf16[128,1024]{1,0:T(8,128)(2,1)S(1)} %collective-permute-done.5.third), channel_id=1, source_target_pairs={{0,1},{1,0},{2,3},{3,2},{4,5},{5,4},{6,7},{7,6},{8,9},{9,8},{10,11... | collective-permute-start | bytes 786440 | tf_op jit(solution)/shard_map/ppermute | solution.py:358
  53.1 1.9 %collective-permute-start.7 = (bf16[72,1024]{1,0:T(8,128)(2,1)S(1)}, bf16[72,1024]{1,0:T(8,128)(2,1)S(1)}, u32[]{:S(2)}, u32[]{:S(2)}) collective-permute-start(bf16[72,1024]{1,0:T(8,128)(2,1)S(1)} %get-tuple-element.14.first), channel_id=1, source_target_pairs={{0,1},{1,0},{2,3},{3,2},{4,5},{5,4},{6,7},{7,6},{8,9},{9,8},{10,11... | collective-permute-start | bytes 442376 | tf_op jit(solution)/shard_map/ppermute | solution.py:358
  55.0 0.0 collective-permute-done.8.third
  55.0 2.4 %collective-permute-start.9 = (bf16[72,1024]{1,0:T(8,128)(2,1)S(1)}, bf16[72,1024]{1,0:T(8,128)(2,1)S(1)}, u32[]{:S(2)}, u32[]{:S(2)}) collective-permute-start(bf16[72,1024]{1,0:T(8,128)(2,1)S(1)} %collective-permute-done.8.third), channel_id=1, source_target_pairs={{0,1},{1,0},{2,3},{3,2},{4,5},{5,4},{6,7},{7,6},{8,9},{9,8},{10,11... | collective-permute-start | bytes 442376 | tf_op jit(solution)/shard_map/ppermute | solution.py:358
  57.4 0.0 collective-permute-done.7.second
  57.4 1.0 collective-permute-done.9.fourth
  58.4 0.0 copy-done
  58.4 1.2 %shard_map.106 = (f32[1024,256]{1,0:T(8,128)S(1)}, f32[64,1024]{1,0:T(8,128)S(1)}, bf16[256,1024]{1,0:T(8,128)(2,1)S(1)}, f32[8,1024]{1,0:T(8,128)S(1)}) custom-call(bf16[72,1024]{1,0:T(8,128)(2,1)S(1)} %get-tuple-element.14.first, bf16[72,1024]{1,0:T(8,128)(2,1)S(1)} %collective-permute-done.7.second, bf16[72,1024]{1,0:T(8,128)(2,1)S(1)} %collective-permute-done.8.third, ...), custom_call_target="tpu_custom_call" | custom-call | tf_op jit(solution)/shard_map/pallas_call | solution.py:333
  59.7 0.0 collective-permute-done.4.second
  59.7 0.0 collective-permute-done.6.fourth
  59.7 0.0 copy-done.2
  59.7 5.1 %shard_map.107 = (f32[128,256]{1,0:T(8,128)}, f32[16,4,384]{2,1,0:T(4,128)S(1)}) custom-call(bf16[128,1024]{1,0:T(8,128)(2,1)S(1)} %shard_map.105.first, bf16[128,1024]{1,0:T(8,128)(2,1)S(1)} %collective-permute-done.4.second, bf16[128,1024]{1,0:T(8,128)(2,1)S(1)} %collective-permute-done.5.third, bf16[128,1024]{1,0:T(8,128)(2,1)S(1)} %collective-permute-done.6.fourth, ...), custom_call_target="tpu_custom_call" | custom-call | tf_op jit(solution)/shard_map/pallas_call | solution.py:333
  64.8 10.4 %all_to_all.15.parts = f32[16,4,384]{2,1,0:T(4,128)S(1)} all-to-all(f32[16,4,384]{2,1,0:T(4,128)S(1)} %get-tuple-element.20), channel_id=1, replica_groups=mesh['yh'=2,'zh'=8,'zp'=2,'x'=4,'yl'=2,'co'=2] {'yh','zp','x'}, dimensions={0} | all-to-all | bytes 196608 | tf_op jit(solution)/shard_map/all_to_all | solution.py:421
  75.2 17.7 %all_to_all.16.parts = f32[8,4,384]{2,1,0:T(4,128)S(1)} all-to-all(f32[8,4,384]{2,1,0:T(4,128)S(1)} %shard_map.108), channel_id=1, replica_groups=mesh['yh'=2,'zh'=8,'zp'=2,'x'=4,'yl'=2,'co'=2] {'zh'}, dimensions={0} | all-to-all | bytes 98304 | tf_op jit(solution)/shard_map/all_to_all | solution.py:423
  93.0 17.5 %all_to_all.17.parts = f32[64,4,384]{2,1,0:T(4,128)S(1)} all-to-all(f32[64,4,384]{2,1,0:T(4,128)S(1)} %shard_map.109), channel_id=1, replica_groups=mesh['yh'=2,'zh'=8,'zp'=2,'x'=4,'yl'=2,'co'=2] {'yh','zp','x','yl','co'}, dimensions={0} | all-to-all | bytes 786432 | tf_op jit(solution)/shard_map/all_to_all | solution.py:425
  110.5 0.9 shard_map.110
  (3 shorter events, 0.1 us)
Async XLA Ops:
  0.6 23.3 %copy-start.1 = (bf16[64,1024]{1,0:T(8,128)(2,1)S(1)}, bf16[64,1024]{1,0:T(8,128)(2,1)}, u32[]{:S(2)}) copy-start(bf16[64,1024]{1,0:T(8,128)(2,1)} %own.1) | copy-start | bytes 393220
  0.6 23.3 %collective-permute-start.1 = (bf16[64,1024]{1,0:T(8,128)(2,1)}, bf16[64,1024]{1,0:T(8,128)(2,1)S(1)}, u32[]{:S(2)}, u32[]{:S(2)}) collective-permute-start(bf16[64,1024]{1,0:T(8,128)(2,1)} %own.1), channel_id=1, source_target_pairs={{0,4},{4,0},{8,12},{12,8},{16,20},{20,16},{24,28},{28,24},{32,36},... | collective-permute-start | bytes 393224 | tf_op jit(solution)/shard_map/ppermute | solution.py:347
  4.7 20.3 %collective-permute-start = (bf16[64,1024]{1,0:T(8,128)(2,1)}, bf16[64,1024]{1,0:T(8,128)(2,1)S(1)}, u32[]{:S(2)}, u32[]{:S(2)}) collective-permute-start(bf16[64,1024]{1,0:T(8,128)(2,1)} %own.1), channel_id=1, source_target_pairs={{0,508},{4,8},{8,4},{12,16},{16,12},{20,24},{24,20},{28,32},{32,28... | collective-permute-start | bytes 393224 | tf_op jit(solution)/shard_map/ppermute | solution.py:346
  23.9 1.1 copy-start.3
  23.9 34.5 %copy-start = (bf16[256,256]{1,0:T(8,128)(2,1)S(1)}, bf16[256,256]{1,0:T(8,128)(2,1)}, u32[]{:S(2)}) copy-start(bf16[256,256]{1,0:T(8,128)(2,1)} %w_in.3) | copy-start | bytes 393220
  25.0 34.7 %copy-start.2 = (bf16[256,128]{1,0:T(8,128)(2,1)S(1)}, bf16[256,128]{1,0:T(8,128)(2,1)}, u32[]{:S(2)}) copy-start(bf16[256,128]{1,0:T(8,128)(2,1)} %w_out.1) | copy-start | bytes 196612
  25.6 8.6 %collective-permute-start.2 = (bf16[64,1024]{1,0:T(8,128)(2,1)S(1)}, bf16[64,1024]{1,0:T(8,128)(2,1)S(1)}, u32[]{:S(2)}, u32[]{:S(2)}) collective-permute-start(bf16[64,1024]{1,0:T(8,128)(2,1)S(1)} %get-tuple-element.13), channel_id=1, source_target_pairs={{0,4},{4,0},{8,12},{12,8},{16,20},{20,16},{24,28},{28,24},{32,36},... | collective-permute-start | bytes 393224 | tf_op jit(solution)/shard_map/ppermute | solution.py:347
  27.5 11.4 %collective-permute-start.3 = (bf16[64,1024]{1,0:T(8,128)(2,1)S(1)}, bf16[64,1024]{1,0:T(8,128)(2,1)S(1)}, u32[]{:S(2)}, u32[]{:S(2)}) collective-permute-start(bf16[64,1024]{1,0:T(8,128)(2,1)S(1)} %get-tuple-element.13), channel_id=1, source_target_pairs={{0,508},{4,8},{8,4},{12,16},{16,12},{20,24},{24,20},{28,32},{32,28... | collective-permute-start | bytes 393224 | tf_op jit(solution)/shard_map/ppermute | solution.py:346
  39.0 10.2 %collective-permute-start.5 = (bf16[128,1024]{1,0:T(8,128)(2,1)S(1)}, bf16[128,1024]{1,0:T(8,128)(2,1)S(1)}, u32[]{:S(2)}, u32[]{:S(2)}) collective-permute-start(bf16[128,1024]{1,0:T(8,128)(2,1)S(1)} %shard_map.105.first), channel_id=1, source_target_pairs={{0,2},{1,3},{2,0},{3,1},{4,6},{5,7},{6,4},{7,5},{8,10},{9,11},{10,... | collective-permute-start | bytes 786440 | tf_op jit(solution)/shard_map/ppermute | solution.py:358
  41.3 13.7 %collective-permute-start.8 = (bf16[72,1024]{1,0:T(8,128)(2,1)S(1)}, bf16[72,1024]{1,0:T(8,128)(2,1)S(1)}, u32[]{:S(2)}, u32[]{:S(2)}) collective-permute-start(bf16[72,1024]{1,0:T(8,128)(2,1)S(1)} %get-tuple-element.14.first), channel_id=1, source_target_pairs={{0,2},{1,3},{2,0},{3,1},{4,6},{5,7},{6,4},{7,5},{8,10},{9,11},{10,... | collective-permute-start | bytes 442376 | tf_op jit(solution)/shard_map/ppermute | solution.py:358
  44.3 15.4 %collective-permute-start.4 = (bf16[128,1024]{1,0:T(8,128)(2,1)S(1)}, bf16[128,1024]{1,0:T(8,128)(2,1)S(1)}, u32[]{:S(2)}, u32[]{:S(2)}) collective-permute-start(bf16[128,1024]{1,0:T(8,128)(2,1)S(1)} %shard_map.105.first), channel_id=1, source_target_pairs={{0,1},{1,0},{2,3},{3,2},{4,5},{5,4},{6,7},{7,6},{8,9},{9,8},{10,11... | collective-permute-start | bytes 786440 | tf_op jit(solution)/shard_map/ppermute | solution.py:358
  49.1 10.5 %collective-permute-start.6 = (bf16[128,1024]{1,0:T(8,128)(2,1)S(1)}, bf16[128,1024]{1,0:T(8,128)(2,1)S(1)}, u32[]{:S(2)}, u32[]{:S(2)}) collective-permute-start(bf16[128,1024]{1,0:T(8,128)(2,1)S(1)} %collective-permute-done.5.third), channel_id=1, source_target_pairs={{0,1},{1,0},{2,3},{3,2},{4,5},{5,4},{6,7},{7,6},{8,9},{9,8},{10,11... | collective-permute-start | bytes 786440 | tf_op jit(solution)/shard_map/ppermute | solution.py:358
  53.1 4.4 %collective-permute-start.7 = (bf16[72,1024]{1,0:T(8,128)(2,1)S(1)}, bf16[72,1024]{1,0:T(8,128)(2,1)S(1)}, u32[]{:S(2)}, u32[]{:S(2)}) collective-permute-start(bf16[72,1024]{1,0:T(8,128)(2,1)S(1)} %get-tuple-element.14.first), channel_id=1, source_target_pairs={{0,1},{1,0},{2,3},{3,2},{4,5},{5,4},{6,7},{7,6},{8,9},{9,8},{10,11... | collective-permute-start | bytes 442376 | tf_op jit(solution)/shard_map/ppermute | solution.py:358
  55.0 3.4 %collective-permute-start.9 = (bf16[72,1024]{1,0:T(8,128)(2,1)S(1)}, bf16[72,1024]{1,0:T(8,128)(2,1)S(1)}, u32[]{:S(2)}, u32[]{:S(2)}) collective-permute-start(bf16[72,1024]{1,0:T(8,128)(2,1)S(1)} %collective-permute-done.8.third), channel_id=1, source_target_pairs={{0,1},{1,0},{2,3},{3,2},{4,5},{5,4},{6,7},{7,6},{8,9},{9,8},{10,11... | collective-permute-start | bytes 442376 | tf_op jit(solution)/shard_map/ppermute | solution.py:358
